TPU v7x, 128 devices: a whole 4x4x4 slice. The times are simulated.
128 devices in a mesh: tok: 8 (over z, x_lo), head: 16 (over x_hi, y, core).
Axes of the slice: x: 4 (x_hi: 2, x_lo: 2; x = x_hi * 2 + x_lo), y: 4, z: 4, core: 2. Of those that a mesh axis runs over, the one named last changes fastest.
Arguments:
- block_states: bfloat16 [2048, 4096], P('tok', 'head'), may hold values from -24 to 24
- token_ids: int32 [2048], replicated, may hold values from 0 to 100351
- accept: int32 [2048], P('tok'), may hold values 0 or 1
- cache_lengths: int32 [8], replicated, may hold values from 1 to 5120, as said below
- cache_keys: bfloat16 [8192, 4096], P('tok', 'head'), may hold values from -300 to 300
- cache_values: bfloat16 [8192, 4096], P('tok', 'head'), may hold values from -6 to 6
- w_query: bfloat16 [4096, 4096], P(None, 'head'), may hold values from -0.09375 to 0.09375
- w_key: bfloat16 [4096, 4096], P(None, 'head'), may hold values from -0.09375 to 0.09375
- w_value: bfloat16 [4096, 4096], P(None, 'head'), may hold values from -0.09375 to 0.09375
- w_out: bfloat16 [4096, 4096], P('head'), may hold values from -0.09375 to 0.09375
- attn_gain: float32 [4096], replicated, may hold values from 0.25 to 1.75
- final_gain: float32 [4096], replicated, may hold values from 0.25 to 1.75
- embed: bfloat16 [100352, 4096], P('tok', 'head'), may hold values from -6 to 6
- lm_head: bfloat16 [100352, 4096], P(('tok', 'head')), may hold values from -0.25 to 0.25
Outputs:
- hiddens: bfloat16 [2048, 4096], P(('tok', 'head'))
- request_norms: float32 [8], replicated
- top_logits: float32 [2048], replicated
Inputs may be any that keep to these rules, and one draw needn't show every extreme that they name: `cache_lengths`: each request has 1 or more cached positions; the counts sum to 8192 and the largest is exactly 5120.
All inputs are finite; a program needn't handle non-finite values. No bound on the sum of `accept` on one device may be relied on, other than what follows from the above.
Results may differ from a plain program's by a relative error of at most 0.0068.
Values may be sent and summed in bfloat16 or wider, within the bound.
A program may use at most 192 MiB of HBM per device.

v0:
```python
import math

import jax
import jax.numpy as jnp
from jax import lax
from jax.sharding import PartitionSpec as P

HEAD_DIM = 128


EPSILON = 1e-06


def row_norm(values):
    return values * lax.rsqrt(jnp.mean(values * values, axis=-1, keepdims=True) + EPSILON)


def softmax_block(softmax_state, query_heads, key_block, value_block, valid_keys, score_scale):
    running_max, running_sum, running_acc = softmax_state
    scores = (
        jnp.einsum("qhd,khd->hqk", query_heads, key_block, preferred_element_type=jnp.float32)
        * score_scale
    )
    masked = jnp.where(valid_keys[None, None, :], scores, -1e30)
    new_max = jnp.maximum(running_max, jnp.max(masked, axis=-1))
    weights = jnp.where(valid_keys[None, None, :], jnp.exp(masked - new_max[:, :, None]), 0.0)
    factor = jnp.exp(running_max - new_max)
    running_sum = running_sum * factor + jnp.sum(weights, axis=-1)
    running_acc = running_acc * factor[:, :, None] + jnp.einsum(
        "hqk,khd->hqd", weights, value_block.astype(jnp.float32)
    )
    return (new_max, running_sum, running_acc)


def shards(
    block_states,
    token_ids,
    accept,
    cache_lengths,
    cache_keys,
    cache_values,
    w_query,
    w_key,
    w_value,
    w_out,
    attn_gain,
    final_gain,
    embed,
    lm_head,
):
    tok_index = lax.axis_index("tok")
    head_index = lax.axis_index("head")
    tok_count = lax.axis_size("tok")
    head_count = lax.axis_size("head")
    block_rows = block_states.shape[0]
    model_width = w_query.shape[0]
    local_width = w_query.shape[1]
    heads_here = local_width // HEAD_DIM
    share_rows = block_rows // head_count
    key_span = 512
    score_scale = 1.0 / math.sqrt(HEAD_DIM)
    offsets = jnp.cumsum(cache_lengths) - cache_lengths
    zero_rows = jnp.zeros((key_span, local_width), jnp.bfloat16)
    gathered_keys, gathered_values = (
        lax.all_gather(cache_keys, "tok", axis=0, tiled=True),
        lax.all_gather(cache_values, "tok", axis=0, tiled=True),
    )
    gathered_keys = jnp.concatenate([gathered_keys, zero_rows], axis=0)
    gathered_values = jnp.concatenate([gathered_values, zero_rows], axis=0)

    def attention(queries, key_rows, value_rows):
        query_heads = queries.reshape(block_rows, heads_here, HEAD_DIM)
        own_state = softmax_block(
            (
                jnp.full((heads_here, block_rows), -1e30, jnp.float32),
                jnp.zeros((heads_here, block_rows), jnp.float32),
                jnp.zeros((heads_here, block_rows, HEAD_DIM), jnp.float32),
            ),
            query_heads,
            key_rows.reshape(block_rows, heads_here, HEAD_DIM),
            value_rows.reshape(block_rows, heads_here, HEAD_DIM),
            jnp.ones((block_rows,), bool),
            score_scale,
        )
        request_begin = offsets[tok_index]
        request_length = cache_lengths[tok_index]
        block_count = (request_length + key_span - 1) // key_span

        def advance(turn_index, softmax_state):
            key_start = request_begin + turn_index * key_span
            key_block = lax.dynamic_slice_in_dim(gathered_keys, key_start, key_span, 0).reshape(
                key_span, heads_here, HEAD_DIM
            )
            value_block = lax.dynamic_slice_in_dim(gathered_values, key_start, key_span, 0).reshape(
                key_span, heads_here, HEAD_DIM
            )
            valid_keys = (
                turn_index * key_span + jnp.arange(key_span, dtype=jnp.int32) < request_length
            )
            return softmax_block(
                softmax_state, query_heads, key_block, value_block, valid_keys, score_scale
            )

        final_state = lax.fori_loop(0, block_count, advance, own_state)
        running_max, running_sum, running_acc = final_state
        result = running_acc / running_sum[:, :, None]
        return (
            jnp.transpose(result, (1, 0, 2)).reshape(block_rows, local_width).astype(jnp.bfloat16)
        )

    def run_layer(features):
        piece_cols = lax.all_gather(features, "head", axis=1, tiled=True)
        query_acc = jnp.dot(piece_cols, w_query, preferred_element_type=jnp.float32)
        key_acc = jnp.dot(piece_cols, w_key, preferred_element_type=jnp.float32)
        value_acc = jnp.dot(piece_cols, w_value, preferred_element_type=jnp.float32)
        own_rows = lax.dynamic_slice_in_dim(piece_cols, head_index * share_rows, share_rows, 0)
        residual = own_rows
        query_acc, key_acc, value_acc, residual = (query_acc, key_acc, value_acc, residual)
        attended = attention(
            query_acc.astype(jnp.bfloat16),
            key_acc.astype(jnp.bfloat16),
            value_acc.astype(jnp.bfloat16),
        )
        projected = lax.psum_scatter(
            jnp.dot(attended, w_out, preferred_element_type=jnp.float32),
            "head",
            scatter_dimension=0,
            tiled=True,
        )
        return (residual.astype(jnp.float32) + row_norm(projected) * attn_gain).astype(jnp.bfloat16)

    first_pass = run_layer(block_states)
    row_piece = lax.all_gather(first_pass, ("tok", "head"), axis=0, tiled=True)
    piece_rows = row_piece.shape[0]
    widened = row_piece.astype(jnp.float32)
    row_squares = jnp.sum(widened * widened, axis=-1)
    normed = (row_norm(widened) * final_gain).astype(jnp.bfloat16)
    logits = lax.dot_general(
        normed, lm_head, (((1,), (1,)), ((), ())), preferred_element_type=jnp.float32
    )
    best = jnp.max(logits, axis=1)
    owners = jnp.arange(piece_rows, dtype=jnp.int32) // block_rows
    one_hot = (owners[:, None] == jnp.arange(tok_count, dtype=jnp.int32)[None, :]).astype(
        jnp.float32
    )
    square_sums = jnp.dot(row_squares, one_hot, precision=lax.Precision.HIGHEST)
    top_local, square_sums = (best, square_sums)
    top_logits = lax.pmax(top_local, ("tok", "head"))
    request_norms = jnp.sqrt(square_sums / (block_rows * model_width))
    vocab_here = embed.shape[0]
    local_ids = token_ids - tok_index * vocab_here
    inside_vocab = (local_ids >= 0) & (local_ids < vocab_here)
    looked_up = jnp.take(embed, jnp.clip(local_ids, 0, vocab_here - 1), axis=0)
    looked_up = jnp.where(inside_vocab[:, None], looked_up, jnp.zeros_like(looked_up)).astype(
        jnp.float32
    )
    embedded = lax.psum_scatter(
        looked_up.astype(jnp.bfloat16), "tok", scatter_dimension=0, tiled=True
    )
    swapped = jnp.where((accept == 1)[:, None], embedded, block_states)
    hiddens = run_layer(swapped)
    return (hiddens, request_norms, top_logits)


def solution(mesh):
    placed = (
        P("tok", "head"),
        P(),
        P("tok"),
        P(),
        P("tok", "head"),
        P("tok", "head"),
        P(None, "head"),
        P(None, "head"),
        P(None, "head"),
        P("head", None),
        P(),
        P(),
        P("tok", "head"),
        P(("tok", "head"), None),
    )
    return jax.shard_map(
        shards,
        mesh=mesh,
        in_specs=placed,
        out_specs=(P(("tok", "head"), None), P(), P()),
        check_vma=False,
    )
```

profile of v0, /device:TPU:1, one launch (start us, length us, event | category | flops | bytes accessed | tf_op | source)
XLA Modules:
  0.0 832.8 jit_solution(10681744635398324091)
XLA Ops:
  8.1 0.8 fusion.34
  8.9 0.7 compare_and_fusion.1
  9.6 10.3 %gather_fusion = bf16[2048,256]{1,0:T(8,128)(2,1)S(1)} fusion(bf16[12544,256]{1,0:T(8,128)(2,1)} %param.30, s32[2048]{0:T(1024)S(1)} %fusion.34), kind=kCustom, calls=%fused_computation | custom fusion | bytes 2105344 | tf_op jit(solution)/shard_map/jit(_take)/gather | solution.py:153
  19.9 2.4 select_select_fusion
  22.5 0.5 all-gather.12.cloned.1.call-update
  23.1 39.3 %reduce-scatter.4.cloned.1.call-done = bf16[256,256]{1,0:T(8,128)(2,1)} async-done(((bf16[2048,256]{1,0:T(8,128)(2,1)}), bf16[256,256]{1,0:T(8,128)(2,1)}) %reduce-scatter.4.cloned.1.call-update) | async-done | bytes 131088 | tf_op jit(solution)/shard_map/reduce_scatter | solution.py:157
  62.4 1.7 broadcast_select_fusion
  64.1 2.0 copy.39
  66.2 1.0 copy.40
  67.3 0.6 dynamic_slice.27
  68.8 0.6 dynamic_slice.28
  69.4 7.6 all-gather.12.cloned.1.call-done
  77.0 3.1 convolution_convert_fusion.2
  80.3 3.3 convolution_convert_fusion.1
  84.0 1.0 convolution_convert_fusion
  85.0 0.3 convolution_add_fusion.2
  85.3 39.0 %all-gather.6.cloned.1.call-done = bf16[256,4096]{1,0:T(8,128)(2,1)} async-done(((bf16[256,256]{1,0:T(8,128)(2,1)}), bf16[256,4096]{1,0:T(8,128)(2,1)}) %all-gather.6.cloned.1.call-update) | async-done | bytes 2097168 | tf_op jit(solution)/shard_map/all_gather | solution.py:112
  124.3 3.3 convolution_convert_fusion.5
  127.8 1.0 convolution_convert_fusion.4
  129.0 85.2 %all-gather.8.cloned.1.call-done = bf16[8192,256]{0,1:T(8,128)(2,1)} async-done(((bf16[1024,256]{0,1:T(8,128)(2,1)}), bf16[8192,256]{0,1:T(8,128)(2,1)}) %all-gather.8.cloned.1.call-update) | async-done | bytes 4194320 | tf_op jit(solution)/shard_map/all_gather | solution.py:65
  214.2 4.6 concatenate.6
  218.8 87.8 %all-gather.10.cloned.1.call-done = bf16[8192,256]{0,1:T(8,128)(2,1)} async-done(((bf16[1024,256]{0,1:T(8,128)(2,1)}), bf16[8192,256]{0,1:T(8,128)(2,1)}) %all-gather.10.cloned.1.call-update) | async-done | bytes 4194320 | tf_op jit(solution)/shard_map/all_gather | solution.py:66
  306.6 4.6 concatenate.7
  311.2 3.8 while.29
  311.8 1.3 constant_dynamic-slice_fusion.7
  313.2 0.7 add_compare_fusion.5
  313.9 0.4 fusion.91
  314.5 0.5 convolution_add_fusion.7
  315.2 2.7 fusion.42
  318.4 3.1 convolution_convert_fusion.3
  321.6 0.3 convolution_add_fusion.3
  321.9 3.8 while.28
  322.5 1.3 constant_dynamic-slice_fusion.6
  323.9 0.7 add_compare_fusion.4
  324.6 0.4 fusion.86
  325.2 0.5 convolution_add_fusion.6
  325.9 2.7 fusion.41
  328.6 102.7 %reduce-scatter.8.cloned.1.call-done = f32[16,4096]{1,0:T(8,128)} async-done(((f32[256,4096]{1,0:T(8,128)}), f32[16,4096]{1,0:T(8,128)}) %reduce-scatter.8.cloned.1.call-update) | async-done | bytes 262160 | tf_op jit(solution)/shard_map/reduce_scatter | solution.py:124
  431.3 1.1 multiply_reduce_fusion
  432.4 82.7 %reduce-scatter.6.cloned.1.call-done = f32[16,4096]{1,0:T(8,128)} async-done(((f32[256,4096]{1,0:T(8,128)}), f32[16,4096]{1,0:T(8,128)}) %reduce-scatter.6.cloned.1.call-update) | async-done | bytes 262160 | tf_op jit(solution)/shard_map/reduce_scatter | solution.py:124
  515.1 1.1 multiply_reduce_fusion.1
  516.2 2.0 add_convert_fusion
  518.2 214.2 %all-gather.14.cloned.1.call-done = bf16[2048,4096]{1,0:T(8,128)(2,1)} async-done(((bf16[16,4096]{1,0:T(8,128)(2,1)}), bf16[2048,4096]{1,0:T(8,128)(2,1)}) %all-gather.14.cloned.1.call-update) | async-done | bytes 16777232 | tf_op jit(solution)/shard_map/all_gather | solution.py:133
  732.5 7.5 fusion.14
  740.1 3.1 copy-done.4
  743.2 17.2 %fusion.21 = f32[2048]{0:T(1024)S(1)} fusion(bf16[784,4096]{1,0:T(8,128)(2,1)} %param.31, bf16[2048,4096]{1,0:T(8,128)(2,1)S(1)} %copy-done.4, f32[4096]{0:T(1024)S(1)} %copy-done.10, f32[2048]{0:T(1024)S(1)} %add_rsqrt_fusion), kind=kOutput, calls=%fused_computation.39 | convolution fusion | flops 13188495360 | bytes 23232512 | tf_op jit(solution)/shard_map/dot_general | solution.py:138
  760.4 63.8 %pmax.7 = f32[2048]{0:T(1024)} all-reduce(f32[2048]{0:T(1024)S(1)} %fusion.21), channel_id=1, replica_groups=mesh['tok'=8,'head'=16] {'tok','head'}, use_global_device_ids=true, to_apply=%region_20.21 | all-reduce | flops 2048 | bytes 16384 | tf_op jit(solution)/shard_map/pmax | solution.py:148
  824.2 1.1 fusion.25
  (69 shorter events, 2.9 us)
Async XLA Ops:
  8.0 307.2 %copy-start = (bf16[256,4096]{1,0:T(8,128)(2,1)S(1)}, bf16[256,4096]{1,0:T(8,128)(2,1)}, u32[]{:S(2)}) copy-start(bf16[256,4096]{1,0:T(8,128)(2,1)} %param.27) | copy-start | bytes 6291460
  8.0 54.4 %reduce-scatter.4.cloned.1.call-start = ((), (), s32[]{:S(2)}) async-start(), calls=%async_computation.3 | async-start | bytes 1179648 | tf_op jit(solution)/shard_map/reduce_scatter | solution.py:157
  19.9 3.1 copy-start.11
  19.9 42.4 %copy-start.8 = (bf16[256,256]{1,0:T(8,128)(2,1)S(1)}, bf16[256,256]{1,0:T(8,128)(2,1)}, u32[]{:S(2)}) copy-start(bf16[256,256]{1,0:T(8,128)(2,1)} %param.18) | copy-start | bytes 393220
  22.4 43.9 %copy-start.7 = (bf16[1024,256]{1,0:T(8,128)(2,1)S(1)}, bf16[1024,256]{1,0:T(8,128)(2,1)}, u32[]{:S(2)}) copy-start(bf16[1024,256]{1,0:T(8,128)(2,1)} %param.23) | copy-start | bytes 1572868
  22.4 44.9 %copy-start.12 = (s32[8]{0:T(128)S(1)}, s32[8]{0:T(128)}, u32[]{:S(2)}) copy-start(s32[8]{0:T(128)} %param.21) | copy-start | bytes 100
  22.4 54.6 %all-gather.12.cloned.1.call-start = ((), (), s32[]{:S(2)}) async-start(), calls=%async_computation.8 | async-start | bytes 2228224 | tf_op jit(solution)/shard_map/all_gather | solution.py:112
  23.0 101.3 %all-gather.6.cloned.1.call-start = ((), (), s32[]{:S(2)}) async-start(), calls=%async_computation.4 | async-start | bytes 2228224 | tf_op jit(solution)/shard_map/all_gather | solution.py:112
  64.1 150.1 %all-gather.8.cloned.1.call-start = ((), (), s32[]{:S(2)}) async-start(), calls=%async_computation.5 | async-start | bytes 4718592 | tf_op jit(solution)/shard_map/all_gather | solution.py:65
  66.2 240.4 %all-gather.10.cloned.1.call-start = ((), (), s32[]{:S(2)}) async-start(), calls=%async_computation.6 | async-start | bytes 4718592 | tf_op jit(solution)/shard_map/all_gather | solution.py:66
  67.3 364.1 %reduce-scatter.8.cloned.1.call-start = ((), (), s32[]{:S(2)}) async-start(), calls=%async_computation.9 | async-start | bytes 4456448 | tf_op jit(solution)/shard_map/reduce_scatter | solution.py:124
  80.3 3.7 copy-start.2
  80.3 3.7 copy-start.6
  124.3 3.3 copy-start.3
  124.3 3.5 copy-start.5
  318.0 197.2 %reduce-scatter.6.cloned.1.call-start = ((), (), s32[]{:S(2)}) async-start(), calls=%async_computation.7 | async-start | bytes 4456448 | tf_op jit(solution)/shard_map/reduce_scatter | solution.py:124
  328.6 187.7 %copy-start.9 = (f32[4096]{0:T(1024)S(1)}, f32[4096]{0:T(1024)}, u32[]{:S(2)}) copy-start(f32[4096]{0:T(1024)} %param.28) | copy-start | bytes 49156
  328.6 403.9 %all-gather.14.cloned.1.call-start = ((), (), s32[]{:S(2)}) async-start(), calls=%async_computation.10 | async-start | bytes 16908288 | tf_op jit(solution)/shard_map/all_gather | solution.py:133
  518.2 221.8 %copy-start.10 = (f32[4096]{0:T(1024)S(1)}, f32[4096]{0:T(1024)}, u32[]{:S(2)}) copy-start(f32[4096]{0:T(1024)} %param.29) | copy-start | bytes 49156
  732.5 10.7 %copy-start.4 = (bf16[2048,4096]{1,0:T(8,128)(2,1)S(1)}, bf16[2048,4096]{1,0:T(8,128)(2,1)}, u32[]{:S(2)}) copy-start(bf16[2048,4096]{1,0:T(8,128)(2,1)} %all-gather.14.cloned.1.call-done) | copy-start | bytes 50331652
  743.2 82.2 %copy-start.1 = (bf16[256,4096]{1,0:T(8,128)(2,1)S(1)}, bf16[256,4096]{1,0:T(8,128)(2,1)}, u32[]{:S(2)}) copy-start(bf16[256,4096]{1,0:T(8,128)(2,1)} %param.27) | copy-start | bytes 6291460
Sparse Core Ops, SparseCore 0:
  22.5 39.8 reduce-scatter.3
  518.3 214.1 all-gather.13
Sparse Core Ops, SparseCore 1:
  25.2 51.8 all-gather.11
  79.7 44.5 all-gather.5
  125.8 88.3 all-gather.7
  215.9 90.7 all-gather.9
  318.0 113.2 reduce-scatter.7
  435.9 79.2 reduce-scatter.5
where the time goes:
time: 834 us; the launch traced here: 833 us
  waiting for transfers between devices  659 us (79%)
  blocking collectives  63.8 us (8%)
  matrix products  41.5 us (5%)
  local copies, waits for them, and re-layouts  30.3 us (4%)
  other arithmetic  19.6 us (2%)
  between operations  16.6 us (2%)
    all_gather x1, waiting for transfers between devices, shards(): row_piece = lax.all_gather(first_pass, ('tok', 'head'), axis=0, tiled=True)  214 us
    reduce_scatter x2, waiting for transfers between devices, run_layer(): lax.psum_scatter(jnp.dot(attended, w_out, preferred_element_type=jnp.floa...  185 us
    all_gather x1, waiting for transfers between devices, shards(): lax.all_gather(cache_values, 'tok', axis=0, tiled=True)  87.8 us
    all_gather x1, waiting for transfers between devices, shards(): lax.all_gather(cache_keys, 'tok', axis=0, tiled=True)  85.2 us
    pmax x1, blocking collectives, shards(): top_logits = lax.pmax(top_local, ('tok', 'head'))  63.8 us
    all_gather x2, waiting for transfers between devices, run_layer(): piece_cols = lax.all_gather(features, 'head', axis=1, tiled=True)  46.6 us
    reduce_scatter x1, waiting for transfers between devices, shards(): lax.psum_scatter(looked_up.astype(jnp.bfloat16), 'tok', scatter_dimension...  39.3 us
    dot_general x1, matrix products, shards(): lax.dot_general(normed, lm_head, (((1,), (1,)), ((), ())), preferred_elem...  17.2 us
  transfers between devices with their start and end apart: 8, of which 8 were waited for; matrix products, arithmetic and copies ran while one was open for 4% of the time, Pallas kernels for 0%

commit v1 on v0

v1 whole, which is shorter than its diff:
```python
import math

import jax
import jax.numpy as jnp
from jax import lax
from jax.experimental import pallas as pl
from jax.experimental.pallas import tpu as pltpu
from jax.sharding import PartitionSpec as P

HEAD_DIM = 128
EPSILON = 1e-06
NEG = -1e30
SCALE2 = (1.0 / math.sqrt(HEAD_DIM)) * math.log2(math.e)
MESH = pl.DeviceIdType.MESH
BF = jnp.bfloat16
F32 = jnp.float32
ANY = pl.BlockSpec(memory_space=pl.ANY)
VM = pl.BlockSpec(memory_space=pltpu.VMEM)
REL8 = ((0, 2), (1, 2), (1, 1), (1, 3), (0, 1), (0, 3), (1, 0))


def coords():
    t = lax.axis_index("tok")
    h = lax.axis_index("head")
    return t // 2, lax.rem(t, 2), h // 8, lax.rem(h // 2, 4), lax.rem(h, 2)


def place(z, xl, xh, y, c):
    return (z * 2 + xl, xh * 8 + y * 2 + c)


def ring(v, d):
    return lax.rem(v + d, 4)


class Links:
    def __init__(self, send, recv):
        self.send, self.recv, self.used = send, recv, 0

    def copy(self, src, dst, device):
        k = self.used
        self.used += 1
        cp = pltpu.make_async_remote_copy(
            src_ref=src,
            dst_ref=dst,
            send_sem=self.send.at[k],
            recv_sem=self.recv.at[k],
            device_id=device,
            device_id_type=MESH,
        )
        cp.start()
        return cp


class Task:
    def __init__(self, body, ins, outs, scratch, copies, local, peers):
        self.body, self.ins, self.outs = body, ins, outs
        self.scratch = list(scratch) + [
            pltpu.SemaphoreType.DMA((copies,)),
            pltpu.SemaphoreType.DMA((copies,)),
            pltpu.SemaphoreType.DMA((max(local, 1),)),
        ]
        self.peers = peers


def head_peers_ag():
    z, xl, xh, y, c = coords()
    out = [("core", place(z, xl, xh, y, 1 - c)), ("x2", place(z, xl, 1 - xh, y, c))]
    return out + [("y%d" % d, place(z, xl, xh, ring(y, d), c)) for d in (1, 2, 3)]


def head_peers_all():
    z, xl, xh, y, c = coords()
    out = [("core", place(z, xl, xh, y, 1 - c))]
    return out + [
        ("h%d%d" % (dx, dy), place(z, xl, lax.rem(xh + dx, 2), ring(y, dy), c)) for dx, dy in REL8
    ]


def tok_peers_ag():
    z, xl, xh, y, c = coords()
    out = [("x1", place(z, 1 - xl, xh, y, c))]
    return out + [("z%d" % d, place(ring(z, d), xl, xh, y, c)) for d in (1, 2, 3)]


def tok_peers_all():
    z, xl, xh, y, c = coords()
    return [
        ("t%d%d" % (dx, dz), place(ring(z, dz), lax.rem(xl + dx, 2), xh, y, c)) for dx, dz in REL8
    ]


CANON = {"h10": "x2", "h01": "y1", "h02": "y2", "h03": "y3"}
CANON.update({"t10": "x1", "t01": "z1", "t02": "z2", "t03": "z3"})


def comm(tasks, cid, name):
    n_in = [len(t.ins) for t in tasks]
    n_out = [len(t.outs) for t in tasks]
    n_scr = [len(t.scratch) for t in tasks]

    def kernel(*refs):
        ins, rest = refs[: sum(n_in)], refs[sum(n_in) :]
        outs, scr = rest[: sum(n_out)], rest[sum(n_out) :]
        peers = {}
        for t in tasks:
            for key, device in t.peers():
                peers.setdefault(CANON.get(key, key), device)
        barrier = pltpu.get_barrier_semaphore()
        for device in peers.values():
            pl.semaphore_signal(barrier, inc=1, device_id=device, device_id_type=MESH)
        pl.semaphore_wait(barrier, len(peers))
        running, a, b, c = [], 0, 0, 0
        for k, t in enumerate(tasks):
            running.append(
                t.body(
                    ins[a : a + n_in[k]], outs[b : b + n_out[k]], scr[c : c + n_scr[k]]
                )
            )
            a, b, c = a + n_in[k], b + n_out[k], c + n_scr[k]
        while running:
            again = []
            for g in running:
                if next(g, StopIteration) is not StopIteration:
                    again.append(g)
            running = again

    flat = pl.pallas_call(
        kernel,
        out_shape=[o[0] for t in tasks for o in t.outs],
        in_specs=[i[1] for t in tasks for i in t.ins],
        out_specs=[o[1] for t in tasks for o in t.outs],
        scratch_shapes=[s for t in tasks for s in t.scratch],
        compiler_params=pltpu.CompilerParams(
            collective_id=cid, has_side_effects=True, vmem_limit_bytes=40 << 20
        ),
        name=name,
    )(*[i[0] for t in tasks for i in t.ins])
    res, b = [], 0
    for n in n_out:
        res.append(flat[b : b + n])
        b += n
    return res


def gather_features(x):
    def body(ins, outs, scr):
        (x_ref,), (f_ref,), (send, recv, loc) = ins, outs, scr
        z, xl, xh, y, c = coords()
        links = Links(send, recv)

        def cols(xh_, y_, c_):
            return f_ref.at[:, pl.ds(pl.multiple_of((xh_ * 8 + y_ * 2 + c_) * 256, 256), 256)]

        core = place(z, xl, xh, y, 1 - c)
        own = cols(xh, y, c)
        keep = pltpu.make_async_copy(x_ref, own, loc.at[0])
        keep.start()
        sent, landed = [], []
        over_x = links.copy(x_ref, own, place(z, xl, 1 - xh, y, c))
        over_y = {d: links.copy(x_ref, own, place(z, xl, xh, ring(y, d), c)) for d in (2, 1, 3)}
        landed.append(links.copy(x_ref, own, core))
        yield 0
        over_x.wait_recv()
        far = cols(1 - xh, y, c)
        far_y = {d: links.copy(far, far, place(z, xl, xh, ring(y, d), c)) for d in (2, 1, 3)}
        landed.append(links.copy(far, far, core))
        yield 0
        for d in (1, 3, 2):
            over_y[d].wait_recv()
            got = cols(xh, ring(y, 4 - d), c)
            landed.append(links.copy(got, got, core))
        yield 0
        for d in (1, 3, 2):
            far_y[d].wait_recv()
            got = cols(1 - xh, ring(y, 4 - d), c)
            landed.append(links.copy(got, got, core))
        yield 0
        keep.wait()
        for cp in [over_x] + list(over_y.values()) + list(far_y.values()):
            cp.wait_send()
        for cp in landed:
            cp.wait()

    return Task(
        body, [(x, ANY)], [(jax.ShapeDtypeStruct((256, 4096), BF), ANY)], [], 15, 1, head_peers_ag
    )


def gather_queries(q):
    def body(ins, outs, scr):
        (q_ref,), (o_ref,), (send, recv, loc) = ins, outs, scr
        z, xl, xh, y, c = coords()
        links = Links(send, recv)
        own = o_ref.at[z * 2 + xl]
        keep = pltpu.make_async_copy(q_ref, own, loc.at[0])
        keep.start()
        over_x = links.copy(q_ref, own, place(z, 1 - xl, xh, y, c))
        over_z = [links.copy(q_ref, own, place(ring(z, d), xl, xh, y, c)) for d in (2, 1, 3)]
        yield 0
        over_x.wait_recv()
        far = o_ref.at[z * 2 + 1 - xl]
        over_z += [links.copy(far, far, place(ring(z, d), xl, xh, y, c)) for d in (2, 1, 3)]
        yield 0
        over_x.wait_send()
        for cp in over_z:
            cp.wait()
        keep.wait()

    return Task(
        body, [(q, ANY)], [(jax.ShapeDtypeStruct((8, 256, 256), BF), ANY)], [], 7, 1, tok_peers_ag
    )


def exchange_tok(*arrays):
    def body(ins, outs, scr):
        send, recv, loc = scr
        z, xl, xh, y, c = coords()
        t = z * 2 + xl
        links = Links(send, recv)
        keep, cps = [], []
        for k, (src, dst) in enumerate(zip(ins, outs)):
            keep.append(pltpu.make_async_copy(src.at[t], dst.at[t], loc.at[k]))
            keep[-1].start()
        for dx, dz in REL8:
            z_, xl_ = ring(z, dz), lax.rem(xl + dx, 2)
            for src, dst in zip(ins, outs):
                cps.append(links.copy(src.at[z_ * 2 + xl_], dst.at[t], place(z_, xl_, xh, y, c)))
        yield 0
        for cp in cps:
            cp.wait()
        for cp in keep:
            cp.wait()

    n = len(arrays)
    return Task(
        body,
        [(a, ANY) for a in arrays],
        [(jax.ShapeDtypeStruct(a.shape, a.dtype), ANY) for a in arrays],
        [],
        7 * n,
        n,
        tok_peers_all,
    )


def unit_rows(v):
    return v * lax.rsqrt(jnp.mean(v * v, axis=-1, keepdims=True) + EPSILON)


def reduce_layer(part, features, attn_gain, final_gain, first):
    def body(ins, outs, scr):
        part_ref, f_ref, again_ref = ins[:3]
        mine, theirs, came, xrow, send, recv, loc = scr
        z, xl, xh, y, c = coords()
        j = xh * 4 + y
        links = Links(send, recv)
        l0 = pltpu.make_async_copy(part_ref.at[:, c], mine, loc.at[0])
        l1 = pltpu.make_async_copy(
            f_ref.at[pl.ds(pl.multiple_of((j * 2 + c) * 16, 16), 16), :], xrow, loc.at[1]
        )
        l0.start()
        l1.start()
        swap = links.copy(part_ref.at[:, 1 - c], theirs, place(z, xl, xh, y, 1 - c))
        yield 0
        l0.wait()
        swap.wait_recv()
        cps = []
        for dx, dy in REL8:
            xh_, y_ = lax.rem(xh + dx, 2), ring(y, dy)
            j_ = xh_ * 4 + y_
            mine[j_] = (mine[j_].astype(F32) + theirs[j_].astype(F32)).astype(BF)
            cps.append(links.copy(mine.at[j_], came.at[j], place(z, xl, xh_, y_, c)))
        total = mine[j].astype(F32) + theirs[j].astype(F32)
        yield 0
        swap.wait_send()
        for cp in cps:
            cp.wait()
        for dx, dy in REL8:
            total = total + came[lax.rem(xh + dx, 2) * 4 + ring(y, dy)].astype(F32)
        l1.wait()
        states = (xrow[...].astype(F32) + unit_rows(total) * again_ref[...]).astype(BF)
        if not first:
            outs[0][...] = states
            return
        wide = states.astype(F32)
        squares = jnp.sum(wide * wide, axis=-1, keepdims=True)
        normed = wide * lax.rsqrt(squares * (1.0 / 4096) + EPSILON) * ins[3][...]
        outs[0][...] = normed.astype(BF)
        lane = lax.broadcasted_iota(jnp.int32, (8, 256), 1)
        row = lax.broadcasted_iota(jnp.int32, (8, 256), 0)
        outs[1][...] = jnp.where((lane == z * 2 + xl) & (row == 4), jnp.sum(squares), 0.0)

    ins = [(part, ANY), (features, ANY), (attn_gain, VM)]
    outs = [(jax.ShapeDtypeStruct((16, 4096), BF), VM)]
    if first:
        ins.append((final_gain, VM))
        outs.append((jax.ShapeDtypeStruct((8, 256), F32), VM))
    block = pltpu.VMEM((8, 16, 4096), BF)
    scratch = [block, block, block, pltpu.VMEM((16, 4096), BF)]
    return Task(body, ins, outs, scratch, 8, 2, head_peers_all)


def axis_peers():
    z, xl, xh, y, c = coords()
    x = xh * 2 + xl
    out = []
    for d in (1, 2, 3):
        x_ = ring(x, d)
        out.append(("x%d" % d, place(z, lax.rem(x_, 2), x_ // 2, y, c)))
        out.append(("y%d" % d, place(z, xl, xh, ring(y, d), c)))
        out.append(("z%d" % d, place(ring(z, d), xl, xh, y, c)))
    return out


def along(axis, d):
    z, xl, xh, y, c = coords()
    if axis == "x":
        x_ = ring(xh * 2 + xl, d)
        return place(z, lax.rem(x_, 2), x_ // 2, y, c)
    if axis == "y":
        return place(z, xl, xh, ring(y, d), c)
    return place(ring(z, d), xl, xh, y, c)


def gather_all(normed):
    spans = ((0, 1408), (1408, 1408), (2816, 1280))
    orders = (("x", "y", "z"), ("y", "z", "x"), ("z", "x", "y"))

    def body(ins, outs, scr):
        (n_ref,), (o_ref,), (send, recv, loc) = ins, outs, scr
        z, xl, xh, y, c = coords()
        links = Links(send, recv)
        full = slice(None)

        def block(known, cut):
            at = (
                full if "z" in known else z,
                full if "x" in known else xl,
                full if "x" in known else xh,
                full if "y" in known else y,
                full,
                pl.ds(*cut),
            )
            return o_ref.at[at]

        keep = pltpu.make_async_copy(n_ref, o_ref.at[z, xl, xh, y], loc.at[0])
        keep.start()
        sent = [[] for _ in spans]
        last = [[] for _ in spans]
        for p, cut in enumerate(spans):
            axis = orders[p][0]
            src, dst = n_ref.at[:, pl.ds(*cut)], block("", cut)
            last[p] = [links.copy(src, dst, along(axis, d)) for d in (2, 1, 3)]
        keep.wait()
        yield 0
        for stage in (1, 2):
            for p, cut in enumerate(spans):
                for cp in last[p]:
                    cp.wait_recv()
                sent[p] += last[p]
                ref = block("".join(orders[p][:stage]), cut)
                axis = orders[p][stage]
                last[p] = [links.copy(ref, ref, along(axis, d)) for d in (2, 1, 3)]
            yield 0
        for p in range(3):
            for cp in last[p]:
                cp.wait_recv()
            for cp in sent[p] + last[p]:
                cp.wait_send()

    return Task(
        body,
        [(normed, ANY)],
        [(jax.ShapeDtypeStruct((4, 2, 2, 4, 16, 4096), BF), ANY)],
        [],
        27,
        1,
        axis_peers,
    )


def reduce_best(best, squares):
    def body(ins, outs, scr):
        best_ref, sq_ref = ins
        out_ref, sum_ref = outs
        held, came, send, recv, loc = scr
        z, xl, xh, y, c = coords()
        links = Links(send, recv)
        held[0] = sq_ref[...]
        held[0, pl.ds(0, 4), :] = best_ref[...]
        top = lax.broadcasted_iota(jnp.int32, (8, 256), 0) < 4
        for s, axis in enumerate("xyz"):
            cps = [links.copy(held.at[s], came.at[s, d - 1], along(axis, d)) for d in (2, 1, 3)]
            for cp in cps:
                cp.wait()
            v = held[s]
            for d in range(3):
                w = came[s, d]
                v = jnp.where(top, jnp.maximum(v, w), v + w)
            held[s + 1] = v
        cp = links.copy(held.at[3], came.at[3, 0], place(z, xl, xh, y, 1 - c))
        cp.wait()
        v, w = held[3], came[3, 0]
        out_ref[c] = v
        out_ref[1 - c] = w
        sum_ref[...] = v + w
        yield 0

    def peers():
        z, xl, xh, y, c = coords()
        return axis_peers() + [("core", place(z, xl, xh, y, 1 - c))]

    return Task(
        body,
        [(best, VM), (squares, VM)],
        [
            (jax.ShapeDtypeStruct((2, 8, 256), F32), VM),
            (jax.ShapeDtypeStruct((8, 256), F32), VM),
        ],
        [pltpu.VMEM((4, 8, 256), F32), pltpu.VMEM((4, 3, 8, 256), F32)],
        10,
        1,
        peers,
    )


def project(x, w_query, w_key, w_value):
    steps = 4
    depth = x.shape[1] // steps
    rows = x.shape[0]

    def kernel(x_ref, a_ref, b_ref, c_ref, q_ref, k_ref, v_ref, acc):
        i = pl.program_id(0)
        xs = x_ref[...]
        for n, w_ref in enumerate((a_ref, b_ref, c_ref)):
            part = jnp.dot(xs, w_ref[...], preferred_element_type=F32)

            @pl.when(i == 0)
            def _():
                acc[n] = part

            @pl.when(i > 0)
            def _():
                acc[n] += part

        @pl.when(i == steps - 1)
        def _():
            for n, o_ref in enumerate((q_ref, k_ref, v_ref)):
                o_ref[...] = acc[n].astype(BF)

    wide = w_query.shape[1]
    weight = pl.BlockSpec((depth, wide), lambda i: (i, 0))
    out = pl.BlockSpec((rows, wide), lambda i: (0, 0))
    return pl.pallas_call(
        kernel,
        grid=(steps,),
        in_specs=[pl.BlockSpec((rows, depth), lambda i: (0, i)), weight, weight, weight],
        out_specs=[out] * 3,
        out_shape=[jax.ShapeDtypeStruct((rows, wide), BF)] * 3,
        scratch_shapes=[pltpu.VMEM((3, rows, wide), F32)],
        compiler_params=pltpu.CompilerParams(vmem_limit_bytes=32 << 20),
        name="project",
    )(x, w_query, w_key, w_value)


def scores(q, k):
    return lax.dot_general(q, k, (((1,), (1,)), ((), ())), preferred_element_type=F32) * SCALE2


def cached_attention(begins, ends, queries, keys, values):
    rows = queries.shape[1]
    span = 256

    def kernel(lo_ref, hi_ref, q_ref, k_ref, v_ref, o_ref, s_ref, m_sc, l_sc, a_sc):
        r = pl.program_id(0)
        lo, hi = lo_ref[r], hi_ref[r]
        m_sc[...] = jnp.full_like(m_sc, NEG)
        l_sc[...] = jnp.zeros_like(l_sc)
        a_sc[...] = jnp.zeros_like(a_sc)

        @pl.when(hi > lo)
        def _():
            def step(b, carry):
                at = pl.multiple_of(b * span, span)
                pos = at + lax.broadcasted_iota(jnp.int32, (rows, span), 1)
                valid = (pos >= lo) & (pos < hi)
                for g in range(2):
                    cut = slice(g * HEAD_DIM, (g + 1) * HEAD_DIM)
                    s = scores(q_ref[0, :, cut], k_ref[pl.ds(at, span), cut])
                    s = jnp.where(valid, s, NEG)
                    old = m_sc[g, :, 0:1]
                    new = jnp.maximum(old, jnp.max(s, axis=-1, keepdims=True))
                    p = jnp.where(valid, jnp.exp2(s - new), 0.0)
                    f = jnp.exp2(old - new)
                    l_sc[g] = l_sc[g] * f + jnp.sum(p, axis=-1, keepdims=True)
                    a_sc[g] = a_sc[g] * f + jnp.dot(
                        p.astype(BF), v_ref[pl.ds(at, span), cut], preferred_element_type=F32
                    )
                    m_sc[g] = jnp.broadcast_to(new, m_sc.shape[1:])
                return carry

            lax.fori_loop(lo // span, (hi + span - 1) // span, step, 0)

        lane = lax.broadcasted_iota(jnp.int32, (rows, 128), 1)
        stats = jnp.where(lane == 0, m_sc[0], jnp.where(lane == 1, m_sc[1], 0.0))
        stats = jnp.where(lane == 2, l_sc[0], jnp.where(lane == 3, l_sc[1], stats))
        s_ref[0] = jnp.transpose(stats)[:8]
        for g in range(2):
            o_ref[0, :, g * HEAD_DIM : (g + 1) * HEAD_DIM] = a_sc[g].astype(BF)

    whole = pl.BlockSpec(keys.shape, lambda r, a, b: (0, 0))
    per = pl.BlockSpec((1, rows, 256), lambda r, a, b: (r, 0, 0))
    return pl.pallas_call(
        kernel,
        grid_spec=pltpu.PrefetchScalarGridSpec(
            num_scalar_prefetch=2,
            grid=(8,),
            in_specs=[per, whole, whole],
            out_specs=[per, pl.BlockSpec((1, 8, rows), lambda r, a, b: (r, 0, 0))],
            scratch_shapes=[
                pltpu.VMEM((2, rows, 128), F32),
                pltpu.VMEM((2, rows, 128), F32),
                pltpu.VMEM((2, rows, HEAD_DIM), F32),
            ],
        ),
        out_shape=[
            jax.ShapeDtypeStruct((8, rows, 256), BF),
            jax.ShapeDtypeStruct((8, 8, rows), F32),
        ],
        compiler_params=pltpu.CompilerParams(vmem_limit_bytes=32 << 20),
        name="cached",
    )(begins, ends, queries, keys, values)


def combine(parts, stats, q, k, v, w_out):
    steps = 4
    wide = w_out.shape[1] // steps

    def kernel(p_ref, s_ref, q_ref, k_ref, v_ref, w_ref, o_ref, att):
        @pl.when(pl.program_id(0) == 0)
        def _():
            st = jnp.concatenate([s_ref[...].reshape(64, 256), jnp.zeros((64, 256), F32)], axis=0)
            st = jnp.transpose(st)
            for g in range(2):
                cut = slice(g * HEAD_DIM, (g + 1) * HEAD_DIM)
                s = scores(q_ref[:, cut], k_ref[:, cut])
                top = jnp.max(s, axis=-1, keepdims=True)
                for i in range(8):
                    top = jnp.maximum(top, st[:, i * 8 + g : i * 8 + g + 1])
                p = jnp.exp2(s - top)
                mass = jnp.sum(p, axis=-1, keepdims=True)
                acc = jnp.dot(p.astype(BF), v_ref[:, cut], preferred_element_type=F32)
                for i in range(8):
                    f = jnp.exp2(st[:, i * 8 + g : i * 8 + g + 1] - top)
                    mass = mass + f * st[:, i * 8 + g + 2 : i * 8 + g + 3]
                    acc = acc + f * p_ref[i, :, cut].astype(F32)
                att[:, cut] = (acc / mass).astype(BF)

        o = jnp.dot(att[...], w_ref[...], preferred_element_type=F32).astype(BF)
        o_ref[...] = o.reshape(o_ref.shape)

    def whole(a):
        return pl.BlockSpec(a.shape, lambda i: (0,) * a.ndim)

    return pl.pallas_call(
        kernel,
        grid=(steps,),
        in_specs=[whole(a) for a in (parts, stats, q, k, v)]
        + [pl.BlockSpec((256, wide), lambda i: (0, i))],
        out_specs=pl.BlockSpec((8, 2, 16, wide), lambda i: (0, 0, 0, i)),
        out_shape=jax.ShapeDtypeStruct((8, 2, 16, w_out.shape[1]), BF),
        scratch_shapes=[pltpu.VMEM((256, 256), BF)],
        compiler_params=pltpu.CompilerParams(vmem_limit_bytes=32 << 20),
        name="combine",
    )(parts, stats, q, k, v, w_out)


def best_logits(rows, own_head, other_head):
    vocab, width = own_head.shape

    def kernel(x_ref, a_ref, b_ref, o_ref):
        i = pl.program_id(0)
        x = x_ref[...]
        top = None
        for w_ref in (a_ref, b_ref):
            logits = lax.dot_general(
                w_ref[...], x, (((1,), (1,)), ((), ())), preferred_element_type=F32
            )
            m = jnp.max(logits, axis=0, keepdims=True)
            top = m if top is None else jnp.maximum(top, m)
        o_ref[pl.ds(i, 1), :] = top

    head = pl.BlockSpec((vocab, width), lambda i: (0, 0), pipeline_mode=pl.Buffered(1))
    return pl.pallas_call(
        kernel,
        grid=(4,),
        in_specs=[pl.BlockSpec((256, width), lambda i: (i, 0)), head, head],
        out_specs=pl.BlockSpec((4, 256), lambda i: (0, 0)),
        out_shape=jax.ShapeDtypeStruct((4, 256), F32),
        compiler_params=pltpu.CompilerParams(vmem_limit_bytes=50 << 20),
        name="logits",
    )(rows, own_head, other_head)


def shards(
    block_states,
    token_ids,
    accept,
    cache_lengths,
    cache_keys,
    cache_values,
    w_query,
    w_key,
    w_value,
    w_out,
    attn_gain,
    final_gain,
    embed,
    lm_head,
):
    tok = lax.axis_index("tok")
    other_head = lax.ppermute(lm_head, "head", [(i, i ^ 1) for i in range(16)])
    cache_here = cache_keys.shape[0]
    offsets = jnp.cumsum(cache_lengths) - cache_lengths - tok * cache_here
    begins = jnp.clip(offsets, 0, cache_here)
    ends = jnp.clip(offsets + cache_lengths, 0, cache_here)
    attn_gain = attn_gain.reshape(1, -1)
    final_gain = final_gain.reshape(1, -1)

    vocab_here = embed.shape[0]
    local_ids = token_ids - tok * vocab_here
    inside = (local_ids >= 0) & (local_ids < vocab_here)
    looked_up = jnp.take(embed, jnp.clip(local_ids, 0, vocab_here - 1), axis=0)
    looked_up = jnp.where(inside[:, None], looked_up, jnp.zeros_like(looked_up))

    (feat1,), (came,) = comm(
        [gather_features(block_states), exchange_tok(looked_up.reshape(8, 256, 256))], 0, "comm_a"
    )
    q1, k1, v1 = project(feat1, w_query, w_key, w_value)
    embedded = jnp.sum(came.astype(F32), axis=0).astype(BF)
    swapped = jnp.where((accept == 1)[:, None], embedded, block_states)

    (qs1,), (feat2,) = comm([gather_queries(q1), gather_features(swapped)], 1, "comm_b")
    part1, stat1 = cached_attention(begins, ends, qs1, cache_keys, cache_values)
    q2, k2, v2 = project(feat2, w_query, w_key, w_value)

    (part1, stat1), (qs2,) = comm([exchange_tok(part1, stat1), gather_queries(q2)], 2, "comm_c")
    sum1 = combine(part1, stat1, q1, k1, v1, w_out)
    part2, stat2 = cached_attention(begins, ends, qs2, cache_keys, cache_values)

    (normed, squares), (part2, stat2) = comm(
        [reduce_layer(sum1, feat1, attn_gain, final_gain, True), exchange_tok(part2, stat2)],
        3,
        "comm_d",
    )
    sum2 = combine(part2, stat2, q2, k2, v2, w_out)

    (rows,), (hiddens,) = comm(
        [gather_all(normed), reduce_layer(sum2, feat2, attn_gain, None, False)], 4, "comm_e"
    )
    best = best_logits(rows.reshape(-1, rows.shape[-1]), lm_head, other_head)
    ((top, sums),) = comm([reduce_best(best, squares)], 5, "comm_f")
    top_logits = top[:, :4].reshape(2, 64, 16).transpose(1, 0, 2).reshape(-1)
    request_norms = jnp.sqrt(sums[4, :8] / (256 * 4096))
    return (hiddens, request_norms, top_logits)


def solution(mesh):
    placed = (
        P("tok", "head"),
        P(),
        P("tok"),
        P(),
        P("tok", "head"),
        P("tok", "head"),
        P(None, "head"),
        P(None, "head"),
        P(None, "head"),
        P("head", None),
        P(),
        P(),
        P("tok", "head"),
        P(("tok", "head"), None),
    )
    return jax.shard_map(
        shards,
        mesh=mesh,
        in_specs=placed,
        out_specs=(P(("tok", "head"), None), P(), P()),
        check_vma=False,
    )
```

time: 834 us -> 263 us (0.32)
  waiting for transfers between devices: 659 us -> 0.01 us
  Pallas kernels: 0 us -> 232 us
  blocking collectives: 63.8 us -> 0 us
  matrix products: 41.5 us -> 0 us
  other arithmetic: 19.6 us -> 3.1 us
  between operations: 16.6 us -> 1.02 us
    all_gather x5 -> x0, waiting for transfers between devices: 434 us -> none  [the longest x1 214 us: shards(): row_piece = lax.all_gather(first_pass, ('tok', 'head'), axis=0, tiled=True)]
    pallas_call x0 -> x13, Pallas kernels: none -> 232 us  [the longest x6 175 us: comm(): pl.pallas_call(kernel, out_shape=[o[0] for t in tasks for o in t.outs], i...]
    reduce_scatter x3 -> x0, waiting for transfers between devices: 225 us -> none  [the longest x2 185 us: run_layer(): lax.psum_scatter(jnp.dot(attended, w_out, preferred_element_type=jnp.floa...]
    pmax x1 -> x0, blocking collectives: 63.8 us -> none  [shards(): top_logits = lax.pmax(top_local, ('tok', 'head'))]
    dot_general x18 -> x0, matrix products: 41.5 us -> none  [the longest x1 17.2 us: shards(): lax.dot_general(normed, lm_head, (((1,), (1,)), ((), ())), preferred_elem...]
    reduce_sum x7 -> x1, other arithmetic: 10.3 us -> 0.15 us  [shards(): embedded = jnp.sum(came.astype(F32), axis=0).astype(BF)]
    concatenate x2 -> x0, local copies, waits for them, and re-layouts: 9.18 us -> none  [the longest x1 4.61 us: shards(): gathered_values = jnp.concatenate([gathered_values, zero_rows], axis=0)]
  transfers between devices with their start and end apart: 8 -> 1, of which waited for: 8 -> 0; matrix products, arithmetic and copies ran while one was open for 4% -> 5% of each run, Pallas kernels for 0% -> 76%
where the time goes in v1:
time: 263 us
  Pallas kernels  232 us (88%)
  local copies, waits for them, and re-layouts  24.8 us (9%)
  other arithmetic  3.1 us (1%)
    pallas_call x6, Pallas kernels, comm(): pl.pallas_call(kernel, out_shape=[o[0] for t in tasks for o in t.outs], i...  175 us
    pallas_call x1, Pallas kernels, best_logits(): pl.pallas_call(kernel, grid=(4,), in_specs=[pl.BlockSpec((256, width), la...  19.4 us
    pallas_call x2, Pallas kernels, cached_attention(): pl.pallas_call(kernel, grid_spec=pltpu.PrefetchScalarGridSpec(num_scalar_...  17.8 us
    unnamed x53, local copies, waits for them, and re-layouts  13.7 us
    pallas_call x2, Pallas kernels, combine(): pl.pallas_call(kernel, grid=(steps,), in_specs=[whole(a) for a in (parts,...  10.3 us
    gather x1, local copies, waits for them, and re-layouts, shards(): looked_up = jnp.take(embed, jnp.clip(local_ids, 0, vocab_here - 1), axis=0)  10.3 us
    pallas_call x2, Pallas kernels, project(): pl.pallas_call(kernel, grid=(steps,), in_specs=[pl.BlockSpec((rows, depth...  10.1 us
  transfers between devices with their start and end apart: 1, of which 0 were waited for; matrix products, arithmetic and copies ran while one was open for 5% of the time, Pallas kernels for 76%

profile of v1, /device:TPU:1, one launch (start us, length us, event | category | flops | bytes accessed | tf_op | source)
XLA Modules:
  0.0 262.8 jit_solution(7819678305984022926)
XLA Ops:
  0.6 1.5 collective-permute-start
  2.1 0.7 compare_and_fusion.1
  2.9 0.7 fusion
  3.6 10.3 %gather_fusion = bf16[2048,256]{1,0:T(8,128)(2,1)S(1)} fusion(bf16[12544,256]{1,0:T(8,128)(2,1)} %param.26, s32[2048]{0:T(1024)S(1)} %fusion), kind=kCustom, calls=%fused_computation | custom fusion | bytes 2105344 | tf_op jit(solution)/shard_map/jit(_take)/gather | solution.py:634
  13.9 0.0 copy-start.15
  13.9 0.0 copy-start.1
  13.9 0.7 select_select_fusion.refs_1_
  14.6 0.2 copy-done.15
  14.8 23.1 %comm_a.1 = (bf16[256,4096]{1,0:T(8,128)(2,1)S(1)}, bf16[8,256,256]{2,1,0:T(8,128)(2,1)S(1)}) custom-call(bf16[256,256]{1,0:T(8,128)(2,1)S(1)} %copy-done.15, bf16[8,256,256]{2,1,0:T(8,128)(2,1)S(1)} %select_select_fusion.refs_1_), custom_call_target="tpu_custom_call" | custom-call | tf_op jit(solution)/shard_map/comm_a/pallas_call | solution.py:128
  37.9 1.3 copy-done.8
  39.2 0.1 reduce_sum.12
  39.4 0.0 copy-done.1
  39.4 0.0 copy-start.3
  39.4 1.6 copy-done.3
  41.0 1.6 copy-done.5
  42.6 1.6 copy-done.9
  44.2 5.1 %project.2 = (bf16[256,256]{1,0:T(8,128)(2,1)S(1)}, bf16[256,256]{1,0:T(8,128)(2,1)S(1)}, bf16[256,256]{1,0:T(8,128)(2,1)S(1)}) custom-call(bf16[256,4096]{1,0:T(8,128)(2,1)S(1)} %copy-done.9, bf16[4096,256]{1,0:T(8,128)(2,1)S(1)} %copy-done.1, bf16[4096,256]{1,0:T(8,128)(2,1)S(1)} %copy-done.3, bf16[4096,256]{1,0:T(8,128)(2,1)S(1)} %copy-done.5), custom_call_target="tpu_custom_call" | custom-call | tf_op jit(solution)/shard_map/project/pallas_call | solution.py:455
  49.2 0.0 copy-start.18
  49.3 0.1 broadcast_select_fusion.refs_1_
  49.4 0.5 copy-done.18
  49.9 0.0 copy-done.20
  49.9 21.9 %comm_b.1 = (bf16[8,256,256]{2,1,0:T(8,128)(2,1)S(1)}, bf16[256,4096]{1,0:T(8,128)(2,1)S(1)}) custom-call(bf16[256,256]{1,0:T(8,128)(2,1)S(1)} %get-tuple-element.29.refs_0_.q_ref, bf16[256,256]{1,0:T(8,128)(2,1)S(1)} %broadcast_select_fusion.refs_1_), custom_call_target="tpu_custom_call" | custom-call | tf_op jit(solution)/shard_map/comm_b/pallas_call | solution.py:128
  71.9 1.0 copy-done.13
  72.8 0.0 copy-start.11
  72.9 0.0 copy-start.12
  72.9 5.1 %project.3 = (bf16[256,256]{1,0:T(8,128)(2,1)S(1)}, bf16[256,256]{1,0:T(8,128)(2,1)S(1)}, bf16[256,256]{1,0:T(8,128)(2,1)S(1)}) custom-call(bf16[256,4096]{1,0:T(8,128)(2,1)S(1)} %get-tuple-element.34.x_ref.refs_2_, bf16[4096,256]{1,0:T(8,128)(2,1)S(1)} %copy-done.2, bf16[4096,256]{1,0:T(8,128)(2,1)S(1)} %copy-done.4, bf16[4096,256]{1,0:T(8,128)(2,1)S(1)} %copy-done.6), custom_call_target="tpu_custom_call" | custom-call | tf_op jit(solution)/shard_map/project/pallas_call | solution.py:455
  77.9 0.6 copy-done.16
  78.6 0.2 reduce-window.9
  78.8 1.2 copy-done.14
  80.0 8.9 %cached.2 = (bf16[8,256,256]{2,1,0:T(8,128)(2,1)S(1)}, f32[8,8,256]{2,1,0:T(8,128)S(1)}) custom-call(s32[8]{0:T(128)S(1)} %get-tuple-element.56.lo_ref, s32[8]{0:T(128)S(1)} %get-tuple-element.55.hi_ref, bf16[8,256,256]{2,1,0:T(8,128)(2,1)S(1)} %copy-done.14, bf16[1024,256]{1,0:T(8,128)(2,1)S(1)} %copy-done.11, bf16[1024,256]{1,0:T(8,128)(2,1)S(1)} %copy-done.12), custom_call_target="tpu_custom_call" | custom-call | tf_op jit(solution)/shard_map/cached/pallas_call | solution.py:514
  88.9 0.0 copy-start.19
  89.0 27.5 %comm_c.1 = (bf16[8,256,256]{2,1,0:T(8,128)(2,1)S(1)}, f32[8,8,256]{2,1,0:T(8,128)S(1)}, bf16[8,256,256]{2,1,0:T(8,128)(2,1)S(1)}) custom-call(bf16[8,256,256]{2,1,0:T(8,128)(2,1)S(1)} %get-tuple-element.32.refs_0_, f32[8,8,256]{2,1,0:T(8,128)S(1)} %get-tuple-element.33.refs_1_, bf16[256,256]{1,0:T(8,128)(2,1)S(1)} %get-tuple-element.35.refs_2_.q_ref), custom_call_target="tpu_custom_call" | custom-call | tf_op jit(solution)/shard_map/comm_c/pallas_call | solution.py:128
  116.5 8.9 %cached.3 = (bf16[8,256,256]{2,1,0:T(8,128)(2,1)S(1)}, f32[8,8,256]{2,1,0:T(8,128)S(1)}) custom-call(s32[8]{0:T(128)S(1)} %get-tuple-element.56.lo_ref, s32[8]{0:T(128)S(1)} %get-tuple-element.55.hi_ref, bf16[8,256,256]{2,1,0:T(8,128)(2,1)S(1)} %get-tuple-element.40.q_ref, bf16[1024,256]{1,0:T(8,128)(2,1)S(1)} %copy-done.11, bf16[1024,256]{1,0:T(8,128)(2,1)S(1)} %copy-done.12), custom_call_target="tpu_custom_call" | custom-call | tf_op jit(solution)/shard_map/cached/pallas_call | solution.py:514
  125.5 0.0 copy-start.22
  125.5 0.0 copy-start.23
  125.5 5.1 %combine.2.refs_0_ = bf16[8,2,16,4096]{3,2,1,0:T(8,128)(2,1)S(1)} custom-call(bf16[8,256,256]{2,1,0:T(8,128)(2,1)S(1)} %get-tuple-element.36.p_ref, f32[8,8,256]{2,1,0:T(8,128)S(1)} %get-tuple-element.37.s_ref, bf16[256,256]{1,0:T(8,128)(2,1)S(1)} %get-tuple-element.29.refs_0_.q_ref, bf16[256,256]{1,0:T(8,128)(2,1)S(1)} %copy-done.19, ...), custom_call_target="tpu_custom_call" | custom-call | tf_op jit(solution)/shard_map/combine/pallas_call | solution.py:566
  130.6 29.5 %comm_d.1 = (bf16[16,4096]{1,0:T(8,128)(2,1)S(1)}, f32[8,256]{1,0:T(8,128)S(1)}, bf16[8,256,256]{2,1,0:T(8,128)(2,1)S(1)}, f32[8,8,256]{2,1,0:T(8,128)S(1)}) custom-call(bf16[8,2,16,4096]{3,2,1,0:T(8,128)(2,1)S(1)} %combine.2.refs_0_, bf16[256,4096]{1,0:T(8,128)(2,1)S(1)} %copy-done.10, f32[1,4096]{1,0:T(1,128)S(1)} %bitcast.17, f32[1,4096]{1,0:T(1,128)S(1)} %bitcast.19, ...), custom_call_target="tpu_custom_call" | custom-call | tf_op jit(solution)/shard_map/comm_d/pallas_call | solution.py:128
  160.1 5.2 %combine.3.refs_1_ = bf16[8,2,16,4096]{3,2,1,0:T(8,128)(2,1)S(1)} custom-call(bf16[8,256,256]{2,1,0:T(8,128)(2,1)S(1)} %get-tuple-element.44.p_ref, f32[8,8,256]{2,1,0:T(8,128)S(1)} %get-tuple-element.45.s_ref, bf16[256,256]{1,0:T(8,128)(2,1)S(1)} %get-tuple-element.35.refs_2_.q_ref, bf16[256,256]{1,0:T(8,128)(2,1)S(1)} %get-tuple-element.46.k_ref, ...), custom_call_target="tpu_custom_call" | custom-call | tf_op jit(solution)/shard_map/combine/pallas_call | solution.py:566
  165.4 59.4 %comm_e.1 = (bf16[4,2,2,4,16,4096]{5,4,3,2,1,0:T(8,128)(2,1)S(1)}, bf16[16,4096]{1,0:T(8,128)(2,1)S(1)}) custom-call(bf16[16,4096]{1,0:T(8,128)(2,1)S(1)} %get-tuple-element.43.refs_0_, bf16[8,2,16,4096]{3,2,1,0:T(8,128)(2,1)S(1)} %combine.3.refs_1_, bf16[256,4096]{1,0:T(8,128)(2,1)S(1)} %get-tuple-element.34.x_ref.refs_2_, f32[1,4096]{1,0:T(1,128)S(1)} %bitcast.18), custom_call_target="tpu_custom_call" | custom-call | tf_op jit(solution)/shard_map/comm_e/pallas_call | solution.py:128
  224.8 3.3 %copy-done = bf16[4,2,2,4,16,4096]{5,4,3,2,1,0:T(8,128)(2,1)} copy-done((bf16[4,2,2,4,16,4096]{5,4,3,2,1,0:T(8,128)(2,1)}, bf16[4,2,2,4,16,4096]{5,4,3,2,1,0:T(8,128)(2,1)S(1)}, u32[]{:S(2)}) %copy-start) | copy-done | bytes 8388632
  228.0 0.0 collective-permute-done.b_ref
  228.0 19.4 %logits.1.refs_0_ = f32[4,256]{1,0:T(4,128)S(1)} custom-call(bf16[1024,4096]{1,0:T(8,128)(2,1)} %bitcast.16, bf16[784,4096]{1,0:T(8,128)(2,1)} %a_ref.5, bf16[784,4096]{1,0:T(8,128)(2,1)} %collective-permute-done.b_ref), custom_call_target="tpu_custom_call" | custom-call | tf_op jit(solution)/shard_map/logits/pallas_call | solution.py:595
  247.5 13.3 %comm_f.1 = (f32[2,8,256]{2,1,0:T(8,128)S(1)}, f32[8,256]{1,0:T(8,128)S(1)}) custom-call(f32[4,256]{1,0:T(4,128)S(1)} %logits.1.refs_0_, f32[8,256]{1,0:T(8,128)S(1)} %get-tuple-element.50.refs_1_), custom_call_target="tpu_custom_call" | custom-call | tf_op jit(solution)/shard_map/comm_f/pallas_call | solution.py:128
  260.8 0.5 sqrt_bitcast_fusion
  261.3 0.1 reshape.74
  261.4 0.1 copy.17
  261.4 0.7 reshape.75
  262.2 0.7 copy.19
  (36 shorter events, 0.1 us)
Async XLA Ops:
  0.6 227.4 %collective-permute-start = (bf16[784,4096]{1,0:T(8,128)(2,1)}, bf16[784,4096]{1,0:T(8,128)(2,1)}, u32[]{:S(2)}, u32[]{:S(2)}) collective-permute-start(bf16[784,4096]{1,0:T(8,128)(2,1)} %a_ref.5), channel_id=1, source_target_pairs={{0,1},{1,0},{2,3},{3,2},{4,5},{5,4},{6,7},{7,6},{8,9},{9,8},{10,11... | collective-permute-start | bytes 19267592 | tf_op jit(solution)/shard_map/ppermute | solution.py:623
  13.9 0.9 copy-start.15
  13.9 25.5 %copy-start.1 = (bf16[4096,256]{1,0:T(8,128)(2,1)S(1)}, bf16[4096,256]{1,0:T(8,128)(2,1)}, u32[]{:S(2)}) copy-start(bf16[4096,256]{1,0:T(8,128)(2,1)} %a_ref.4) | copy-start | bytes 6291460
  37.9 1.4 copy-start.8
  39.4 1.6 copy-start.3
  41.0 1.6 copy-start.5
  42.6 1.6 copy-start.9
  44.2 5.1 %copy-start.25 = (s32[256]{0:T(256)S(1)}, s32[256]{0:T(256)}, u32[]{:S(2)}) copy-start(s32[256]{0:T(256)} %param.16) | copy-start | bytes 3076
  44.2 28.7 %copy-start.2 = (bf16[4096,256]{1,0:T(8,128)(2,1)S(1)}, bf16[4096,256]{1,0:T(8,128)(2,1)}, u32[]{:S(2)}) copy-start(bf16[4096,256]{1,0:T(8,128)(2,1)} %a_ref.4) | copy-start | bytes 6291460
  44.2 28.7 %copy-start.4 = (bf16[4096,256]{1,0:T(8,128)(2,1)S(1)}, bf16[4096,256]{1,0:T(8,128)(2,1)}, u32[]{:S(2)}) copy-start(bf16[4096,256]{1,0:T(8,128)(2,1)} %b_ref.3) | copy-start | bytes 6291460
  44.2 28.7 %copy-start.6 = (bf16[4096,256]{1,0:T(8,128)(2,1)S(1)}, bf16[4096,256]{1,0:T(8,128)(2,1)}, u32[]{:S(2)}) copy-start(bf16[4096,256]{1,0:T(8,128)(2,1)} %c_ref.3) | copy-start | bytes 6291460
  49.2 0.7 copy-start.18
  49.3 0.7 copy-start.20
  71.8 1.0 copy-start.13
  72.8 5.7 %copy-start.24 = (s32[8]{0:T(128)S(1)}, s32[8]{0:T(128)}, u32[]{:S(2)}) copy-start(s32[8]{0:T(128)} %param.17) | copy-start | bytes 100
  72.8 5.9 %copy-start.11 = (bf16[1024,256]{1,0:T(8,128)(2,1)S(1)}, bf16[1024,256]{1,0:T(8,128)(2,1)}, u32[]{:S(2)}) copy-start(bf16[1024,256]{1,0:T(8,128)(2,1)} %k_ref.3) | copy-start | bytes 1572868
  72.9 5.9 %copy-start.12 = (bf16[1024,256]{1,0:T(8,128)(2,1)S(1)}, bf16[1024,256]{1,0:T(8,128)(2,1)}, u32[]{:S(2)}) copy-start(bf16[1024,256]{1,0:T(8,128)(2,1)} %v_ref.3) | copy-start | bytes 1572868
  77.9 0.6 copy-start.16
  78.8 1.2 copy-start.14
  88.9 36.5 %copy-start.7 = (bf16[256,4096]{1,0:T(8,128)(2,1)S(1)}, bf16[256,4096]{1,0:T(8,128)(2,1)}, u32[]{:S(2)}) copy-start(bf16[256,4096]{1,0:T(8,128)(2,1)} %w_ref.3) | copy-start | bytes 6291460
  88.9 36.5 %copy-start.19 = (bf16[256,256]{1,0:T(8,128)(2,1)S(1)}, bf16[256,256]{1,0:T(8,128)(2,1)}, u32[]{:S(2)}) copy-start(bf16[256,256]{1,0:T(8,128)(2,1)} %copy-done.18) | copy-start | bytes 393220
  88.9 36.5 %copy-start.21 = (bf16[256,256]{1,0:T(8,128)(2,1)S(1)}, bf16[256,256]{1,0:T(8,128)(2,1)}, u32[]{:S(2)}) copy-start(bf16[256,256]{1,0:T(8,128)(2,1)} %copy-done.20) | copy-start | bytes 393220
  125.4 5.1 %copy-start.10 = (bf16[256,4096]{1,0:T(8,128)(2,1)S(1)}, bf16[256,4096]{1,0:T(8,128)(2,1)}, u32[]{:S(2)}) copy-start(bf16[256,4096]{1,0:T(8,128)(2,1)} %copy-done.8) | copy-start | bytes 6291460
  125.5 5.1 %copy-start.22 = (f32[4096]{0:T(1024)S(1)}, f32[4096]{0:T(1024)}, u32[]{:S(2)}) copy-start(f32[4096]{0:T(1024)} %param.24) | copy-start | bytes 49156
  125.5 5.1 %copy-start.23 = (f32[4096]{0:T(1024)S(1)}, f32[4096]{0:T(1024)}, u32[]{:S(2)}) copy-start(f32[4096]{0:T(1024)} %param.25) | copy-start | bytes 49156
  130.6 29.5 %copy-start.17 = (bf16[256,256]{1,0:T(8,128)(2,1)S(1)}, bf16[256,256]{1,0:T(8,128)(2,1)}, u32[]{:S(2)}) copy-start(bf16[256,256]{1,0:T(8,128)(2,1)} %copy-done.16) | copy-start | bytes 393220
  224.7 3.3 %copy-start = (bf16[4,2,2,4,16,4096]{5,4,3,2,1,0:T(8,128)(2,1)}, bf16[4,2,2,4,16,4096]{5,4,3,2,1,0:T(8,128)(2,1)S(1)}, u32[]{:S(2)}) copy-start(bf16[4,2,2,4,16,4096]{5,4,3,2,1,0:T(8,128)(2,1)S(1)} %get-tuple-element.49) | copy-start | bytes 25165828

commit v2 on v1

--- a/solution.py
+++ b/solution.py
@@ -63,38 +63,26 @@
         self.peers = peers
 
 
-def head_peers_ag():
+def shift(dx, dy, dz, dc):
     z, xl, xh, y, c = coords()
-    out = [("core", place(z, xl, xh, y, 1 - c)), ("x2", place(z, xl, 1 - xh, y, c))]
-    return out + [("y%d" % d, place(z, xl, xh, ring(y, d), c)) for d in (1, 2, 3)]
-
-
-def head_peers_all():
-    z, xl, xh, y, c = coords()
-    out = [("core", place(z, xl, xh, y, 1 - c))]
-    return out + [
-        ("h%d%d" % (dx, dy), place(z, xl, lax.rem(xh + dx, 2), ring(y, dy), c)) for dx, dy in REL8
-    ]
-
-
-def tok_peers_ag():
-    z, xl, xh, y, c = coords()
-    out = [("x1", place(z, 1 - xl, xh, y, c))]
-    return out + [("z%d" % d, place(ring(z, d), xl, xh, y, c)) for d in (1, 2, 3)]
-
-
-def tok_peers_all():
-    z, xl, xh, y, c = coords()
-    return [
-        ("t%d%d" % (dx, dz), place(ring(z, dz), lax.rem(xl + dx, 2), xh, y, c)) for dx, dz in REL8
-    ]
-
-
-CANON = {"h10": "x2", "h01": "y1", "h02": "y2", "h03": "y3"}
-CANON.update({"t10": "x1", "t01": "z1", "t02": "z2", "t03": "z3"})
-
-
-def comm(tasks, cid, name):
+    c_ = lax.rem(c + dc, 2)
+    if dx == "s":
+        return place(ring(z, dz), 1 - xl, xh, ring(y, dy), c_)
+    x_ = ring(xh * 2 + xl, dx)
+    return place(ring(z, dz), lax.rem(x_, 2), x_ // 2, ring(y, dy), c_)
+
+
+HEAD_AG = [(0, 0, 0, 1), (2, 0, 0, 0), (0, 1, 0, 0), (0, 2, 0, 0), (0, 3, 0, 0)]
+HEAD_ALL = [(0, 0, 0, 1)] + [(2 * dx, dy, 0, 0) for dx, dy in REL8]
+TOK_AG = [("s", 0, 0, 0), (0, 0, 1, 0), (0, 0, 2, 0), (0, 0, 3, 0)]
+TOK_ALL = [("s" if dx else 0, 0, dz, 0) for dx, dz in REL8]
+AXES = [(d, 0, 0, 0) for d in (1, 2, 3)] + [(0, d, 0, 0) for d in (1, 2, 3)]
+AXES += [(0, 0, d, 0) for d in (1, 2, 3)]
+PLANE = [(k // 4, k % 4, 0, 0) for k in range(1, 16)]
+DEEP = [(0, 0, k % 4, k // 4) for k in range(1, 8)]
+
+
+def comm(tasks, cid, name, vmem=4):
     n_in = [len(t.ins) for t in tasks]
     n_out = [len(t.outs) for t in tasks]
     n_scr = [len(t.scratch) for t in tasks]
@@ -104,8 +92,8 @@
         outs, scr = rest[: sum(n_out)], rest[sum(n_out) :]
         peers = {}
         for t in tasks:
-            for key, device in t.peers():
-                peers.setdefault(CANON.get(key, key), device)
+            for key in t.peers:
+                peers.setdefault(key, shift(*key))
         barrier = pltpu.get_barrier_semaphore()
         for device in peers.values():
             pl.semaphore_signal(barrier, inc=1, device_id=device, device_id_type=MESH)
@@ -132,7 +120,7 @@
         out_specs=[o[1] for t in tasks for o in t.outs],
         scratch_shapes=[s for t in tasks for s in t.scratch],
         compiler_params=pltpu.CompilerParams(
-            collective_id=cid, has_side_effects=True, vmem_limit_bytes=40 << 20
+            collective_id=cid, has_side_effects=True, vmem_limit_bytes=vmem << 20
         ),
         name=name,
     )(*[i[0] for t in tasks for i in t.ins])
@@ -150,7 +138,7 @@
         links = Links(send, recv)
 
         def cols(xh_, y_, c_):
-            return f_ref.at[:, pl.ds(pl.multiple_of((xh_ * 8 + y_ * 2 + c_) * 256, 256), 256)]
+            return f_ref.at[xh_ * 8 + y_ * 2 + c_]
 
         core = place(z, xl, xh, y, 1 - c)
         own = cols(xh, y, c)
@@ -183,7 +171,7 @@
             cp.wait()
 
     return Task(
-        body, [(x, ANY)], [(jax.ShapeDtypeStruct((256, 4096), BF), ANY)], [], 15, 1, head_peers_ag
+        body, [(x, ANY)], [(jax.ShapeDtypeStruct((16, 256, 256), BF), ANY)], [], 15, 1, HEAD_AG
     )
 
 
@@ -208,7 +196,7 @@
         keep.wait()
 
     return Task(
-        body, [(q, ANY)], [(jax.ShapeDtypeStruct((8, 256, 256), BF), ANY)], [], 7, 1, tok_peers_ag
+        body, [(q, ANY)], [(jax.ShapeDtypeStruct((8, 256, 256), BF), ANY)], [], 7, 1, TOK_AG
     )
 
 
@@ -240,7 +228,7 @@
         [],
         7 * n,
         n,
-        tok_peers_all,
+        TOK_ALL,
     )
 
 
@@ -248,38 +236,66 @@
     return v * lax.rsqrt(jnp.mean(v * v, axis=-1, keepdims=True) + EPSILON)
 
 
-def reduce_layer(part, features, attn_gain, final_gain, first):
+def reduce_layer(part, features, attn_gain, final_gain, first, y_first):
     def body(ins, outs, scr):
         part_ref, f_ref, again_ref = ins[:3]
-        mine, theirs, came, xrow, send, recv, loc = scr
+        mine, theirs, came, far, xrow, send, recv, loc = scr
         z, xl, xh, y, c = coords()
-        j = xh * 4 + y
+        h = xh * 8 + y * 2 + c
         links = Links(send, recv)
-        l0 = pltpu.make_async_copy(part_ref.at[:, c], mine, loc.at[0])
+        l0 = pltpu.make_async_copy(part_ref.at[:, :, c], mine, loc.at[0])
         l1 = pltpu.make_async_copy(
-            f_ref.at[pl.ds(pl.multiple_of((j * 2 + c) * 16, 16), 16), :], xrow, loc.at[1]
+            f_ref.at[:, pl.ds(pl.multiple_of(h * 16, 16), 16), :], xrow, loc.at[1]
         )
+        swap = links.copy(part_ref.at[:, :, 1 - c], theirs, place(z, xl, xh, y, 1 - c))
         l0.start()
         l1.start()
-        swap = links.copy(part_ref.at[:, 1 - c], theirs, place(z, xl, xh, y, 1 - c))
         yield 0
         l0.wait()
         swap.wait_recv()
         cps = []
-        for dx, dy in REL8:
-            xh_, y_ = lax.rem(xh + dx, 2), ring(y, dy)
-            j_ = xh_ * 4 + y_
-            mine[j_] = (mine[j_].astype(F32) + theirs[j_].astype(F32)).astype(BF)
-            cps.append(links.copy(mine.at[j_], came.at[j], place(z, xl, xh_, y_, c)))
-        total = mine[j].astype(F32) + theirs[j].astype(F32)
-        yield 0
+
+        def both(xh_, y_):
+            return mine[xh_, y_].astype(F32) + theirs[xh_, y_].astype(F32)
+
+        if y_first:
+            for dy in (2, 1, 3):
+                y_ = ring(y, dy)
+                for xh_ in (0, 1):
+                    mine[xh_, y_] = both(xh_, y_).astype(BF)
+                cps.append(links.copy(mine.at[:, y_], came.at[:, y], place(z, xl, xh, y_, c)))
+            total, away = both(xh, y), both(1 - xh, y)
+            yield 0
+            for cp in cps:
+                cp.wait_recv()
+            for dy in (1, 3, 2):
+                y_ = ring(y, dy)
+                away = away + came[1 - xh, y_].astype(F32)
+                total = total + came[xh, y_].astype(F32)
+            mine[1 - xh, y] = away.astype(BF)
+            over = links.copy(mine.at[1 - xh, y], far, place(z, xl, 1 - xh, y, c))
+            yield 0
+            over.wait()
+            total = total + far[...].astype(F32)
+            for cp in cps:
+                cp.wait_send()
+        else:
+            for dx, dy in REL8:
+                xh_, y_ = lax.rem(xh + dx, 2), ring(y, dy)
+                mine[xh_, y_] = both(xh_, y_).astype(BF)
+                cps.append(
+                    links.copy(mine.at[xh_, y_], came.at[xh, y], place(z, xl, xh_, y_, c))
+                )
+            total = both(xh, y)
+            yield 0
+            for cp in cps:
+                cp.wait()
+            for dx, dy in REL8:
+                total = total + came[lax.rem(xh + dx, 2), ring(y, dy)].astype(F32)
         swap.wait_send()
-        for cp in cps:
-            cp.wait()
-        for dx, dy in REL8:
-            total = total + came[lax.rem(xh + dx, 2) * 4 + ring(y, dy)].astype(F32)
         l1.wait()
-        states = (xrow[...].astype(F32) + unit_rows(total) * again_ref[...]).astype(BF)
+        before = jnp.concatenate([xrow[k] for k in range(16)], axis=1).astype(F32)
+        states = (before + unit_rows(total) * again_ref[...]).astype(BF)
         if not first:
             outs[0][...] = states
             return
@@ -296,87 +312,151 @@
     if first:
         ins.append((final_gain, VM))
         outs.append((jax.ShapeDtypeStruct((8, 256), F32), VM))
-    block = pltpu.VMEM((8, 16, 4096), BF)
-    scratch = [block, block, block, pltpu.VMEM((16, 4096), BF)]
-    return Task(body, ins, outs, scratch, 8, 2, head_peers_all)
-
-
-def axis_peers():
-    z, xl, xh, y, c = coords()
-    x = xh * 2 + xl
-    out = []
-    for d in (1, 2, 3):
-        x_ = ring(x, d)
-        out.append(("x%d" % d, place(z, lax.rem(x_, 2), x_ // 2, y, c)))
-        out.append(("y%d" % d, place(z, xl, xh, ring(y, d), c)))
-        out.append(("z%d" % d, place(ring(z, d), xl, xh, y, c)))
-    return out
+    block = pltpu.VMEM((2, 4, 16, 4096), BF)
+    scratch = [block, block, block, pltpu.VMEM((16, 4096), BF), pltpu.VMEM((16, 16, 256), BF)]
+    return Task(body, ins, outs, scratch, 8, 2, HEAD_AG if y_first else HEAD_ALL)
 
 
 def along(axis, d):
-    z, xl, xh, y, c = coords()
-    if axis == "x":
-        x_ = ring(xh * 2 + xl, d)
-        return place(z, lax.rem(x_, 2), x_ // 2, y, c)
-    if axis == "y":
-        return place(z, xl, xh, ring(y, d), c)
-    return place(ring(z, d), xl, xh, y, c)
-
-
-def gather_all(normed):
-    spans = ((0, 1408), (1408, 1408), (2816, 1280))
-    orders = (("x", "y", "z"), ("y", "z", "x"), ("z", "x", "y"))
+    return shift(*{"x": (d, 0, 0, 0), "y": (0, d, 0, 0), "z": (0, 0, d, 0)}[axis])
+
+
+CHUNKS = ((384, 384, 256), (384, 256, 384), (256, 384, 384), (384, 384, 256))
+ORDERS = ("xyz", "yzx", "zxy")
+
+
+def gather_logits(normed, own_head, other_head):
+    vocab = own_head.shape[0]
 
     def body(ins, outs, scr):
-        (n_ref,), (o_ref,), (send, recv, loc) = ins, outs, scr
+        n_ref, own_ref, other_ref = ins
+        (best_ref,) = outs
+        bufs = [scr[3 * i : 3 * i + 3] for i in range(4)]
+        heads, acc, send, recv, loc = scr[12:]
         z, xl, xh, y, c = coords()
+        x = xh * 2 + xl
         links = Links(send, recv)
         full = slice(None)
-
-        def block(known, cut):
-            at = (
-                full if "z" in known else z,
-                full if "x" in known else xl,
-                full if "x" in known else xh,
-                full if "y" in known else y,
-                full,
-                pl.ds(*cut),
-            )
-            return o_ref.at[at]
-
-        keep = pltpu.make_async_copy(n_ref, o_ref.at[z, xl, xh, y], loc.at[0])
-        keep.start()
-        sent = [[] for _ in spans]
-        last = [[] for _ in spans]
-        for p, cut in enumerate(spans):
-            axis = orders[p][0]
-            src, dst = n_ref.at[:, pl.ds(*cut)], block("", cut)
-            last[p] = [links.copy(src, dst, along(axis, d)) for d in (2, 1, 3)]
-        keep.wait()
-        yield 0
-        for stage in (1, 2):
-            for p, cut in enumerate(spans):
-                for cp in last[p]:
+        loads = [
+            pltpu.make_async_copy(src, heads.at[k], loc.at[k])
+            for k, src in enumerate((own_ref, other_ref))
+        ]
+
+        def block(i, p, known, step=0, half=None):
+            last = ORDERS[p][2]
+            z_, y_, x_ = z, y, x
+            if step:
+                if last == "z":
+                    z_ = ring(z, step)
+                elif last == "y":
+                    y_ = ring(y, step)
+                else:
+                    x_ = ring(x, step)
+            at = [
+                full if "z" in known else z_,
+                full if "x" in known else lax.rem(x_, 2),
+                full if "x" in known else x_ // 2,
+                full if "y" in known else y_,
+            ]
+            if half is not None:
+                if last == "z":
+                    at[1] = half
+                else:
+                    at[0] = pl.ds(2 * half, 2)
+            return bufs[i][p].at[tuple(at)]
+
+        start = 0
+        for i in range(4):
+            for p in range(3):
+                bufs[i][p][z, xl, xh, y] = n_ref[:, start : start + CHUNKS[i][p]]
+                start += CHUNKS[i][p]
+
+        everything = []
+
+        def push(i, p, ref, axis, d):
+            cp = links.copy(ref, ref, along(axis, d))
+            everything.append(cp)
+            return cp
+
+        def spread(i, stage, before):
+            out = []
+            for p in range(3):
+                if before is not None:
+                    for cp in before[p]:
+                        cp.wait_recv()
+                ref = block(i, p, ORDERS[p][:stage])
+                ds = (2, 1, 3) if stage < 2 else (1, 3)
+                out.append([push(i, p, ref, ORDERS[p][stage], d) for d in ds])
+            return out
+
+        def relay(i, before):
+            out = []
+            for p in range(3):
+                axis, known = ORDERS[p][2], ORDERS[p][:2]
+                before[p][0].wait_recv()
+                lower = push(i, p, block(i, p, known, 3, 0), axis, 1)
+                before[p][1].wait_recv()
+                upper = push(i, p, block(i, p, known, 1, 1), axis, 3)
+                out.append([lower, upper])
+            return out
+
+        def multiply(i):
+            cut = pl.ds(1024 * i, 1024)
+
+            def step(r, carry):
+                rows = jnp.concatenate(
+                    [bufs[i][p][r].reshape(256, CHUNKS[i][p]) for p in range(3)], axis=1
+                )
+                top = None
+                for k in range(2):
+                    part = lax.dot_general(
+                        heads[k, :, cut], rows, (((1,), (1,)), ((), ())), preferred_element_type=F32
+                    )
+                    if i > 0:
+                        part = acc[k, r] + part
+                    if i < 3:
+                        acc[k, r] = part
+                    else:
+                        m = jnp.max(part, axis=0, keepdims=True)
+                        top = m if top is None else jnp.maximum(top, m)
+                if i == 3:
+                    best_ref[pl.ds(r, 1), :] = top
+                return carry
+
+            lax.fori_loop(0, 4, step, 0)
+
+        one = [spread(i, 0, None) for i in range(4)]
+        for cp in loads:
+            cp.start()
+        two = [spread(i, 1, one[i]) for i in range(4)]
+        three = {0: spread(0, 2, two[0]), 1: spread(1, 2, two[1])}
+        four = {0: relay(0, three[0])}
+        for i in range(4):
+            if i + 1 < 4:
+                four[i + 1] = relay(i + 1, three[i + 1])
+            if i + 2 < 4:
+                three[i + 2] = spread(i + 2, 2, two[i + 2])
+            for pair in four[i]:
+                for cp in pair:
                     cp.wait_recv()
-                sent[p] += last[p]
-                ref = block("".join(orders[p][:stage]), cut)
-                axis = orders[p][stage]
-                last[p] = [links.copy(ref, ref, along(axis, d)) for d in (2, 1, 3)]
-            yield 0
-        for p in range(3):
-            for cp in last[p]:
-                cp.wait_recv()
-            for cp in sent[p] + last[p]:
-                cp.wait_send()
-
+            if i == 0:
+                for cp in loads:
+                    cp.wait()
+            multiply(i)
+        for cp in everything:
+            cp.wait_send()
+        yield 0
+
+    scratch = [pltpu.VMEM((4, 2, 2, 4, 16, w), BF) for ws in CHUNKS for w in ws]
+    scratch += [pltpu.VMEM((2, vocab, 4096), BF), pltpu.VMEM((2, 4, vocab, 256), F32)]
     return Task(
         body,
-        [(normed, ANY)],
-        [(jax.ShapeDtypeStruct((4, 2, 2, 4, 16, 4096), BF), ANY)],
-        [],
-        27,
-        1,
-        axis_peers,
+        [(normed, VM), (own_head, ANY), (other_head, ANY)],
+        [(jax.ShapeDtypeStruct((4, 256), F32), VM)],
+        scratch,
+        4 * 3 * 10,
+        2,
+        AXES,
     )
 
 
@@ -384,32 +464,36 @@
     def body(ins, outs, scr):
         best_ref, sq_ref = ins
         out_ref, sum_ref = outs
-        held, came, send, recv, loc = scr
+        held, wide, deep, send, recv, loc = scr
         z, xl, xh, y, c = coords()
         links = Links(send, recv)
         held[0] = sq_ref[...]
         held[0, pl.ds(0, 4), :] = best_ref[...]
         top = lax.broadcasted_iota(jnp.int32, (8, 256), 0) < 4
-        for s, axis in enumerate("xyz"):
-            cps = [links.copy(held.at[s], came.at[s, d - 1], along(axis, d)) for d in (2, 1, 3)]
-            for cp in cps:
-                cp.wait()
-            v = held[s]
-            for d in range(3):
-                w = came[s, d]
-                v = jnp.where(top, jnp.maximum(v, w), v + w)
-            held[s + 1] = v
-        cp = links.copy(held.at[3], came.at[3, 0], place(z, xl, xh, y, 1 - c))
-        cp.wait()
-        v, w = held[3], came[3, 0]
-        out_ref[c] = v
-        out_ref[1 - c] = w
-        sum_ref[...] = v + w
-        yield 0
-
-    def peers():
-        z, xl, xh, y, c = coords()
-        return axis_peers() + [("core", place(z, xl, xh, y, 1 - c))]
+
+        def join(v, w):
+            return jnp.where(top, jnp.maximum(v, w), v + w)
+
+        cps = [links.copy(held.at[0], wide.at[k], shift(*key)) for k, key in enumerate(PLANE)]
+        yield 0
+        for cp in cps:
+            cp.wait()
+        mine = held[0]
+        for k in range(15):
+            mine = join(mine, wide[k])
+        held[1] = mine
+        cps = [links.copy(held.at[1], deep.at[k], shift(*key)) for k, key in enumerate(DEEP)]
+        yield 0
+        for cp in cps:
+            cp.wait()
+        for k in range(3):
+            mine = join(mine, deep[k])
+        theirs = deep[3]
+        for k in range(4, 7):
+            theirs = join(theirs, deep[k])
+        out_ref[c] = mine
+        out_ref[1 - c] = theirs
+        sum_ref[...] = mine + theirs
 
     return Task(
         body,
@@ -418,48 +502,51 @@
             (jax.ShapeDtypeStruct((2, 8, 256), F32), VM),
             (jax.ShapeDtypeStruct((8, 256), F32), VM),
         ],
-        [pltpu.VMEM((4, 8, 256), F32), pltpu.VMEM((4, 3, 8, 256), F32)],
-        10,
+        [
+            pltpu.VMEM((2, 8, 256), F32),
+            pltpu.VMEM((15, 8, 256), F32),
+            pltpu.VMEM((7, 8, 256), F32),
+        ],
+        22,
         1,
-        peers,
+        PLANE + DEEP,
     )
 
 
 def project(x, w_query, w_key, w_value):
     steps = 4
-    depth = x.shape[1] // steps
-    rows = x.shape[0]
+    slots, rows, wide = x.shape
+    per = slots // steps
+    depth = per * wide
 
     def kernel(x_ref, a_ref, b_ref, c_ref, q_ref, k_ref, v_ref, acc):
         i = pl.program_id(0)
-        xs = x_ref[...]
-        for n, w_ref in enumerate((a_ref, b_ref, c_ref)):
+        xs = jnp.concatenate([x_ref[s] for s in range(per)], axis=1)
+        for n, (w_ref, o_ref) in enumerate(((a_ref, q_ref), (b_ref, k_ref), (c_ref, v_ref))):
             part = jnp.dot(xs, w_ref[...], preferred_element_type=F32)
 
             @pl.when(i == 0)
             def _():
                 acc[n] = part
 
-            @pl.when(i > 0)
+            @pl.when((i > 0) & (i < steps - 1))
             def _():
                 acc[n] += part
 
-        @pl.when(i == steps - 1)
-        def _():
-            for n, o_ref in enumerate((q_ref, k_ref, v_ref)):
-                o_ref[...] = acc[n].astype(BF)
-
-    wide = w_query.shape[1]
+            @pl.when(i == steps - 1)
+            def _():
+                o_ref[...] = (acc[n] + part).astype(BF)
+
     weight = pl.BlockSpec((depth, wide), lambda i: (i, 0))
     out = pl.BlockSpec((rows, wide), lambda i: (0, 0))
     return pl.pallas_call(
         kernel,
         grid=(steps,),
-        in_specs=[pl.BlockSpec((rows, depth), lambda i: (0, i)), weight, weight, weight],
+        in_specs=[pl.BlockSpec((per, rows, wide), lambda i: (i, 0, 0)), weight, weight, weight],
         out_specs=[out] * 3,
         out_shape=[jax.ShapeDtypeStruct((rows, wide), BF)] * 3,
         scratch_shapes=[pltpu.VMEM((3, rows, wide), F32)],
-        compiler_params=pltpu.CompilerParams(vmem_limit_bytes=32 << 20),
+        compiler_params=pltpu.CompilerParams(vmem_limit_bytes=24 << 20),
         name="project",
     )(x, w_query, w_key, w_value)
 
@@ -568,39 +655,12 @@
         grid=(steps,),
         in_specs=[whole(a) for a in (parts, stats, q, k, v)]
         + [pl.BlockSpec((256, wide), lambda i: (0, i))],
-        out_specs=pl.BlockSpec((8, 2, 16, wide), lambda i: (0, 0, 0, i)),
-        out_shape=jax.ShapeDtypeStruct((8, 2, 16, w_out.shape[1]), BF),
+        out_specs=pl.BlockSpec((2, 4, 2, 16, wide), lambda i: (0, 0, 0, 0, i)),
+        out_shape=jax.ShapeDtypeStruct((2, 4, 2, 16, w_out.shape[1]), BF),
         scratch_shapes=[pltpu.VMEM((256, 256), BF)],
         compiler_params=pltpu.CompilerParams(vmem_limit_bytes=32 << 20),
         name="combine",
     )(parts, stats, q, k, v, w_out)
-
-
-def best_logits(rows, own_head, other_head):
-    vocab, width = own_head.shape
-
-    def kernel(x_ref, a_ref, b_ref, o_ref):
-        i = pl.program_id(0)
-        x = x_ref[...]
-        top = None
-        for w_ref in (a_ref, b_ref):
-            logits = lax.dot_general(
-                w_ref[...], x, (((1,), (1,)), ((), ())), preferred_element_type=F32
-            )
-            m = jnp.max(logits, axis=0, keepdims=True)
-            top = m if top is None else jnp.maximum(top, m)
-        o_ref[pl.ds(i, 1), :] = top
-
-    head = pl.BlockSpec((vocab, width), lambda i: (0, 0), pipeline_mode=pl.Buffered(1))
-    return pl.pallas_call(
-        kernel,
-        grid=(4,),
-        in_specs=[pl.BlockSpec((256, width), lambda i: (i, 0)), head, head],
-        out_specs=pl.BlockSpec((4, 256), lambda i: (0, 0)),
-        out_shape=jax.ShapeDtypeStruct((4, 256), F32),
-        compiler_params=pltpu.CompilerParams(vmem_limit_bytes=50 << 20),
-        name="logits",
-    )(rows, own_head, other_head)
 
 
 def shards(
@@ -650,17 +710,23 @@
     part2, stat2 = cached_attention(begins, ends, qs2, cache_keys, cache_values)
 
     (normed, squares), (part2, stat2) = comm(
-        [reduce_layer(sum1, feat1, attn_gain, final_gain, True), exchange_tok(part2, stat2)],
+        [
+            reduce_layer(sum1, feat1, attn_gain, final_gain, True, True),
+            exchange_tok(part2, stat2),
+        ],
         3,
         "comm_d",
+        12,
     )
     sum2 = combine(part2, stat2, q2, k2, v2, w_out)
 
-    (rows,), (hiddens,) = comm(
-        [gather_all(normed), reduce_layer(sum2, feat2, attn_gain, None, False)], 4, "comm_e"
-    )
-    best = best_logits(rows.reshape(-1, rows.shape[-1]), lm_head, other_head)
-    ((top, sums),) = comm([reduce_best(best, squares)], 5, "comm_f")
+    ((best,),) = comm([gather_logits(normed, lm_head, other_head)], 4, "comm_e", 48)
+    (top, sums), (hiddens,) = comm(
+        [reduce_best(best, squares), reduce_layer(sum2, feat2, attn_gain, None, False, False)],
+        5,
+        "comm_f",
+        12,
+    )
     top_logits = top[:, :4].reshape(2, 64, 16).transpose(1, 0, 2).reshape(-1)
     request_norms = jnp.sqrt(sums[4, :8] / (256 * 4096))
     return (hiddens, request_norms, top_logits)

time: 263 us -> 232 us (0.88)
  Pallas kernels: 232 us -> 206 us
  local copies, waits for them, and re-layouts: 24.8 us -> 20.7 us
    pallas_call x3 -> x2, Pallas kernels: 29.5 us -> 9.62 us  [project(): pl.pallas_call(kernel, grid=(steps,), in_specs=[pl.BlockSpec((per, rows,...]
    pallas_call x6, Pallas kernels: 175 us -> 168 us  [comm(): pl.pallas_call(kernel, out_shape=[o[0] for t in tasks for o in t.outs], i...]
    unnamed x53 -> x47, local copies, waits for them, and re-layouts: 13.7 us -> 9.56 us
  transfers between devices with their start and end apart: 1 -> 1, of which waited for: 0 -> 0; matrix products, arithmetic and copies ran while one was open for 5% -> 6% of each run, Pallas kernels for 76% -> 58%
where the time goes in v2:
time: 232 us
  Pallas kernels  206 us (89%)
  local copies, waits for them, and re-layouts  20.7 us (9%)
  other arithmetic  3.1 us (1%)
    pallas_call x6, Pallas kernels, comm(): pl.pallas_call(kernel, out_shape=[o[0] for t in tasks for o in t.outs], i...  168 us
    pallas_call x2, Pallas kernels, cached_attention(): pl.pallas_call(kernel, grid_spec=pltpu.PrefetchScalarGridSpec(num_scalar_...  17.8 us
    pallas_call x2, Pallas kernels, combine(): pl.pallas_call(kernel, grid=(steps,), in_specs=[whole(a) for a in (parts,...  10.4 us
    gather x1, local copies, waits for them, and re-layouts, shards(): looked_up = jnp.take(embed, jnp.clip(local_ids, 0, vocab_here - 1), axis=0)  10.3 us
    pallas_call x2, Pallas kernels, project(): pl.pallas_call(kernel, grid=(steps,), in_specs=[pl.BlockSpec((per, rows,...  9.62 us
    unnamed x47, local copies, waits for them, and re-layouts  9.56 us
  transfers between devices with their start and end apart: 1, of which 0 were waited for; matrix products, arithmetic and copies ran while one was open for 6% of the time, Pallas kernels for 58%

profile of v2, /device:TPU:1, one launch (start us, length us, event | category | flops | bytes accessed | tf_op | source)
XLA Modules:
  0.0 232.1 jit_solution(2543866003671069655)
XLA Ops:
  0.6 1.5 collective-permute-start
  2.1 0.7 compare_and_fusion.1
  2.9 0.7 fusion
  3.6 10.3 %gather_fusion = bf16[2048,256]{1,0:T(8,128)(2,1)S(1)} fusion(bf16[12544,256]{1,0:T(8,128)(2,1)} %param.26, s32[2048]{0:T(1024)S(1)} %fusion), kind=kCustom, calls=%fused_computation | custom fusion | bytes 2105344 | tf_op jit(solution)/shard_map/jit(_take)/gather | solution.py:694
  13.9 0.0 copy-start.12
  13.9 0.0 copy-start
  13.9 0.7 select_select_fusion.refs_1_
  14.6 0.2 copy-done.12
  14.8 23.2 %comm_a.1 = (bf16[16,256,256]{2,1,0:T(8,128)(2,1)S(1)}, bf16[8,256,256]{2,1,0:T(8,128)(2,1)S(1)}) custom-call(bf16[256,256]{1,0:T(8,128)(2,1)S(1)} %copy-done.12, bf16[8,256,256]{2,1,0:T(8,128)(2,1)S(1)} %select_select_fusion.refs_1_), custom_call_target="tpu_custom_call" | custom-call | tf_op jit(solution)/shard_map/comm_a/pallas_call | solution.py:116
  38.0 1.4 copy-done.5
  39.4 0.1 reduce_sum.12
  39.6 0.0 copy-done
  39.6 0.0 copy-start.2
  39.6 1.6 copy-done.2
  41.2 1.6 copy-done.3
  42.8 1.6 copy-done.6
  44.4 4.8 %project.2 = (bf16[256,256]{1,0:T(8,128)(2,1)S(1)}, bf16[256,256]{1,0:T(8,128)(2,1)S(1)}, bf16[256,256]{1,0:T(8,128)(2,1)S(1)}) custom-call(bf16[16,256,256]{2,1,0:T(8,128)(2,1)S(1)} %copy-done.6, bf16[4096,256]{1,0:T(8,128)(2,1)S(1)} %copy-done, bf16[4096,256]{1,0:T(8,128)(2,1)S(1)} %copy-done.2, bf16[4096,256]{1,0:T(8,128)(2,1)S(1)} %copy-done.3), custom_call_target="tpu_custom_call" | custom-call | tf_op jit(solution)/shard_map/project/pallas_call | solution.py:542
  49.2 0.0 copy-start.15
  49.2 0.6 copy-done.15
  49.8 0.1 broadcast_select_fusion.refs_1_
  50.0 22.1 %comm_b.1 = (bf16[8,256,256]{2,1,0:T(8,128)(2,1)S(1)}, bf16[16,256,256]{2,1,0:T(8,128)(2,1)S(1)}) custom-call(bf16[256,256]{1,0:T(8,128)(2,1)S(1)} %get-tuple-element.28.refs_0_.q_ref, bf16[256,256]{1,0:T(8,128)(2,1)S(1)} %broadcast_select_fusion.refs_1_), custom_call_target="tpu_custom_call" | custom-call | tf_op jit(solution)/shard_map/comm_b/pallas_call | solution.py:116
  72.1 0.0 copy-start.21
  72.1 0.0 copy-start.8
  72.1 0.0 copy-start.9
  72.1 4.8 %project.3 = (bf16[256,256]{1,0:T(8,128)(2,1)S(1)}, bf16[256,256]{1,0:T(8,128)(2,1)S(1)}, bf16[256,256]{1,0:T(8,128)(2,1)S(1)}) custom-call(bf16[16,256,256]{2,1,0:T(8,128)(2,1)S(1)} %get-tuple-element.33.x_ref.refs_3_, bf16[4096,256]{1,0:T(8,128)(2,1)S(1)} %copy-done.1, bf16[4096,256]{1,0:T(8,128)(2,1)S(1)} %copy-done.2, bf16[4096,256]{1,0:T(8,128)(2,1)S(1)} %copy-done.3), custom_call_target="tpu_custom_call" | custom-call | tf_op jit(solution)/shard_map/project/pallas_call | solution.py:542
  77.0 0.6 copy-done.13
  77.6 0.0 copy-done.21
  77.6 0.2 reduce-window.9
  77.8 0.0 copy-done.9
  77.8 1.2 copy-done.11
  79.1 8.9 %cached.2 = (bf16[8,256,256]{2,1,0:T(8,128)(2,1)S(1)}, f32[8,8,256]{2,1,0:T(8,128)S(1)}) custom-call(s32[8]{0:T(128)S(1)} %get-tuple-element.54.lo_ref, s32[8]{0:T(128)S(1)} %get-tuple-element.53.hi_ref, bf16[8,256,256]{2,1,0:T(8,128)(2,1)S(1)} %copy-done.11, bf16[1024,256]{1,0:T(8,128)(2,1)S(1)} %copy-done.8, bf16[1024,256]{1,0:T(8,128)(2,1)S(1)} %copy-done.9), custom_call_target="tpu_custom_call" | custom-call | tf_op jit(solution)/shard_map/cached/pallas_call | solution.py:601
  88.0 0.0 copy-start.16
  88.0 27.6 %comm_c.1 = (bf16[8,256,256]{2,1,0:T(8,128)(2,1)S(1)}, f32[8,8,256]{2,1,0:T(8,128)S(1)}, bf16[8,256,256]{2,1,0:T(8,128)(2,1)S(1)}) custom-call(bf16[8,256,256]{2,1,0:T(8,128)(2,1)S(1)} %get-tuple-element.31.refs_0_, f32[8,8,256]{2,1,0:T(8,128)S(1)} %get-tuple-element.32.refs_1_, bf16[256,256]{1,0:T(8,128)(2,1)S(1)} %get-tuple-element.34.refs_2_.q_ref), custom_call_target="tpu_custom_call" | custom-call | tf_op jit(solution)/shard_map/comm_c/pallas_call | solution.py:116
  115.6 8.9 %cached.3 = (bf16[8,256,256]{2,1,0:T(8,128)(2,1)S(1)}, f32[8,8,256]{2,1,0:T(8,128)S(1)}) custom-call(s32[8]{0:T(128)S(1)} %get-tuple-element.54.lo_ref, s32[8]{0:T(128)S(1)} %get-tuple-element.53.hi_ref, bf16[8,256,256]{2,1,0:T(8,128)(2,1)S(1)} %get-tuple-element.39.q_ref, bf16[1024,256]{1,0:T(8,128)(2,1)S(1)} %copy-done.8, bf16[1024,256]{1,0:T(8,128)(2,1)S(1)} %copy-done.9), custom_call_target="tpu_custom_call" | custom-call | tf_op jit(solution)/shard_map/cached/pallas_call | solution.py:601
  124.5 0.0 copy-done.18
  124.5 0.0 copy-start.19
  124.5 0.0 copy-start.20
  124.5 5.1 %combine.2.refs_0_ = bf16[2,4,2,16,4096]{4,3,2,1,0:T(8,128)(2,1)S(1)} custom-call(bf16[8,256,256]{2,1,0:T(8,128)(2,1)S(1)} %get-tuple-element.35.p_ref, f32[8,8,256]{2,1,0:T(8,128)S(1)} %get-tuple-element.36.s_ref, bf16[256,256]{1,0:T(8,128)(2,1)S(1)} %get-tuple-element.28.refs_0_.q_ref, bf16[256,256]{1,0:T(8,128)(2,1)S(1)} %copy-done.16, ...), custom_call_target="tpu_custom_call" | custom-call | tf_op jit(solution)/shard_map/combine/pallas_call | solution.py:653
  129.7 24.2 %comm_d.1 = (bf16[16,4096]{1,0:T(8,128)(2,1)S(1)}, f32[8,256]{1,0:T(8,128)S(1)}, bf16[8,256,256]{2,1,0:T(8,128)(2,1)S(1)}, f32[8,8,256]{2,1,0:T(8,128)S(1)}) custom-call(bf16[2,4,2,16,4096]{4,3,2,1,0:T(8,128)(2,1)S(1)} %combine.2.refs_0_, bf16[16,256,256]{2,1,0:T(8,128)(2,1)S(1)} %copy-done.7, f32[1,4096]{1,0:T(1,128)S(1)} %bitcast.15, ...), custom_call_target="tpu_custom_call" | custom-call | tf_op jit(solution)/shard_map/comm_d/pallas_call | solution.py:116
  153.9 5.3 %combine.3.refs_2_ = bf16[2,4,2,16,4096]{4,3,2,1,0:T(8,128)(2,1)S(1)} custom-call(bf16[8,256,256]{2,1,0:T(8,128)(2,1)S(1)} %get-tuple-element.44.p_ref, f32[8,8,256]{2,1,0:T(8,128)S(1)} %get-tuple-element.45.s_ref, bf16[256,256]{1,0:T(8,128)(2,1)S(1)} %get-tuple-element.34.refs_2_.q_ref, bf16[256,256]{1,0:T(8,128)(2,1)S(1)} %get-tuple-element.46.k_ref, ...), custom_call_target="tpu_custom_call" | custom-call | tf_op jit(solution)/shard_map/combine/pallas_call | solution.py:653
  159.2 0.0 collective-permute-done.refs_2_
  159.2 45.4 %comm_e.1.refs_0_ = f32[4,256]{1,0:T(4,128)S(1)} custom-call(bf16[16,4096]{1,0:T(8,128)(2,1)S(1)} %get-tuple-element.42.refs_0_, bf16[784,4096]{1,0:T(8,128)(2,1)} %refs_1_.1, bf16[784,4096]{1,0:T(8,128)(2,1)} %collective-permute-done.refs_2_), custom_call_target="tpu_custom_call" | custom-call | tf_op jit(solution)/shard_map/comm_e/pallas_call | solution.py:116
  204.7 25.4 %comm_f.1 = (f32[2,8,256]{2,1,0:T(8,128)S(1)}, f32[8,256]{1,0:T(8,128)S(1)}, bf16[16,4096]{1,0:T(8,128)(2,1)S(1)}) custom-call(f32[4,256]{1,0:T(4,128)S(1)} %comm_e.1.refs_0_, f32[8,256]{1,0:T(8,128)S(1)} %get-tuple-element.43.refs_1_, bf16[2,4,2,16,4096]{4,3,2,1,0:T(8,128)(2,1)S(1)} %combine.3.refs_2_, ...), custom_call_target="tpu_custom_call" | custom-call | tf_op jit(solution)/shard_map/comm_f/pallas_call | solution.py:116
  230.0 0.5 sqrt_bitcast_fusion
  230.5 0.1 reshape.70
  230.6 0.1 copy.17
  230.7 0.7 reshape.71
  231.4 0.7 copy.19
  (29 shorter events, 0.1 us)
Async XLA Ops:
  0.6 158.6 %collective-permute-start = (bf16[784,4096]{1,0:T(8,128)(2,1)}, bf16[784,4096]{1,0:T(8,128)(2,1)}, u32[]{:S(2)}, u32[]{:S(2)}) collective-permute-start(bf16[784,4096]{1,0:T(8,128)(2,1)} %refs_1_.1), channel_id=1, source_target_pairs={{0,1},{1,0},{2,3},{3,2},{4,5},{5,4},{6,7},{7,6},{8,9},{9,8},{10,11... | collective-permute-start | bytes 19267592 | tf_op jit(solution)/shard_map/ppermute | solution.py:683
  13.9 0.9 copy-start.12
  13.9 25.7 %copy-start = (bf16[4096,256]{1,0:T(8,128)(2,1)S(1)}, bf16[4096,256]{1,0:T(8,128)(2,1)}, u32[]{:S(2)}) copy-start(bf16[4096,256]{1,0:T(8,128)(2,1)} %a_ref.3) | copy-start | bytes 6291460
  38.0 1.4 copy-start.5
  39.6 1.6 copy-start.2
  41.2 1.6 copy-start.3
  42.8 1.6 copy-start.6
  44.4 5.5 %copy-start.22 = (s32[256]{0:T(256)S(1)}, s32[256]{0:T(256)}, u32[]{:S(2)}) copy-start(s32[256]{0:T(256)} %param.16) | copy-start | bytes 3076
  44.4 27.7 %copy-start.1 = (bf16[4096,256]{1,0:T(8,128)(2,1)S(1)}, bf16[4096,256]{1,0:T(8,128)(2,1)}, u32[]{:S(2)}) copy-start(bf16[4096,256]{1,0:T(8,128)(2,1)} %a_ref.3) | copy-start | bytes 6291460
  49.2 0.7 copy-start.15
  49.8 22.2 %copy-start.17 = (bf16[256,256]{1,0:T(8,128)(2,1)}, bf16[256,256]{1,0:T(8,128)(2,1)S(1)}, u32[]{:S(2)}) copy-start(bf16[256,256]{1,0:T(8,128)(2,1)S(1)} %get-tuple-element.38.v_ref) | copy-start | bytes 393220
  72.1 4.9 %copy-start.10 = (bf16[8,256,256]{2,1,0:T(8,128)(2,1)}, bf16[8,256,256]{2,1,0:T(8,128)(2,1)S(1)}, u32[]{:S(2)}) copy-start(bf16[8,256,256]{2,1,0:T(8,128)(2,1)S(1)} %get-tuple-element.30.q_ref) | copy-start | bytes 3145732
  72.1 5.5 %copy-start.21 = (s32[8]{0:T(128)S(1)}, s32[8]{0:T(128)}, u32[]{:S(2)}) copy-start(s32[8]{0:T(128)} %param.17) | copy-start | bytes 100
  72.1 5.7 %copy-start.8 = (bf16[1024,256]{1,0:T(8,128)(2,1)S(1)}, bf16[1024,256]{1,0:T(8,128)(2,1)}, u32[]{:S(2)}) copy-start(bf16[1024,256]{1,0:T(8,128)(2,1)} %k_ref.3) | copy-start | bytes 1572868
  72.1 5.7 %copy-start.9 = (bf16[1024,256]{1,0:T(8,128)(2,1)S(1)}, bf16[1024,256]{1,0:T(8,128)(2,1)}, u32[]{:S(2)}) copy-start(bf16[1024,256]{1,0:T(8,128)(2,1)} %v_ref.3) | copy-start | bytes 1572868
  77.0 0.7 copy-start.13
  77.8 1.2 copy-start.11
  88.0 36.5 %copy-start.4 = (bf16[256,4096]{1,0:T(8,128)(2,1)S(1)}, bf16[256,4096]{1,0:T(8,128)(2,1)}, u32[]{:S(2)}) copy-start(bf16[256,4096]{1,0:T(8,128)(2,1)} %w_ref.3) | copy-start | bytes 6291460
  88.0 36.5 %copy-start.16 = (bf16[256,256]{1,0:T(8,128)(2,1)S(1)}, bf16[256,256]{1,0:T(8,128)(2,1)}, u32[]{:S(2)}) copy-start(bf16[256,256]{1,0:T(8,128)(2,1)} %copy-done.15) | copy-start | bytes 393220
  88.0 36.5 %copy-start.18 = (bf16[256,256]{1,0:T(8,128)(2,1)S(1)}, bf16[256,256]{1,0:T(8,128)(2,1)}, u32[]{:S(2)}) copy-start(bf16[256,256]{1,0:T(8,128)(2,1)} %copy-done.17) | copy-start | bytes 393220
  124.5 5.1 %copy-start.7 = (bf16[16,256,256]{2,1,0:T(8,128)(2,1)S(1)}, bf16[16,256,256]{2,1,0:T(8,128)(2,1)}, u32[]{:S(2)}) copy-start(bf16[16,256,256]{2,1,0:T(8,128)(2,1)} %copy-done.5) | copy-start | bytes 6291460
  124.5 5.1 %copy-start.19 = (f32[4096]{0:T(1024)S(1)}, f32[4096]{0:T(1024)}, u32[]{:S(2)}) copy-start(f32[4096]{0:T(1024)} %param.24) | copy-start | bytes 49156
  124.5 5.1 %copy-start.20 = (f32[4096]{0:T(1024)S(1)}, f32[4096]{0:T(1024)}, u32[]{:S(2)}) copy-start(f32[4096]{0:T(1024)} %param.25) | copy-start | bytes 49156
  129.7 24.3 %copy-start.14 = (bf16[256,256]{1,0:T(8,128)(2,1)S(1)}, bf16[256,256]{1,0:T(8,128)(2,1)}, u32[]{:S(2)}) copy-start(bf16[256,256]{1,0:T(8,128)(2,1)} %copy-done.13) | copy-start | bytes 393220

commit v3 on v2

--- a/solution.py
+++ b/solution.py
@@ -14,7 +14,7 @@
 MESH = pl.DeviceIdType.MESH
 BF = jnp.bfloat16
 F32 = jnp.float32
-ANY = pl.BlockSpec(memory_space=pl.ANY)
+ANY = pl.BlockSpec(memory_space=pltpu.HBM)
 VM = pl.BlockSpec(memory_space=pltpu.VMEM)
 REL8 = ((0, 2), (1, 2), (1, 1), (1, 3), (0, 1), (0, 3), (1, 0))
 
@@ -131,47 +131,88 @@
     return res
 
 
-def gather_features(x):
+def gather_project(x, weights):
+    rows, wide = x.shape
+
     def body(ins, outs, scr):
-        (x_ref,), (f_ref,), (send, recv, loc) = ins, outs, scr
+        x_ref, w_refs = ins[0], ins[1:]
+        own_rows, outs = outs[0], outs[1:]
+        f_ref, w_ref, acc, send, recv, loc = scr
         z, xl, xh, y, c = coords()
         links = Links(send, recv)
 
-        def cols(xh_, y_, c_):
-            return f_ref.at[xh_ * 8 + y_ * 2 + c_]
+        def index(xh_, y_, c_):
+            return xh_ * 8 + y_ * 2 + c_
+
+        def slot(*at):
+            return f_ref.at[index(*at)]
+
+        def absorb(*at):
+            k = index(*at)
+            v = f_ref[k]
+            for n in range(3):
+                w = w_ref[n, pl.ds(pl.multiple_of(k * wide, wide), wide), :]
+                acc[n] += jnp.dot(v, w, preferred_element_type=F32)
 
         core = place(z, xl, xh, y, 1 - c)
-        own = cols(xh, y, c)
+        own = slot(xh, y, c)
         keep = pltpu.make_async_copy(x_ref, own, loc.at[0])
         keep.start()
-        sent, landed = [], []
+        landed = []
         over_x = links.copy(x_ref, own, place(z, xl, 1 - xh, y, c))
         over_y = {d: links.copy(x_ref, own, place(z, xl, xh, ring(y, d), c)) for d in (2, 1, 3)}
         landed.append(links.copy(x_ref, own, core))
+        loads = [pltpu.make_async_copy(w_refs[n], w_ref.at[n], loc.at[1 + n]) for n in range(3)]
+        for cp in loads:
+            cp.start()
+        acc[...] = jnp.zeros_like(acc)
         yield 0
         over_x.wait_recv()
-        far = cols(1 - xh, y, c)
+        far = slot(1 - xh, y, c)
         far_y = {d: links.copy(far, far, place(z, xl, xh, ring(y, d), c)) for d in (2, 1, 3)}
         landed.append(links.copy(far, far, core))
         yield 0
-        for d in (1, 3, 2):
-            over_y[d].wait_recv()
-            got = cols(xh, ring(y, 4 - d), c)
-            landed.append(links.copy(got, got, core))
+        keep.wait()
+        for cp in loads:
+            cp.wait()
+        absorb(xh, y, c)
+        absorb(1 - xh, y, c)
+        for k, xh_ in enumerate((xh, 1 - xh)):
+            landed[k].wait_recv()
+            absorb(xh_, y, 1 - c)
         yield 0
-        for d in (1, 3, 2):
-            far_y[d].wait_recv()
-            got = cols(1 - xh, ring(y, 4 - d), c)
-            landed.append(links.copy(got, got, core))
-        yield 0
-        keep.wait()
-        for cp in [over_x] + list(over_y.values()) + list(far_y.values()):
+        for xh_, arrive in ((xh, over_y), (1 - xh, far_y)):
+            for d in (1, 3, 2):
+                y_ = ring(y, 4 - d)
+                arrive[d].wait_recv()
+                got = slot(xh_, y_, c)
+                landed.append(links.copy(got, got, core))
+                absorb(xh_, y_, c)
+            for k, d in enumerate((1, 3, 2)):
+                landed[k - 3].wait_recv()
+                absorb(xh_, ring(y, 4 - d), 1 - c)
+            yield 0
+        h = pl.multiple_of(index(xh, y, c) * 16, 16)
+        for k in range(16):
+            own_rows[:, k * wide : (k + 1) * wide] = f_ref[k, pl.ds(h, 16), :]
+        for n in range(3):
+            outs[n][...] = acc[n].astype(BF)
+        for cp in [over_x] + list(over_y.values()) + list(far_y.values()) + landed:
             cp.wait_send()
-        for cp in landed:
-            cp.wait()
 
     return Task(
-        body, [(x, ANY)], [(jax.ShapeDtypeStruct((16, 256, 256), BF), ANY)], [], 15, 1, HEAD_AG
+        body,
+        [(x, ANY)] + [(w, ANY) for w in weights],
+        [(jax.ShapeDtypeStruct((16, 16 * wide), BF), VM)]
+        + [(jax.ShapeDtypeStruct((rows, wide), BF), VM)] * 3,
+        [
+            pltpu.VMEM((16, rows, wide), BF),
+            pltpu.VMEM((3, 16 * wide, wide), BF),
+            pltpu.VMEM((3, rows, wide), F32),
+        ],
+        15,
+        4,
+        HEAD_AG,
     )
 
 
@@ -236,29 +277,26 @@
     return v * lax.rsqrt(jnp.mean(v * v, axis=-1, keepdims=True) + EPSILON)
 
 
-def reduce_layer(part, features, attn_gain, final_gain, first, y_first):
+def reduce_layer(part, states_in, attn_gain, final_gain):
+    first = final_gain is not None
+
     def body(ins, outs, scr):
-        part_ref, f_ref, again_ref = ins[:3]
-        mine, theirs, came, far, xrow, send, recv, loc = scr
+        part_ref, x_ref, again_ref = ins[:3]
+        mine, theirs, came, far, send, recv, loc = scr
         z, xl, xh, y, c = coords()
-        h = xh * 8 + y * 2 + c
         links = Links(send, recv)
-        l0 = pltpu.make_async_copy(part_ref.at[:, :, c], mine, loc.at[0])
-        l1 = pltpu.make_async_copy(
-            f_ref.at[:, pl.ds(pl.multiple_of(h * 16, 16), 16), :], xrow, loc.at[1]
-        )
-        swap = links.copy(part_ref.at[:, :, 1 - c], theirs, place(z, xl, xh, y, 1 - c))
-        l0.start()
-        l1.start()
-        yield 0
-        l0.wait()
-        swap.wait_recv()
         cps = []
-
-        def both(xh_, y_):
-            return mine[xh_, y_].astype(F32) + theirs[xh_, y_].astype(F32)
-
-        if y_first:
+        if first:
+            l0 = pltpu.make_async_copy(part_ref.at[:, :, c], mine, loc.at[0])
+            l0.start()
+            swap = links.copy(part_ref.at[:, :, 1 - c], theirs, place(z, xl, xh, y, 1 - c))
+            yield 0
+            l0.wait()
+            swap.wait_recv()
+
+            def both(xh_, y_):
+                return mine[xh_, y_].astype(F32) + theirs[xh_, y_].astype(F32)
+
             for dy in (2, 1, 3):
                 y_ = ring(y, dy)
                 for xh_ in (0, 1):
@@ -279,23 +317,24 @@
             total = total + far[...].astype(F32)
             for cp in cps:
                 cp.wait_send()
+            swap.wait_send()
         else:
+            l0 = pltpu.make_async_copy(part_ref.at[xh, y], far, loc.at[0])
+            l0.start()
             for dx, dy in REL8:
                 xh_, y_ = lax.rem(xh + dx, 2), ring(y, dy)
-                mine[xh_, y_] = both(xh_, y_).astype(BF)
                 cps.append(
-                    links.copy(mine.at[xh_, y_], came.at[xh, y], place(z, xl, xh_, y_, c))
+                    links.copy(part_ref.at[xh_, y_], came.at[xh, y], place(z, xl, xh_, y_, c))
                 )
-            total = both(xh, y)
             yield 0
+            yield 0
+            l0.wait()
+            total = far[...].astype(F32)
             for cp in cps:
                 cp.wait()
             for dx, dy in REL8:
                 total = total + came[lax.rem(xh + dx, 2), ring(y, dy)].astype(F32)
-        swap.wait_send()
-        l1.wait()
-        before = jnp.concatenate([xrow[k] for k in range(16)], axis=1).astype(F32)
-        states = (before + unit_rows(total) * again_ref[...]).astype(BF)
+        states = (x_ref[...].astype(F32) + unit_rows(total) * again_ref[...]).astype(BF)
         if not first:
             outs[0][...] = states
             return
@@ -307,14 +346,14 @@
         row = lax.broadcasted_iota(jnp.int32, (8, 256), 0)
         outs[1][...] = jnp.where((lane == z * 2 + xl) & (row == 4), jnp.sum(squares), 0.0)
 
-    ins = [(part, ANY), (features, ANY), (attn_gain, VM)]
+    ins = [(part, ANY), (states_in, VM), (attn_gain, VM)]
     outs = [(jax.ShapeDtypeStruct((16, 4096), BF), VM)]
     if first:
         ins.append((final_gain, VM))
         outs.append((jax.ShapeDtypeStruct((8, 256), F32), VM))
     block = pltpu.VMEM((2, 4, 16, 4096), BF)
-    scratch = [block, block, block, pltpu.VMEM((16, 4096), BF), pltpu.VMEM((16, 16, 256), BF)]
-    return Task(body, ins, outs, scratch, 8, 2, HEAD_AG if y_first else HEAD_ALL)
+    scratch = [block, block, block, pltpu.VMEM((16, 4096), BF)]
+    return Task(body, ins, outs, scratch, 8, 1, HEAD_AG if first else HEAD_ALL[1:])
 
 
 def along(axis, d):
@@ -325,14 +364,16 @@
 ORDERS = ("xyz", "yzx", "zxy")
 
 
-def gather_logits(normed, own_head, other_head):
+def gather_logits(normed, own_head, other_head, second):
     vocab = own_head.shape[0]
 
     def body(ins, outs, scr):
-        n_ref, own_ref, other_ref = ins
-        (best_ref,) = outs
+        n_ref, own_ref, other_ref = ins[:3]
+        best_ref, sums_ref = outs
         bufs = [scr[3 * i : 3 * i + 3] for i in range(4)]
-        heads, acc, send, recv, loc = scr[12:]
+        heads, acc = scr[12:14]
+        held = scr[14:20]
+        att, out, theirs, sums, send, recv, loc = scr[20:]
         z, xl, xh, y, c = coords()
         x = xh * 2 + xl
         links = Links(send, recv)
@@ -425,11 +466,27 @@
 
             lax.fori_loop(0, 4, step, 0)
 
+        fetch = [
+            pltpu.make_async_copy(src, dst, loc.at[2 + k])
+            for k, (src, dst) in enumerate(zip(ins[3:], held))
+        ]
         one = [spread(i, 0, None) for i in range(4)]
-        for cp in loads:
+        for cp in fetch + loads:
             cp.start()
         two = [spread(i, 1, one[i]) for i in range(4)]
         three = {0: spread(0, 2, two[0]), 1: spread(1, 2, two[1])}
+        for cp in fetch:
+            cp.wait()
+        attend(*held[:5], att)
+
+        def times_out(k, carry):
+            cut = pl.ds(pl.multiple_of(k * 1024, 1024), 1024)
+            o = jnp.dot(att[...], held[5][:, cut], preferred_element_type=F32).astype(BF)
+            out[:, :, :, :, cut] = o.reshape(2, 4, 2, 16, 1024)
+            return carry
+
+        lax.fori_loop(0, 4, times_out, 0)
+        swap = links.copy(out.at[:, :, 1 - c], theirs, shift(0, 0, 0, 1))
         four = {0: relay(0, three[0])}
         for i in range(4):
             if i + 1 < 4:
@@ -443,20 +500,39 @@
                 for cp in loads:
                     cp.wait()
             multiply(i)
+            if i == 0:
+                swap.wait()
+                for xh_ in range(2):
+                    for y_ in range(4):
+                        v = out[xh_, y_, c].astype(F32) + theirs[xh_, y_].astype(F32)
+                        sums[xh_, y_] = v.astype(BF)
+                keep = pltpu.make_async_copy(sums, sums_ref, loc.at[8])
+                keep.start()
+        keep.wait()
         for cp in everything:
             cp.wait_send()
         yield 0
 
     scratch = [pltpu.VMEM((4, 2, 2, 4, 16, w), BF) for ws in CHUNKS for w in ws]
     scratch += [pltpu.VMEM((2, vocab, 4096), BF), pltpu.VMEM((2, 4, vocab, 256), F32)]
+    scratch += [pltpu.VMEM(a.shape, a.dtype) for a in second]
+    scratch += [
+        pltpu.VMEM((256, 256), BF),
+        pltpu.VMEM((2, 4, 2, 16, 4096), BF),
+        pltpu.VMEM((2, 4, 16, 4096), BF),
+        pltpu.VMEM((2, 4, 16, 4096), BF),
+    ]
     return Task(
         body,
-        [(normed, VM), (own_head, ANY), (other_head, ANY)],
-        [(jax.ShapeDtypeStruct((4, 256), F32), VM)],
+        [(normed, VM), (own_head, ANY), (other_head, ANY)] + [(a, ANY) for a in second],
+        [
+            (jax.ShapeDtypeStruct((4, 256), F32), VM),
+            (jax.ShapeDtypeStruct((2, 4, 16, 4096), BF), ANY),
+        ],
         scratch,
-        4 * 3 * 10,
-        2,
-        AXES,
+        4 * 3 * 10 + 1,
+        9,
+        AXES + [(0, 0, 0, 1)],
     )
 
 
@@ -511,44 +587,6 @@
         1,
         PLANE + DEEP,
     )
-
-
-def project(x, w_query, w_key, w_value):
-    steps = 4
-    slots, rows, wide = x.shape
-    per = slots // steps
-    depth = per * wide
-
-    def kernel(x_ref, a_ref, b_ref, c_ref, q_ref, k_ref, v_ref, acc):
-        i = pl.program_id(0)
-        xs = jnp.concatenate([x_ref[s] for s in range(per)], axis=1)
-        for n, (w_ref, o_ref) in enumerate(((a_ref, q_ref), (b_ref, k_ref), (c_ref, v_ref))):
-            part = jnp.dot(xs, w_ref[...], preferred_element_type=F32)
-
-            @pl.when(i == 0)
-            def _():
-                acc[n] = part
-
-            @pl.when((i > 0) & (i < steps - 1))
-            def _():
-                acc[n] += part
-
-            @pl.when(i == steps - 1)
-            def _():
-                o_ref[...] = (acc[n] + part).astype(BF)
-
-    weight = pl.BlockSpec((depth, wide), lambda i: (i, 0))
-    out = pl.BlockSpec((rows, wide), lambda i: (0, 0))
-    return pl.pallas_call(
-        kernel,
-        grid=(steps,),
-        in_specs=[pl.BlockSpec((per, rows, wide), lambda i: (i, 0, 0)), weight, weight, weight],
-        out_specs=[out] * 3,
-        out_shape=[jax.ShapeDtypeStruct((rows, wide), BF)] * 3,
-        scratch_shapes=[pltpu.VMEM((3, rows, wide), F32)],
-        compiler_params=pltpu.CompilerParams(vmem_limit_bytes=24 << 20),
-        name="project",
-    )(x, w_query, w_key, w_value)
 
 
 def scores(q, k):
@@ -620,6 +658,25 @@
     )(begins, ends, queries, keys, values)
 
 
+def attend(p_ref, s_ref, q_ref, k_ref, v_ref, att):
+    st = jnp.concatenate([s_ref[...].reshape(64, 256), jnp.zeros((64, 256), F32)], axis=0)
+    st = jnp.transpose(st)
+    for g in range(2):
+        cut = slice(g * HEAD_DIM, (g + 1) * HEAD_DIM)
+        s = scores(q_ref[:, cut], k_ref[:, cut])
+        top = jnp.max(s, axis=-1, keepdims=True)
+        for i in range(8):
+            top = jnp.maximum(top, st[:, i * 8 + g : i * 8 + g + 1])
+        p = jnp.exp2(s - top)
+        mass = jnp.sum(p, axis=-1, keepdims=True)
+        acc = jnp.dot(p.astype(BF), v_ref[:, cut], preferred_element_type=F32)
+        for i in range(8):
+            f = jnp.exp2(st[:, i * 8 + g : i * 8 + g + 1] - top)
+            mass = mass + f * st[:, i * 8 + g + 2 : i * 8 + g + 3]
+            acc = acc + f * p_ref[i, :, cut].astype(F32)
+        att[:, cut] = (acc / mass).astype(BF)
+
+
 def combine(parts, stats, q, k, v, w_out):
     steps = 4
     wide = w_out.shape[1] // steps
@@ -627,22 +684,7 @@
     def kernel(p_ref, s_ref, q_ref, k_ref, v_ref, w_ref, o_ref, att):
         @pl.when(pl.program_id(0) == 0)
         def _():
-            st = jnp.concatenate([s_ref[...].reshape(64, 256), jnp.zeros((64, 256), F32)], axis=0)
-            st = jnp.transpose(st)
-            for g in range(2):
-                cut = slice(g * HEAD_DIM, (g + 1) * HEAD_DIM)
-                s = scores(q_ref[:, cut], k_ref[:, cut])
-                top = jnp.max(s, axis=-1, keepdims=True)
-                for i in range(8):
-                    top = jnp.maximum(top, st[:, i * 8 + g : i * 8 + g + 1])
-                p = jnp.exp2(s - top)
-                mass = jnp.sum(p, axis=-1, keepdims=True)
-                acc = jnp.dot(p.astype(BF), v_ref[:, cut], preferred_element_type=F32)
-                for i in range(8):
-                    f = jnp.exp2(st[:, i * 8 + g : i * 8 + g + 1] - top)
-                    mass = mass + f * st[:, i * 8 + g + 2 : i * 8 + g + 3]
-                    acc = acc + f * p_ref[i, :, cut].astype(F32)
-                att[:, cut] = (acc / mass).astype(BF)
+            attend(p_ref, s_ref, q_ref, k_ref, v_ref, att)
 
         o = jnp.dot(att[...], w_ref[...], preferred_element_type=F32).astype(BF)
         o_ref[...] = o.reshape(o_ref.shape)
@@ -658,7 +700,7 @@
         out_specs=pl.BlockSpec((2, 4, 2, 16, wide), lambda i: (0, 0, 0, 0, i)),
         out_shape=jax.ShapeDtypeStruct((2, 4, 2, 16, w_out.shape[1]), BF),
         scratch_shapes=[pltpu.VMEM((256, 256), BF)],
-        compiler_params=pltpu.CompilerParams(vmem_limit_bytes=32 << 20),
+        compiler_params=pltpu.CompilerParams(vmem_limit_bytes=16 << 20),
         name="combine",
     )(parts, stats, q, k, v, w_out)
 
@@ -694,35 +736,38 @@
     looked_up = jnp.take(embed, jnp.clip(local_ids, 0, vocab_here - 1), axis=0)
     looked_up = jnp.where(inside[:, None], looked_up, jnp.zeros_like(looked_up))
 
-    (feat1,), (came,) = comm(
-        [gather_features(block_states), exchange_tok(looked_up.reshape(8, 256, 256))], 0, "comm_a"
-    )
-    q1, k1, v1 = project(feat1, w_query, w_key, w_value)
+    weights = (w_query, w_key, w_value)
+    (rows1, q1, k1, v1), (came,) = comm(
+        [
+            gather_project(block_states, weights),
+            exchange_tok(looked_up.reshape(8, 256, 256)),
+        ],
+        0,
+        "comm_a",
+        16,
+    )
     embedded = jnp.sum(came.astype(F32), axis=0).astype(BF)
     swapped = jnp.where((accept == 1)[:, None], embedded, block_states)
 
-    (qs1,), (feat2,) = comm([gather_queries(q1), gather_features(swapped)], 1, "comm_b")
+    (qs1,), (rows2, q2, k2, v2) = comm(
+        [gather_queries(q1), gather_project(swapped, weights)], 1, "comm_b", 16
+    )
     part1, stat1 = cached_attention(begins, ends, qs1, cache_keys, cache_values)
-    q2, k2, v2 = project(feat2, w_query, w_key, w_value)
 
     (part1, stat1), (qs2,) = comm([exchange_tok(part1, stat1), gather_queries(q2)], 2, "comm_c")
     sum1 = combine(part1, stat1, q1, k1, v1, w_out)
     part2, stat2 = cached_attention(begins, ends, qs2, cache_keys, cache_values)
 
     (normed, squares), (part2, stat2) = comm(
-        [
-            reduce_layer(sum1, feat1, attn_gain, final_gain, True, True),
-            exchange_tok(part2, stat2),
-        ],
+        [reduce_layer(sum1, rows1, attn_gain, final_gain), exchange_tok(part2, stat2)],
         3,
         "comm_d",
         12,
     )
-    sum2 = combine(part2, stat2, q2, k2, v2, w_out)
-
-    ((best,),) = comm([gather_logits(normed, lm_head, other_head)], 4, "comm_e", 48)
+    second = (part2, stat2, q2, k2, v2, w_out)
+    ((best, sum2),) = comm([gather_logits(normed, lm_head, other_head, second)], 4, "comm_e", 52)
     (top, sums), (hiddens,) = comm(
-        [reduce_best(best, squares), reduce_layer(sum2, feat2, attn_gain, None, False, False)],
+        [reduce_best(best, squares), reduce_layer(sum2, rows2, attn_gain, None)],
         5,
         "comm_f",
         12,

time: 232 us -> 228 us (0.983)
  Pallas kernels: 206 us -> 199 us
    pallas_call x2 -> x0, Pallas kernels: 9.62 us -> none  [project(): pl.pallas_call(kernel, grid=(steps,), in_specs=[pl.BlockSpec((per, rows,...]
    pallas_call x2 -> x1, Pallas kernels: 10.4 us -> 5.09 us  [combine(): pl.pallas_call(kernel, grid=(steps,), in_specs=[whole(a) for a in (parts,...]
    pallas_call x6, Pallas kernels: 168 us -> 172 us  [comm(): pl.pallas_call(kernel, out_shape=[o[0] for t in tasks for o in t.outs], i...]
    pallas_call x2, Pallas kernels: 17.8 us -> 21.5 us  [cached_attention(): pl.pallas_call(kernel, grid_spec=pltpu.PrefetchScalarGridSpec(num_scalar_...]
    unnamed x47 -> x37, local copies, waits for them, and re-layouts: 9.56 us -> 10.2 us
  transfers between devices with their start and end apart: 1 -> 1, of which waited for: 0 -> 0; matrix products, arithmetic and copies ran while one was open for 6% -> 7% of each run, Pallas kernels for 58% -> 56%
where the time goes in v3:
time: 228 us
  Pallas kernels  199 us (87%)
  local copies, waits for them, and re-layouts  21.4 us (9%)
  other arithmetic  5.32 us (2%)
    pallas_call x6, Pallas kernels, comm(): pl.pallas_call(kernel, out_shape=[o[0] for t in tasks for o in t.outs], i...  172 us
    pallas_call x2, Pallas kernels, cached_attention(): pl.pallas_call(kernel, grid_spec=pltpu.PrefetchScalarGridSpec(num_scalar_...  21.5 us
    gather x1, local copies, waits for them, and re-layouts, shards(): looked_up = jnp.take(embed, jnp.clip(local_ids, 0, vocab_here - 1), axis=0)  10.3 us
    unnamed x37, local copies, waits for them, and re-layouts  10.2 us
    pallas_call x1, Pallas kernels, combine(): pl.pallas_call(kernel, grid=(steps,), in_specs=[whole(a) for a in (parts,...  5.09 us
  transfers between devices with their start and end apart: 1, of which 0 were waited for; matrix products, arithmetic and copies ran while one was open for 7% of the time, Pallas kernels for 56%

profile of v3, /device:TPU:1, one launch (start us, length us, event | category | flops | bytes accessed | tf_op | source)
XLA Modules:
  0.0 227.8 jit_solution(14045171315984260933)
XLA Ops:
  0.6 1.5 collective-permute-start
  2.1 0.7 compare_and_fusion.1
  2.9 0.8 reduce-window.9
  3.7 0.7 fusion
  4.4 10.3 %gather_fusion = bf16[2048,256]{1,0:T(8,128)(2,1)S(1)} fusion(bf16[12544,256]{1,0:T(8,128)(2,1)} %param.26, s32[2048]{0:T(1024)S(1)} %fusion), kind=kCustom, calls=%fused_computation | custom fusion | bytes 2105344 | tf_op jit(solution)/shard_map/jit(_take)/gather | solution.py:736
  14.7 0.0 copy-start
  14.8 0.7 select_select_fusion.refs_4_
  15.5 0.0 copy-done.9
  15.5 0.8 copy-done
  16.3 1.6 copy-done.1
  17.9 1.6 copy-done.3
  19.5 25.2 %comm_a.1 = (bf16[16,4096]{1,0:T(8,128)(2,1)S(1)}, bf16[256,256]{1,0:T(8,128)(2,1)S(1)}, bf16[256,256]{1,0:T(8,128)(2,1)S(1)}, bf16[256,256]{1,0:T(8,128)(2,1)S(1)}, bf16[8,256,256]{2,1,0:T(8,128)(2,1)S(1)}) custom-call(bf16[256,256]{1,0:T(8,128)(2,1)S(1)} %copy-done.9, bf16[4096,256]{1,0:T(8,128)(2,1)S(1)} %copy-done, bf16[4096,256]{1,0:T(8,128)(2,1)S(1)} %copy-done.1, ...), custom_call_target="tpu_custom_call" | custom-call | tf_op jit(solution)/shard_map/comm_a/pallas_call | solution.py:116
  44.7 0.0 copy-start.10
  44.7 0.6 copy-done.10
  45.4 0.6 copy-done.12
  46.0 0.8 reduce_sum.12
  46.8 0.0 copy-done.17
  46.8 1.0 broadcast_select_fusion.refs_1_
  47.8 0.0 copy-start.2
  47.9 1.6 copy-done.2
  49.4 1.6 copy-done.4
  51.0 22.7 %comm_b.1 = (bf16[8,256,256]{2,1,0:T(8,128)(2,1)S(1)}, bf16[16,4096]{1,0:T(8,128)(2,1)S(1)}, bf16[256,256]{1,0:T(8,128)(2,1)S(1)}, bf16[256,256]{1,0:T(8,128)(2,1)S(1)}, bf16[256,256]{1,0:T(8,128)(2,1)S(1)}) custom-call(bf16[256,256]{1,0:T(8,128)(2,1)S(1)} %get-tuple-element.29.refs_0_.q_ref, bf16[256,256]{1,0:T(8,128)(2,1)S(1)} %broadcast_select_fusion.refs_1_, ...), custom_call_target="tpu_custom_call" | custom-call | tf_op jit(solution)/shard_map/comm_b/pallas_call | solution.py:116
  73.7 0.0 copy-done.16
  73.7 0.0 copy-done.6
  73.8 0.0 copy-done.7
  73.8 10.7 %cached.2 = (bf16[8,256,256]{2,1,0:T(8,128)(2,1)S(1)}, f32[8,8,256]{2,1,0:T(8,128)S(1)}) custom-call(s32[8]{0:T(128)S(1)} %get-tuple-element.58.lo_ref, s32[8]{0:T(128)S(1)} %get-tuple-element.57.hi_ref, bf16[8,256,256]{2,1,0:T(8,128)(2,1)S(1)} %get-tuple-element.31.q_ref, bf16[1024,256]{1,0:T(8,128)(2,1)S(1)} %copy-done.6, bf16[1024,256]{1,0:T(8,128)(2,1)S(1)} %copy-done.7), custom_call_target="tpu_custom_call" | custom-call | tf_op jit(solution)/shard_map/cached/pallas_call | solution.py:639
  84.5 0.0 copy-start.11
  84.5 0.0 copy-start.13
  84.5 27.6 %comm_c.1 = (bf16[8,256,256]{2,1,0:T(8,128)(2,1)S(1)}, f32[8,8,256]{2,1,0:T(8,128)S(1)}, bf16[8,256,256]{2,1,0:T(8,128)(2,1)S(1)}) custom-call(bf16[8,256,256]{2,1,0:T(8,128)(2,1)S(1)} %get-tuple-element.32.refs_0_, f32[8,8,256]{2,1,0:T(8,128)S(1)} %get-tuple-element.33.refs_1_, bf16[256,256]{1,0:T(8,128)(2,1)S(1)} %get-tuple-element.34.refs_2_.refs_5_), custom_call_target="tpu_custom_call" | custom-call | tf_op jit(solution)/shard_map/comm_c/pallas_call | solution.py:116
  112.1 10.8 %cached.3 = (bf16[8,256,256]{2,1,0:T(8,128)(2,1)S(1)}, f32[8,8,256]{2,1,0:T(8,128)S(1)}) custom-call(s32[8]{0:T(128)S(1)} %get-tuple-element.58.lo_ref, s32[8]{0:T(128)S(1)} %get-tuple-element.57.hi_ref, bf16[8,256,256]{2,1,0:T(8,128)(2,1)S(1)} %get-tuple-element.40.q_ref, bf16[1024,256]{1,0:T(8,128)(2,1)S(1)} %copy-done.6, bf16[1024,256]{1,0:T(8,128)(2,1)S(1)} %copy-done.7), custom_call_target="tpu_custom_call" | custom-call | tf_op jit(solution)/shard_map/cached/pallas_call | solution.py:639
  122.8 0.0 copy-done.5
  122.9 0.0 copy-done.11
  122.9 0.0 copy-done.13
  122.9 0.0 copy-start.14
  122.9 0.0 copy-start.15
  122.9 5.1 %combine.1.refs_0_ = bf16[2,4,2,16,4096]{4,3,2,1,0:T(8,128)(2,1)S(1)} custom-call(bf16[8,256,256]{2,1,0:T(8,128)(2,1)S(1)} %get-tuple-element.35.p_ref, f32[8,8,256]{2,1,0:T(8,128)S(1)} %get-tuple-element.36.s_ref, bf16[256,256]{1,0:T(8,128)(2,1)S(1)} %get-tuple-element.29.refs_0_.q_ref, bf16[256,256]{1,0:T(8,128)(2,1)S(1)} %copy-done.11, ...), custom_call_target="tpu_custom_call" | custom-call | tf_op jit(solution)/shard_map/combine/pallas_call | solution.py:695
  128.0 0.0 copy-done.14
  128.0 0.0 copy-done.15
  128.0 24.4 %comm_d.1 = (bf16[16,4096]{1,0:T(8,128)(2,1)S(1)}, f32[8,256]{1,0:T(8,128)S(1)}, bf16[8,256,256]{2,1,0:T(8,128)(2,1)S(1)}, f32[8,8,256]{2,1,0:T(8,128)S(1)}) custom-call(bf16[2,4,2,16,4096]{4,3,2,1,0:T(8,128)(2,1)S(1)} %combine.1.refs_0_, bf16[16,4096]{1,0:T(8,128)(2,1)S(1)} %get-tuple-element.39.refs_1_, f32[1,4096]{1,0:T(1,128)S(1)} %bitcast.15, ...), custom_call_target="tpu_custom_call" | custom-call | tf_op jit(solution)/shard_map/comm_d/pallas_call | solution.py:116
  152.5 1.0 copy-done.8
  153.4 0.0 collective-permute-done.refs_2_
  153.4 45.5 %comm_e.1 = (f32[4,256]{1,0:T(4,128)S(1)}, bf16[2,4,16,4096]{3,2,1,0:T(8,128)(2,1)S(1)}) custom-call(bf16[16,4096]{1,0:T(8,128)(2,1)S(1)} %get-tuple-element.43.refs_0_, bf16[784,4096]{1,0:T(8,128)(2,1)} %refs_1_.3, bf16[784,4096]{1,0:T(8,128)(2,1)} %collective-permute-done.refs_2_, bf16[8,256,256]{2,1,0:T(8,128)(2,1)} %copy-done.8, ...), custom_call_target="tpu_custom_call" | custom-call | tf_op jit(solution)/shard_map/comm_e/pallas_call | solution.py:116
  198.9 26.9 %comm_f.1 = (f32[2,8,256]{2,1,0:T(8,128)S(1)}, f32[8,256]{1,0:T(8,128)S(1)}, bf16[16,4096]{1,0:T(8,128)(2,1)S(1)}) custom-call(f32[4,256]{1,0:T(4,128)S(1)} %get-tuple-element.48.refs_0_, f32[8,256]{1,0:T(8,128)S(1)} %get-tuple-element.49.refs_1_, bf16[2,4,16,4096]{3,2,1,0:T(8,128)(2,1)S(1)} %get-tuple-element.50.refs_2_, ...), custom_call_target="tpu_custom_call" | custom-call | tf_op jit(solution)/shard_map/comm_f/pallas_call | solution.py:116
  225.8 0.5 sqrt_bitcast_fusion
  226.3 0.1 reshape.70
  226.4 0.1 copy.17
  226.5 0.7 reshape.71
  227.2 0.7 copy.19
  (16 shorter events, 0.1 us)
Async XLA Ops:
  0.6 152.8 %collective-permute-start = (bf16[784,4096]{1,0:T(8,128)(2,1)}, bf16[784,4096]{1,0:T(8,128)(2,1)}, u32[]{:S(2)}, u32[]{:S(2)}) collective-permute-start(bf16[784,4096]{1,0:T(8,128)(2,1)} %refs_1_.3), channel_id=1, source_target_pairs={{0,1},{1,0},{2,3},{3,2},{4,5},{5,4},{6,7},{7,6},{8,9},{9,8},{10,11... | collective-permute-start | bytes 19267592 | tf_op jit(solution)/shard_map/ppermute | solution.py:725
  4.4 11.1 %copy-start.9 = (bf16[256,256]{1,0:T(8,128)(2,1)S(1)}, bf16[256,256]{1,0:T(8,128)(2,1)}, u32[]{:S(2)}) copy-start(bf16[256,256]{1,0:T(8,128)(2,1)} %refs_0_.1) | copy-start | bytes 393220
  14.7 1.6 copy-start
  16.3 1.6 copy-start.1
  17.9 1.6 copy-start.3
  19.5 27.3 %copy-start.17 = (s32[256]{0:T(256)S(1)}, s32[256]{0:T(256)}, u32[]{:S(2)}) copy-start(s32[256]{0:T(256)} %param.16) | copy-start | bytes 3076
  44.7 0.6 copy-start.10
  45.4 0.7 copy-start.12
  47.8 1.6 copy-start.2
  49.4 1.6 copy-start.4
  51.0 22.7 %copy-start.16 = (s32[8]{0:T(128)S(1)}, s32[8]{0:T(128)}, u32[]{:S(2)}) copy-start(s32[8]{0:T(128)} %param.17) | copy-start | bytes 100
  51.0 22.7 %copy-start.6 = (bf16[1024,256]{1,0:T(8,128)(2,1)S(1)}, bf16[1024,256]{1,0:T(8,128)(2,1)}, u32[]{:S(2)}) copy-start(bf16[1024,256]{1,0:T(8,128)(2,1)} %k_ref.3) | copy-start | bytes 1572868
  51.0 22.7 %copy-start.7 = (bf16[1024,256]{1,0:T(8,128)(2,1)S(1)}, bf16[1024,256]{1,0:T(8,128)(2,1)}, u32[]{:S(2)}) copy-start(bf16[1024,256]{1,0:T(8,128)(2,1)} %v_ref.3) | copy-start | bytes 1572868
  84.5 38.3 %copy-start.5 = (bf16[256,4096]{1,0:T(8,128)(2,1)S(1)}, bf16[256,4096]{1,0:T(8,128)(2,1)}, u32[]{:S(2)}) copy-start(bf16[256,4096]{1,0:T(8,128)(2,1)} %refs_8_.1) | copy-start | bytes 6291460
  84.5 38.3 %copy-start.11 = (bf16[256,256]{1,0:T(8,128)(2,1)S(1)}, bf16[256,256]{1,0:T(8,128)(2,1)}, u32[]{:S(2)}) copy-start(bf16[256,256]{1,0:T(8,128)(2,1)} %copy-done.10) | copy-start | bytes 393220
  84.5 38.3 %copy-start.13 = (bf16[256,256]{1,0:T(8,128)(2,1)S(1)}, bf16[256,256]{1,0:T(8,128)(2,1)}, u32[]{:S(2)}) copy-start(bf16[256,256]{1,0:T(8,128)(2,1)} %copy-done.12) | copy-start | bytes 393220
  122.9 5.1 %copy-start.14 = (f32[4096]{0:T(1024)S(1)}, f32[4096]{0:T(1024)}, u32[]{:S(2)}) copy-start(f32[4096]{0:T(1024)} %param.24) | copy-start | bytes 49156
  122.9 5.1 %copy-start.15 = (f32[4096]{0:T(1024)S(1)}, f32[4096]{0:T(1024)}, u32[]{:S(2)}) copy-start(f32[4096]{0:T(1024)} %param.25) | copy-start | bytes 49156
  152.5 1.0 copy-start.8

commit v4 on v3

--- a/solution.py
+++ b/solution.py
@@ -224,20 +224,27 @@
         own = o_ref.at[z * 2 + xl]
         keep = pltpu.make_async_copy(q_ref, own, loc.at[0])
         keep.start()
-        over_x = links.copy(q_ref, own, place(z, 1 - xl, xh, y, c))
-        over_z = [links.copy(q_ref, own, place(ring(z, d), xl, xh, y, c)) for d in (2, 1, 3)]
-        yield 0
-        over_x.wait_recv()
-        far = o_ref.at[z * 2 + 1 - xl]
-        over_z += [links.copy(far, far, place(ring(z, d), xl, xh, y, c)) for d in (2, 1, 3)]
-        yield 0
-        over_x.wait_send()
-        for cp in over_z:
-            cp.wait()
+        side = place(z, 1 - xl, xh, y, c)
+        over_x = [links.copy(q_ref, own, side)]
+        over_z = {d: links.copy(q_ref, own, place(ring(z, d), xl, xh, y, c)) for d in (2, 1, 3)}
+        yield 0
+        over_x[0].wait_recv()
+        far = o_ref.at[z * 2 + 1 - xl, pl.ds(0, 128)]
+        more = [links.copy(far, far, place(ring(z, d), xl, xh, y, c)) for d in (2, 1, 3)]
+        yield 0
+        for d in (1, 3, 2):
+            over_z[d].wait_recv()
+            got = o_ref.at[ring(z, 4 - d) * 2 + xl, pl.ds(128, 128)]
+            over_x.append(links.copy(got, got, side))
+        yield 0
+        for cp in over_x[1:] + more:
+            cp.wait_recv()
+        for cp in over_x + more + list(over_z.values()):
+            cp.wait_send()
         keep.wait()
 
     return Task(
-        body, [(q, ANY)], [(jax.ShapeDtypeStruct((8, 256, 256), BF), ANY)], [], 7, 1, TOK_AG
+        body, [(q, ANY)], [(jax.ShapeDtypeStruct((8, 256, 256), BF), ANY)], [], 10, 1, TOK_AG
     )
 
 
@@ -277,103 +284,86 @@
     return v * lax.rsqrt(jnp.mean(v * v, axis=-1, keepdims=True) + EPSILON)
 
 
+def layer_end(before, total, gain):
+    return (before.astype(F32) + unit_rows(total) * gain).astype(BF)
+
+
 def reduce_layer(part, states_in, attn_gain, final_gain):
-    first = final_gain is not None
-
     def body(ins, outs, scr):
-        part_ref, x_ref, again_ref = ins[:3]
+        part_ref, x_ref, again_ref, fgain_ref = ins
         mine, theirs, came, far, send, recv, loc = scr
         z, xl, xh, y, c = coords()
         links = Links(send, recv)
         cps = []
-        if first:
-            l0 = pltpu.make_async_copy(part_ref.at[:, :, c], mine, loc.at[0])
-            l0.start()
-            swap = links.copy(part_ref.at[:, :, 1 - c], theirs, place(z, xl, xh, y, 1 - c))
-            yield 0
-            l0.wait()
-            swap.wait_recv()
-
-            def both(xh_, y_):
-                return mine[xh_, y_].astype(F32) + theirs[xh_, y_].astype(F32)
-
-            for dy in (2, 1, 3):
-                y_ = ring(y, dy)
-                for xh_ in (0, 1):
-                    mine[xh_, y_] = both(xh_, y_).astype(BF)
-                cps.append(links.copy(mine.at[:, y_], came.at[:, y], place(z, xl, xh, y_, c)))
-            total, away = both(xh, y), both(1 - xh, y)
-            yield 0
-            for cp in cps:
-                cp.wait_recv()
-            for dy in (1, 3, 2):
-                y_ = ring(y, dy)
-                away = away + came[1 - xh, y_].astype(F32)
-                total = total + came[xh, y_].astype(F32)
-            mine[1 - xh, y] = away.astype(BF)
-            over = links.copy(mine.at[1 - xh, y], far, place(z, xl, 1 - xh, y, c))
-            yield 0
-            over.wait()
-            total = total + far[...].astype(F32)
-            for cp in cps:
-                cp.wait_send()
-            swap.wait_send()
-        else:
-            l0 = pltpu.make_async_copy(part_ref.at[xh, y], far, loc.at[0])
-            l0.start()
-            for dx, dy in REL8:
-                xh_, y_ = lax.rem(xh + dx, 2), ring(y, dy)
-                cps.append(
-                    links.copy(part_ref.at[xh_, y_], came.at[xh, y], place(z, xl, xh_, y_, c))
-                )
-            yield 0
-            yield 0
-            l0.wait()
-            total = far[...].astype(F32)
-            for cp in cps:
-                cp.wait()
-            for dx, dy in REL8:
-                total = total + came[lax.rem(xh + dx, 2), ring(y, dy)].astype(F32)
-        states = (x_ref[...].astype(F32) + unit_rows(total) * again_ref[...]).astype(BF)
-        if not first:
-            outs[0][...] = states
-            return
-        wide = states.astype(F32)
+        l0 = pltpu.make_async_copy(part_ref.at[:, :, c], mine, loc.at[0])
+        l0.start()
+        swap = links.copy(part_ref.at[:, :, 1 - c], theirs, place(z, xl, xh, y, 1 - c))
+        yield 0
+        l0.wait()
+        swap.wait_recv()
+
+        def both(xh_, y_):
+            return mine[xh_, y_].astype(F32) + theirs[xh_, y_].astype(F32)
+
+        for dy in (2, 1, 3):
+            y_ = ring(y, dy)
+            for xh_ in (0, 1):
+                mine[xh_, y_] = both(xh_, y_).astype(BF)
+            cps.append(links.copy(mine.at[:, y_], came.at[:, y], place(z, xl, xh, y_, c)))
+        total, away = both(xh, y), both(1 - xh, y)
+        yield 0
+        for cp in cps:
+            cp.wait_recv()
+        for dy in (1, 3, 2):
+            y_ = ring(y, dy)
+            away = away + came[1 - xh, y_].astype(F32)
+            total = total + came[xh, y_].astype(F32)
+        mine[1 - xh, y] = away.astype(BF)
+        over = links.copy(mine.at[1 - xh, y], far, place(z, xl, 1 - xh, y, c))
+        yield 0
+        over.wait()
+        total = total + far[...].astype(F32)
+        for cp in cps:
+            cp.wait_send()
+        swap.wait_send()
+        wide = layer_end(x_ref[...], total, again_ref[...]).astype(F32)
         squares = jnp.sum(wide * wide, axis=-1, keepdims=True)
-        normed = wide * lax.rsqrt(squares * (1.0 / 4096) + EPSILON) * ins[3][...]
+        normed = wide * lax.rsqrt(squares * (1.0 / 4096) + EPSILON) * fgain_ref[...]
         outs[0][...] = normed.astype(BF)
         lane = lax.broadcasted_iota(jnp.int32, (8, 256), 1)
         row = lax.broadcasted_iota(jnp.int32, (8, 256), 0)
         outs[1][...] = jnp.where((lane == z * 2 + xl) & (row == 4), jnp.sum(squares), 0.0)
 
-    ins = [(part, ANY), (states_in, VM), (attn_gain, VM)]
-    outs = [(jax.ShapeDtypeStruct((16, 4096), BF), VM)]
-    if first:
-        ins.append((final_gain, VM))
-        outs.append((jax.ShapeDtypeStruct((8, 256), F32), VM))
     block = pltpu.VMEM((2, 4, 16, 4096), BF)
-    scratch = [block, block, block, pltpu.VMEM((16, 4096), BF)]
-    return Task(body, ins, outs, scratch, 8, 1, HEAD_AG if first else HEAD_ALL[1:])
+    return Task(
+        body,
+        [(part, ANY), (states_in, VM), (attn_gain, VM), (final_gain, VM)],
+        [(jax.ShapeDtypeStruct((16, 4096), BF), VM), (jax.ShapeDtypeStruct((8, 256), F32), VM)],
+        [block, block, block, pltpu.VMEM((16, 4096), BF)],
+        8,
+        1,
+        HEAD_AG,
+    )
 
 
 def along(axis, d):
     return shift(*{"x": (d, 0, 0, 0), "y": (0, d, 0, 0), "z": (0, 0, d, 0)}[axis])
 
 
-CHUNKS = ((384, 384, 256), (384, 256, 384), (256, 384, 384), (384, 384, 256))
+CHUNKS = ((384, 384, 256), (384, 384, 256), (384, 384, 256), (512, 384, 128))
 ORDERS = ("xyz", "yzx", "zxy")
 
 
-def gather_logits(normed, own_head, other_head, second):
+def gather_logits(normed, squares, own_head, other_head, second, states_in, attn_gain):
     vocab = own_head.shape[0]
 
     def body(ins, outs, scr):
-        n_ref, own_ref, other_ref = ins[:3]
-        best_ref, sums_ref = outs
+        n_ref, sq_ref, x_ref, again_ref, own_ref, other_ref = ins[:6]
+        top_ref, sum_ref, hid_ref = outs
         bufs = [scr[3 * i : 3 * i + 3] for i in range(4)]
         heads, acc = scr[12:14]
         held = scr[14:20]
-        att, out, theirs, sums, send, recv, loc = scr[20:]
+        att, out, theirs, came, far, maxima, wide, deep, send, recv, loc = scr[20:]
         z, xl, xh, y, c = coords()
         x = xh * 2 + xl
         links = Links(send, recv)
@@ -461,14 +451,14 @@
                         m = jnp.max(part, axis=0, keepdims=True)
                         top = m if top is None else jnp.maximum(top, m)
                 if i == 3:
-                    best_ref[pl.ds(r, 1), :] = top
+                    maxima[0, pl.ds(r, 1), :] = top
                 return carry
 
             lax.fori_loop(0, 4, step, 0)
 
         fetch = [
             pltpu.make_async_copy(src, dst, loc.at[2 + k])
-            for k, (src, dst) in enumerate(zip(ins[3:], held))
+            for k, (src, dst) in enumerate(zip(ins[6:], held))
         ]
         one = [spread(i, 0, None) for i in range(4)]
         for cp in fetch + loads:
@@ -487,6 +477,7 @@
 
         lax.fori_loop(0, 4, times_out, 0)
         swap = links.copy(out.at[:, :, 1 - c], theirs, shift(0, 0, 0, 1))
+        over_y = []
         four = {0: relay(0, three[0])}
         for i in range(4):
             if i + 1 < 4:
@@ -499,16 +490,60 @@
             if i == 0:
                 for cp in loads:
                     cp.wait()
+            if i == 3:
+                maxima[0] = sq_ref[...]
             multiply(i)
             if i == 0:
                 swap.wait()
-                for xh_ in range(2):
-                    for y_ in range(4):
+                for dy in (2, 1, 3, 0):
+                    y_ = ring(y, dy)
+                    for xh_ in (0, 1):
                         v = out[xh_, y_, c].astype(F32) + theirs[xh_, y_].astype(F32)
-                        sums[xh_, y_] = v.astype(BF)
-                keep = pltpu.make_async_copy(sums, sums_ref, loc.at[8])
-                keep.start()
-        keep.wait()
+                        theirs[xh_, y_] = v.astype(BF)
+                    if dy:
+                        over_y.append(
+                            links.copy(
+                                theirs.at[:, y_], came.at[:, y], place(z, xl, xh, y_, c)
+                            )
+                        )
+            if i == 2:
+                for cp in over_y:
+                    cp.wait_recv()
+                for xh_ in (0, 1):
+                    v = theirs[xh_, y].astype(F32)
+                    for dy in (1, 3, 2):
+                        v = v + came[xh_, ring(y, dy)].astype(F32)
+                    theirs[xh_, y] = v.astype(BF)
+                over_x = links.copy(
+                    theirs.at[1 - xh, y], far, place(z, xl, 1 - xh, y, c)
+                )
+        top = lax.broadcasted_iota(jnp.int32, (8, 256), 0) < 4
+
+        def join(v, w):
+            return jnp.where(top, jnp.maximum(v, w), v + w)
+
+        cps = [links.copy(maxima.at[0], wide.at[k], shift(*key)) for k, key in enumerate(PLANE)]
+        over_x.wait_recv()
+        total = theirs[xh, y].astype(F32) + far[...].astype(F32)
+        hid_ref[...] = layer_end(x_ref[...], total, again_ref[...])
+        everything += over_y + [over_x]
+        for cp in cps:
+            cp.wait()
+        mine = maxima[0]
+        for k in range(15):
+            mine = join(mine, wide[k])
+        maxima[1] = mine
+        cps = [links.copy(maxima.at[1], deep.at[k], shift(*key)) for k, key in enumerate(DEEP)]
+        for cp in cps:
+            cp.wait()
+        for k in range(3):
+            mine = join(mine, deep[k])
+        other = deep[3]
+        for k in range(4, 7):
+            other = join(other, deep[k])
+        top_ref[c] = mine
+        top_ref[1 - c] = other
+        sum_ref[...] = mine + other
         for cp in everything:
             cp.wait_send()
         yield 0
@@ -521,71 +556,24 @@
         pltpu.VMEM((2, 4, 2, 16, 4096), BF),
         pltpu.VMEM((2, 4, 16, 4096), BF),
         pltpu.VMEM((2, 4, 16, 4096), BF),
+        pltpu.VMEM((16, 4096), BF),
+        pltpu.VMEM((2, 8, 256), F32),
+        pltpu.VMEM((15, 8, 256), F32),
+        pltpu.VMEM((7, 8, 256), F32),
     ]
     return Task(
         body,
-        [(normed, VM), (own_head, ANY), (other_head, ANY)] + [(a, ANY) for a in second],
-        [
-            (jax.ShapeDtypeStruct((4, 256), F32), VM),
-            (jax.ShapeDtypeStruct((2, 4, 16, 4096), BF), ANY),
-        ],
-        scratch,
-        4 * 3 * 10 + 1,
-        9,
-        AXES + [(0, 0, 0, 1)],
-    )
-
-
-def reduce_best(best, squares):
-    def body(ins, outs, scr):
-        best_ref, sq_ref = ins
-        out_ref, sum_ref = outs
-        held, wide, deep, send, recv, loc = scr
-        z, xl, xh, y, c = coords()
-        links = Links(send, recv)
-        held[0] = sq_ref[...]
-        held[0, pl.ds(0, 4), :] = best_ref[...]
-        top = lax.broadcasted_iota(jnp.int32, (8, 256), 0) < 4
-
-        def join(v, w):
-            return jnp.where(top, jnp.maximum(v, w), v + w)
-
-        cps = [links.copy(held.at[0], wide.at[k], shift(*key)) for k, key in enumerate(PLANE)]
-        yield 0
-        for cp in cps:
-            cp.wait()
-        mine = held[0]
-        for k in range(15):
-            mine = join(mine, wide[k])
-        held[1] = mine
-        cps = [links.copy(held.at[1], deep.at[k], shift(*key)) for k, key in enumerate(DEEP)]
-        yield 0
-        for cp in cps:
-            cp.wait()
-        for k in range(3):
-            mine = join(mine, deep[k])
-        theirs = deep[3]
-        for k in range(4, 7):
-            theirs = join(theirs, deep[k])
-        out_ref[c] = mine
-        out_ref[1 - c] = theirs
-        sum_ref[...] = mine + theirs
-
-    return Task(
-        body,
-        [(best, VM), (squares, VM)],
+        [(normed, VM), (squares, VM), (states_in, VM), (attn_gain, VM)]
+        + [(a, ANY) for a in (own_head, other_head) + second],
         [
             (jax.ShapeDtypeStruct((2, 8, 256), F32), VM),
             (jax.ShapeDtypeStruct((8, 256), F32), VM),
+            (jax.ShapeDtypeStruct((16, 4096), BF), VM),
         ],
-        [
-            pltpu.VMEM((2, 8, 256), F32),
-            pltpu.VMEM((15, 8, 256), F32),
-            pltpu.VMEM((7, 8, 256), F32),
-        ],
-        22,
-        1,
-        PLANE + DEEP,
+        scratch,
+        4 * 3 * 10 + 5 + 22,
+        8,
+        AXES + PLANE + DEEP,
     )
 
 
@@ -597,63 +585,70 @@
     rows = queries.shape[1]
     span = 256
 
-    def kernel(lo_ref, hi_ref, q_ref, k_ref, v_ref, o_ref, s_ref, m_sc, l_sc, a_sc):
-        r = pl.program_id(0)
-        lo, hi = lo_ref[r], hi_ref[r]
-        m_sc[...] = jnp.full_like(m_sc, NEG)
-        l_sc[...] = jnp.zeros_like(l_sc)
-        a_sc[...] = jnp.zeros_like(a_sc)
-
-        @pl.when(hi > lo)
-        def _():
-            def step(b, carry):
-                at = pl.multiple_of(b * span, span)
-                pos = at + lax.broadcasted_iota(jnp.int32, (rows, span), 1)
-                valid = (pos >= lo) & (pos < hi)
+    def kernel(lo_ref, hi_ref, q_ref, k_ref, v_ref, o_ref, s_ref, v_sc, m_sc, a_sc):
+        for g in range(2):
+            v_sc[g, :, :HEAD_DIM] = v_ref[:, g * HEAD_DIM : (g + 1) * HEAD_DIM]
+            v_sc[g, :, HEAD_DIM:] = jnp.ones((v_ref.shape[0], HEAD_DIM), BF)
+        lane = lax.broadcasted_iota(jnp.int32, (rows, 128), 1)
+        sub = lax.broadcasted_iota(jnp.int32, (8, rows), 0)
+
+        def request(r, carry):
+            lo, hi = lo_ref[r], hi_ref[r]
+
+            @pl.when(hi <= lo)
+            def _():
+                o_ref[r] = jnp.zeros(o_ref.shape[1:], BF)
+                s_ref[r] = jnp.where(sub < 2, NEG, 0.0)
+
+            @pl.when(hi > lo)
+            def _():
+                m_sc[...] = jnp.full_like(m_sc, NEG)
+                a_sc[...] = jnp.zeros_like(a_sc)
+
+                def step(b, carry):
+                    at = pl.multiple_of(b * span, span)
+                    pos = at + lax.broadcasted_iota(jnp.int32, (1, span), 1)
+                    bias = jnp.where((pos >= lo) & (pos < hi), 0.0, NEG)
+                    for g in range(2):
+                        cut = slice(g * HEAD_DIM, (g + 1) * HEAD_DIM)
+                        s = scores(q_ref[r, :, cut], k_ref[pl.ds(at, span), cut]) + bias
+                        old = m_sc[g]
+                        new = jnp.maximum(old, jnp.max(s, axis=-1, keepdims=True))
+                        p = jnp.exp2(s - new[:, 0:1]).astype(BF)
+                        f = jnp.exp2(old - new)
+                        a_sc[g] = a_sc[g] * jnp.concatenate([f, f], axis=1) + jnp.dot(
+                            p, v_sc[g, pl.ds(at, span), :], preferred_element_type=F32
+                        )
+                        m_sc[g] = new
+                    return carry
+
+                lax.fori_loop(lo // span, (hi + span - 1) // span, step, 0)
+                stats = jnp.where(lane == 0, m_sc[0], m_sc[1])
+                stats = jnp.where(lane == 2, a_sc[0, :, HEAD_DIM:], stats)
+                stats = jnp.where(lane == 3, a_sc[1, :, HEAD_DIM:], stats)
+                s_ref[r] = jnp.transpose(stats)[:8]
                 for g in range(2):
-                    cut = slice(g * HEAD_DIM, (g + 1) * HEAD_DIM)
-                    s = scores(q_ref[0, :, cut], k_ref[pl.ds(at, span), cut])
-                    s = jnp.where(valid, s, NEG)
-                    old = m_sc[g, :, 0:1]
-                    new = jnp.maximum(old, jnp.max(s, axis=-1, keepdims=True))
-                    p = jnp.where(valid, jnp.exp2(s - new), 0.0)
-                    f = jnp.exp2(old - new)
-                    l_sc[g] = l_sc[g] * f + jnp.sum(p, axis=-1, keepdims=True)
-                    a_sc[g] = a_sc[g] * f + jnp.dot(
-                        p.astype(BF), v_ref[pl.ds(at, span), cut], preferred_element_type=F32
-                    )
-                    m_sc[g] = jnp.broadcast_to(new, m_sc.shape[1:])
-                return carry
-
-            lax.fori_loop(lo // span, (hi + span - 1) // span, step, 0)
-
-        lane = lax.broadcasted_iota(jnp.int32, (rows, 128), 1)
-        stats = jnp.where(lane == 0, m_sc[0], jnp.where(lane == 1, m_sc[1], 0.0))
-        stats = jnp.where(lane == 2, l_sc[0], jnp.where(lane == 3, l_sc[1], stats))
-        s_ref[0] = jnp.transpose(stats)[:8]
-        for g in range(2):
-            o_ref[0, :, g * HEAD_DIM : (g + 1) * HEAD_DIM] = a_sc[g].astype(BF)
-
-    whole = pl.BlockSpec(keys.shape, lambda r, a, b: (0, 0))
-    per = pl.BlockSpec((1, rows, 256), lambda r, a, b: (r, 0, 0))
+                    o_ref[r, :, g * HEAD_DIM : (g + 1) * HEAD_DIM] = a_sc[g, :, :HEAD_DIM].astype(BF)
+
+            return carry
+
+        lax.fori_loop(0, 8, request, 0)
+
+    smem = pl.BlockSpec(memory_space=pltpu.SMEM)
     return pl.pallas_call(
         kernel,
-        grid_spec=pltpu.PrefetchScalarGridSpec(
-            num_scalar_prefetch=2,
-            grid=(8,),
-            in_specs=[per, whole, whole],
-            out_specs=[per, pl.BlockSpec((1, 8, rows), lambda r, a, b: (r, 0, 0))],
-            scratch_shapes=[
-                pltpu.VMEM((2, rows, 128), F32),
-                pltpu.VMEM((2, rows, 128), F32),
-                pltpu.VMEM((2, rows, HEAD_DIM), F32),
-            ],
-        ),
+        in_specs=[smem, smem, VM, VM, VM],
+        out_specs=[VM, VM],
+        scratch_shapes=[
+            pltpu.VMEM((2, values.shape[0], 256), BF),
+            pltpu.VMEM((2, rows, 128), F32),
+            pltpu.VMEM((2, rows, 256), F32),
+        ],
         out_shape=[
             jax.ShapeDtypeStruct((8, rows, 256), BF),
             jax.ShapeDtypeStruct((8, 8, rows), F32),
         ],
-        compiler_params=pltpu.CompilerParams(vmem_limit_bytes=32 << 20),
+        compiler_params=pltpu.CompilerParams(vmem_limit_bytes=16 << 20),
         name="cached",
     )(begins, ends, queries, keys, values)
 
@@ -744,13 +739,13 @@
         ],
         0,
         "comm_a",
-        16,
+        60,
     )
     embedded = jnp.sum(came.astype(F32), axis=0).astype(BF)
     swapped = jnp.where((accept == 1)[:, None], embedded, block_states)
 
     (qs1,), (rows2, q2, k2, v2) = comm(
-        [gather_queries(q1), gather_project(swapped, weights)], 1, "comm_b", 16
+        [gather_queries(q1), gather_project(swapped, weights)], 1, "comm_b", 60
     )
     part1, stat1 = cached_attention(begins, ends, qs1, cache_keys, cache_values)
 
@@ -765,12 +760,11 @@
         12,
     )
     second = (part2, stat2, q2, k2, v2, w_out)
-    ((best, sum2),) = comm([gather_logits(normed, lm_head, other_head, second)], 4, "comm_e", 52)
-    (top, sums), (hiddens,) = comm(
-        [reduce_best(best, squares), reduce_layer(sum2, rows2, attn_gain, None)],
-        5,
-        "comm_f",
-        12,
+    ((top, sums, hiddens),) = comm(
+        [gather_logits(normed, squares, lm_head, other_head, second, rows2, attn_gain)],
+        4,
+        "comm_e",
+        56,
     )
     top_logits = top[:, :4].reshape(2, 64, 16).transpose(1, 0, 2).reshape(-1)
     request_norms = jnp.sqrt(sums[4, :8] / (256 * 4096))

time: 228 us -> 218 us (0.956)
  Pallas kernels: 199 us -> 191 us
  local copies, waits for them, and re-layouts: 21.4 us -> 17.6 us
    pallas_call x2, Pallas kernels: 21.5 us -> 15.5 us  [cached_attention(): pl.pallas_call(kernel, in_specs=[smem, smem, VM, VM, VM], out_specs=[VM,...]
    unnamed x37, local copies, waits for them, and re-layouts: 10.2 us -> 5.67 us
    pallas_call x6 -> x5, Pallas kernels: 172 us -> 170 us  [comm(): pl.pallas_call(kernel, out_shape=[o[0] for t in tasks for o in t.outs], i...]
  transfers between devices with their start and end apart: 1 -> 1, of which waited for: 0 -> 0; matrix products, arithmetic and copies ran while one was open for 7% -> 7% of each run, Pallas kernels for 56% -> 57%
where the time goes in v4:
time: 218 us
  Pallas kernels  191 us (88%)
  local copies, waits for them, and re-layouts  17.6 us (8%)
  other arithmetic  7.12 us (3%)
    pallas_call x5, Pallas kernels, comm(): pl.pallas_call(kernel, out_shape=[o[0] for t in tasks for o in t.outs], i...  170 us
    pallas_call x2, Pallas kernels, cached_attention(): pl.pallas_call(kernel, in_specs=[smem, smem, VM, VM, VM], out_specs=[VM,...  15.5 us
    gather x1, local copies, waits for them, and re-layouts, shards(): looked_up = jnp.take(embed, jnp.clip(local_ids, 0, vocab_here - 1), axis=0)  10.3 us
    unnamed x37, local copies, waits for them, and re-layouts  5.67 us
    pallas_call x1, Pallas kernels, combine(): pl.pallas_call(kernel, grid=(steps,), in_specs=[whole(a) for a in (parts,...  5.08 us
  transfers between devices with their start and end apart: 1, of which 0 were waited for; matrix products, arithmetic and copies ran while one was open for 7% of the time, Pallas kernels for 57%

profile of v4, /device:TPU:1, one launch (start us, length us, event | category | flops | bytes accessed | tf_op | source)
XLA Modules:
  0.0 217.8 jit_solution(10250811984538778306)
XLA Ops:
  0.6 1.5 collective-permute-start
  2.1 0.7 compare_and_fusion.1
  2.9 0.8 reduce-window.9
  3.7 0.7 fusion
  4.4 10.3 %gather_fusion = bf16[2048,256]{1,0:T(8,128)(2,1)S(1)} fusion(bf16[12544,256]{1,0:T(8,128)(2,1)} %param.26, s32[2048]{0:T(1024)S(1)} %fusion), kind=kCustom, calls=%fused_computation | custom fusion | bytes 2105344 | tf_op jit(solution)/shard_map/jit(_take)/gather | solution.py:731
  14.7 1.5 select_select_fusion.refs_4_
  16.2 26.3 %comm_a.1 = (bf16[16,4096]{1,0:T(8,128)(2,1)}, bf16[256,256]{1,0:T(8,128)(2,1)}, bf16[256,256]{1,0:T(8,128)(2,1)}, bf16[256,256]{1,0:T(8,128)(2,1)}, bf16[8,256,256]{2,1,0:T(8,128)(2,1)}) custom-call(bf16[256,256]{1,0:T(8,128)(2,1)} %refs_0_.1, bf16[4096,256]{1,0:T(8,128)(2,1)} %refs_2_.3, bf16[4096,256]{1,0:T(8,128)(2,1)} %refs_3_.3, ...), custom_call_target="tpu_custom_call" | custom-call | tf_op jit(solution)/shard_map/comm_a/pallas_call | solution.py:116
  42.5 1.4 reduce_sum.12
  43.9 0.0 copy-done.17
  43.9 0.0 copy-done.15
  43.9 0.8 broadcast_select_fusion.refs_1_
  44.7 23.9 %comm_b.1 = (bf16[8,256,256]{2,1,0:T(8,128)(2,1)}, bf16[16,4096]{1,0:T(8,128)(2,1)}, bf16[256,256]{1,0:T(8,128)(2,1)}, bf16[256,256]{1,0:T(8,128)(2,1)}, bf16[256,256]{1,0:T(8,128)(2,1)}) custom-call(bf16[256,256]{1,0:T(8,128)(2,1)} %get-tuple-element.27.refs_0_.q_ref, bf16[256,256]{1,0:T(8,128)(2,1)} %broadcast_select_fusion.refs_1_, ...), custom_call_target="tpu_custom_call" | custom-call | tf_op jit(solution)/shard_map/comm_b/pallas_call | solution.py:116
  68.6 0.0 copy-done.16
  68.6 0.0 copy-done.1
  68.6 0.0 copy-done.2
  68.6 0.0 copy-start.4
  68.6 1.2 copy-done.4
  69.8 7.7 %cached.2 = (bf16[8,256,256]{2,1,0:T(8,128)(2,1)S(1)}, f32[8,8,256]{2,1,0:T(8,128)S(1)}) custom-call(s32[8]{0:T(128)S(1)} %get-tuple-element.54.lo_ref, s32[8]{0:T(128)S(1)} %get-tuple-element.53.hi_ref, bf16[8,256,256]{2,1,0:T(8,128)(2,1)S(1)} %copy-done.4, bf16[1024,256]{1,0:T(8,128)(2,1)S(1)} %copy-done.1, bf16[1024,256]{1,0:T(8,128)(2,1)S(1)} %copy-done.2), custom_call_target="tpu_custom_call" | custom-call | tf_op jit(solution)/shard_map/cached/pallas_call | solution.py:638
  77.6 0.0 copy-start
  77.6 0.0 copy-start.6
  77.6 0.0 copy-start.9
  77.6 0.0 copy-start.10
  77.6 0.0 copy-done.5
  77.6 27.2 %comm_c.1 = (bf16[8,256,256]{2,1,0:T(8,128)(2,1)S(1)}, f32[8,8,256]{2,1,0:T(8,128)S(1)}, bf16[8,256,256]{2,1,0:T(8,128)(2,1)S(1)}) custom-call(bf16[8,256,256]{2,1,0:T(8,128)(2,1)S(1)} %get-tuple-element.30.refs_0_, f32[8,8,256]{2,1,0:T(8,128)S(1)} %get-tuple-element.31.refs_1_, bf16[256,256]{1,0:T(8,128)(2,1)S(1)} %copy-done.5), custom_call_target="tpu_custom_call" | custom-call | tf_op jit(solution)/shard_map/comm_c/pallas_call | solution.py:116
  104.9 7.7 %cached.3 = (bf16[8,256,256]{2,1,0:T(8,128)(2,1)S(1)}, f32[8,8,256]{2,1,0:T(8,128)S(1)}) custom-call(s32[8]{0:T(128)S(1)} %get-tuple-element.54.lo_ref, s32[8]{0:T(128)S(1)} %get-tuple-element.53.hi_ref, bf16[8,256,256]{2,1,0:T(8,128)(2,1)S(1)} %get-tuple-element.38.q_ref, bf16[1024,256]{1,0:T(8,128)(2,1)S(1)} %copy-done.1, bf16[1024,256]{1,0:T(8,128)(2,1)S(1)} %copy-done.2), custom_call_target="tpu_custom_call" | custom-call | tf_op jit(solution)/shard_map/cached/pallas_call | solution.py:638
  112.6 0.0 copy-done
  112.6 0.0 copy-done.6
  112.6 0.0 copy-done.9
  112.6 0.0 copy-done.10
  112.7 0.0 copy-start.8
  112.7 0.0 copy-start.12
  112.7 0.0 copy-start.13
  112.7 5.1 %combine.1.refs_0_ = bf16[2,4,2,16,4096]{4,3,2,1,0:T(8,128)(2,1)S(1)} custom-call(bf16[8,256,256]{2,1,0:T(8,128)(2,1)S(1)} %get-tuple-element.33.p_ref, f32[8,8,256]{2,1,0:T(8,128)S(1)} %get-tuple-element.34.s_ref, bf16[256,256]{1,0:T(8,128)(2,1)S(1)} %copy-done.6, bf16[256,256]{1,0:T(8,128)(2,1)S(1)} %copy-done.9, bf16[256,256]{1,0:T(8,128)(2,1)S(1)} %copy-done.10, ...), custom_call_target="tpu_custom_call" | custom-call | tf_op jit(solution)/shard_map/combine/pallas_call | solution.py:690
  117.8 0.0 copy-done.8
  117.8 0.0 copy-done.12
  117.8 25.3 %comm_d.1 = (bf16[16,4096]{1,0:T(8,128)(2,1)S(1)}, f32[8,256]{1,0:T(8,128)S(1)}, bf16[8,256,256]{2,1,0:T(8,128)(2,1)S(1)}, f32[8,8,256]{2,1,0:T(8,128)S(1)}) custom-call(bf16[2,4,2,16,4096]{4,3,2,1,0:T(8,128)(2,1)S(1)} %combine.1.refs_0_, bf16[16,4096]{1,0:T(8,128)(2,1)S(1)} %copy-done.8, f32[1,4096]{1,0:T(1,128)S(1)} %bitcast.16, f32[1,4096]{1,0:T(1,128)S(1)} %bitcast.17, ...), custom_call_target="tpu_custom_call" | custom-call | tf_op jit(solution)/shard_map/comm_d/pallas_call | solution.py:116
  143.1 0.9 copy-done.3
  144.1 0.7 copy-done.7
  144.7 0.6 copy-done.11
  145.4 0.6 copy-done.14
  146.0 0.0 collective-permute-done.refs_5_
  146.0 67.5 %comm_e.1 = (f32[2,8,256]{2,1,0:T(8,128)}, f32[8,256]{1,0:T(8,128)}, bf16[16,4096]{1,0:T(8,128)(2,1)}) custom-call(bf16[16,4096]{1,0:T(8,128)(2,1)} %copy-done.7, f32[8,256]{1,0:T(8,128)} %copy-done.14, bf16[16,4096]{1,0:T(8,128)(2,1)} %get-tuple-element.43.refs_2_, f32[1,4096]{1,0:T(1,128)} %bitcast.15, bf16[784,4096]{1,0:T(8,128)(2,1)} %refs_4_.3, ...), custom_call_target="tpu_custom_call" | custom-call | tf_op jit(solution)/shard_map/comm_e/pallas_call | solution.py:116
  213.5 1.2 sqrt_bitcast_fusion
  214.7 0.7 slice.7
  215.4 0.1 reshape.70
  215.5 0.1 copy.17
  215.5 0.7 reshape.71
  216.3 1.6 copy.19
  (15 shorter events, 0.1 us)
Async XLA Ops:
  0.6 145.4 %collective-permute-start = (bf16[784,4096]{1,0:T(8,128)(2,1)}, bf16[784,4096]{1,0:T(8,128)(2,1)}, u32[]{:S(2)}, u32[]{:S(2)}) collective-permute-start(bf16[784,4096]{1,0:T(8,128)(2,1)} %refs_4_.3), channel_id=1, source_target_pairs={{0,1},{1,0},{2,3},{3,2},{4,5},{5,4},{6,7},{7,6},{8,9},{9,8},{10,11... | collective-permute-start | bytes 19267592 | tf_op jit(solution)/shard_map/ppermute | solution.py:720
  16.2 27.7 %copy-start.17 = (s32[256]{0:T(256)S(1)}, s32[256]{0:T(256)}, u32[]{:S(2)}) copy-start(s32[256]{0:T(256)} %param.16) | copy-start | bytes 3076
  16.2 27.7 %copy-start.15 = (bf16[256,256]{1,0:T(8,128)(2,1)S(1)}, bf16[256,256]{1,0:T(8,128)(2,1)}, u32[]{:S(2)}) copy-start(bf16[256,256]{1,0:T(8,128)(2,1)} %refs_0_.1) | copy-start | bytes 393220
  44.7 23.9 %copy-start.16 = (s32[8]{0:T(128)S(1)}, s32[8]{0:T(128)}, u32[]{:S(2)}) copy-start(s32[8]{0:T(128)} %param.17) | copy-start | bytes 100
  44.7 23.9 %copy-start.1 = (bf16[1024,256]{1,0:T(8,128)(2,1)S(1)}, bf16[1024,256]{1,0:T(8,128)(2,1)}, u32[]{:S(2)}) copy-start(bf16[1024,256]{1,0:T(8,128)(2,1)} %k_ref.3) | copy-start | bytes 1572868
  44.7 23.9 %copy-start.2 = (bf16[1024,256]{1,0:T(8,128)(2,1)S(1)}, bf16[1024,256]{1,0:T(8,128)(2,1)}, u32[]{:S(2)}) copy-start(bf16[1024,256]{1,0:T(8,128)(2,1)} %v_ref.3) | copy-start | bytes 1572868
  68.6 1.2 copy-start.4
  69.8 7.8 %copy-start.5 = (bf16[256,256]{1,0:T(8,128)(2,1)S(1)}, bf16[256,256]{1,0:T(8,128)(2,1)}, u32[]{:S(2)}) copy-start(bf16[256,256]{1,0:T(8,128)(2,1)} %get-tuple-element.32.refs_2_.refs_8_) | copy-start | bytes 393220
  77.6 35.0 %copy-start = (bf16[256,4096]{1,0:T(8,128)(2,1)S(1)}, bf16[256,4096]{1,0:T(8,128)(2,1)}, u32[]{:S(2)}) copy-start(bf16[256,4096]{1,0:T(8,128)(2,1)} %refs_11_.1) | copy-start | bytes 6291460
  77.6 35.0 %copy-start.6 = (bf16[256,256]{1,0:T(8,128)(2,1)S(1)}, bf16[256,256]{1,0:T(8,128)(2,1)}, u32[]{:S(2)}) copy-start(bf16[256,256]{1,0:T(8,128)(2,1)} %get-tuple-element.27.refs_0_.q_ref) | copy-start | bytes 393220
  77.6 35.0 %copy-start.9 = (bf16[256,256]{1,0:T(8,128)(2,1)S(1)}, bf16[256,256]{1,0:T(8,128)(2,1)}, u32[]{:S(2)}) copy-start(bf16[256,256]{1,0:T(8,128)(2,1)} %get-tuple-element.35.k_ref) | copy-start | bytes 393220
  77.6 35.0 %copy-start.10 = (bf16[256,256]{1,0:T(8,128)(2,1)S(1)}, bf16[256,256]{1,0:T(8,128)(2,1)}, u32[]{:S(2)}) copy-start(bf16[256,256]{1,0:T(8,128)(2,1)} %get-tuple-element.36.v_ref) | copy-start | bytes 393220
  112.7 5.1 %copy-start.8 = (bf16[16,4096]{1,0:T(8,128)(2,1)S(1)}, bf16[16,4096]{1,0:T(8,128)(2,1)}, u32[]{:S(2)}) copy-start(bf16[16,4096]{1,0:T(8,128)(2,1)} %get-tuple-element.37.refs_1_) | copy-start | bytes 393220
  112.7 5.1 %copy-start.12 = (f32[4096]{0:T(1024)S(1)}, f32[4096]{0:T(1024)}, u32[]{:S(2)}) copy-start(f32[4096]{0:T(1024)} %param.24) | copy-start | bytes 49156
  112.7 5.1 %copy-start.13 = (f32[4096]{0:T(1024)S(1)}, f32[4096]{0:T(1024)}, u32[]{:S(2)}) copy-start(f32[4096]{0:T(1024)} %param.25) | copy-start | bytes 49156
  143.1 1.0 copy-start.3
  144.1 0.7 copy-start.7
  144.7 0.6 copy-start.11
  145.4 0.6 copy-start.14

commit v5 on v4

--- a/solution.py
+++ b/solution.py
@@ -350,20 +350,22 @@
     return shift(*{"x": (d, 0, 0, 0), "y": (0, d, 0, 0), "z": (0, 0, d, 0)}[axis])
 
 
-CHUNKS = ((384, 384, 256), (384, 384, 256), (384, 384, 256), (512, 384, 128))
+CHUNKS = ((512, 512, 512), (512, 512, 512), (384, 384, 256))
+STARTS = (0, 1536, 3072, 4096)
 ORDERS = ("xyz", "yzx", "zxy")
 
 
 def gather_logits(normed, squares, own_head, other_head, second, states_in, attn_gain):
     vocab = own_head.shape[0]
+    n = len(CHUNKS)
 
     def body(ins, outs, scr):
         n_ref, sq_ref, x_ref, again_ref, own_ref, other_ref = ins[:6]
         top_ref, sum_ref, hid_ref = outs
-        bufs = [scr[3 * i : 3 * i + 3] for i in range(4)]
-        heads, acc = scr[12:14]
-        held = scr[14:20]
-        att, out, theirs, came, far, maxima, wide, deep, send, recv, loc = scr[20:]
+        bufs = [scr[3 * i : 3 * i + 3] for i in range(n)]
+        heads, acc = scr[9:11]
+        held = scr[11:17]
+        att, out, theirs, came, far, maxima, wide, deep, send, recv, loc = scr[17:]
         z, xl, xh, y, c = coords()
         x = xh * 2 + xl
         links = Links(send, recv)
@@ -397,7 +399,7 @@
             return bufs[i][p].at[tuple(at)]
 
         start = 0
-        for i in range(4):
+        for i in range(n):
             for p in range(3):
                 bufs[i][p][z, xl, xh, y] = n_ref[:, start : start + CHUNKS[i][p]]
                 start += CHUNKS[i][p]
@@ -432,7 +434,7 @@
             return out
 
         def multiply(i):
-            cut = pl.ds(1024 * i, 1024)
+            cut = pl.ds(STARTS[i], STARTS[i + 1] - STARTS[i])
 
             def step(r, carry):
                 rows = jnp.concatenate(
@@ -445,12 +447,12 @@
                     )
                     if i > 0:
                         part = acc[k, r] + part
-                    if i < 3:
+                    if i < n - 1:
                         acc[k, r] = part
                     else:
                         m = jnp.max(part, axis=0, keepdims=True)
                         top = m if top is None else jnp.maximum(top, m)
-                if i == 3:
+                if i == n - 1:
                     maxima[0, pl.ds(r, 1), :] = top
                 return carry
 
@@ -460,10 +462,10 @@
             pltpu.make_async_copy(src, dst, loc.at[2 + k])
             for k, (src, dst) in enumerate(zip(ins[6:], held))
         ]
-        one = [spread(i, 0, None) for i in range(4)]
+        one = [spread(i, 0, None) for i in range(n)]
         for cp in fetch + loads:
             cp.start()
-        two = [spread(i, 1, one[i]) for i in range(4)]
+        two = [spread(i, 1, one[i]) for i in range(n)]
         three = {0: spread(0, 2, two[0]), 1: spread(1, 2, two[1])}
         for cp in fetch:
             cp.wait()
@@ -479,10 +481,10 @@
         swap = links.copy(out.at[:, :, 1 - c], theirs, shift(0, 0, 0, 1))
         over_y = []
         four = {0: relay(0, three[0])}
-        for i in range(4):
-            if i + 1 < 4:
+        for i in range(n):
+            if i + 1 < n:
                 four[i + 1] = relay(i + 1, three[i + 1])
-            if i + 2 < 4:
+            if i + 2 < n:
                 three[i + 2] = spread(i + 2, 2, two[i + 2])
             for pair in four[i]:
                 for cp in pair:
@@ -490,10 +492,8 @@
             if i == 0:
                 for cp in loads:
                     cp.wait()
-            if i == 3:
+            if i == n - 1:
                 maxima[0] = sq_ref[...]
-            multiply(i)
-            if i == 0:
                 swap.wait()
                 for dy in (2, 1, 3, 0):
                     y_ = ring(y, dy)
@@ -506,35 +506,29 @@
                                 theirs.at[:, y_], came.at[:, y], place(z, xl, xh, y_, c)
                             )
                         )
-            if i == 2:
-                for cp in over_y:
-                    cp.wait_recv()
-                for xh_ in (0, 1):
-                    v = theirs[xh_, y].astype(F32)
-                    for dy in (1, 3, 2):
-                        v = v + came[xh_, ring(y, dy)].astype(F32)
-                    theirs[xh_, y] = v.astype(BF)
-                over_x = links.copy(
-                    theirs.at[1 - xh, y], far, place(z, xl, 1 - xh, y, c)
-                )
+            multiply(i)
         top = lax.broadcasted_iota(jnp.int32, (8, 256), 0) < 4
 
         def join(v, w):
             return jnp.where(top, jnp.maximum(v, w), v + w)
 
-        cps = [links.copy(maxima.at[0], wide.at[k], shift(*key)) for k, key in enumerate(PLANE)]
-        over_x.wait_recv()
-        total = theirs[xh, y].astype(F32) + far[...].astype(F32)
-        hid_ref[...] = layer_end(x_ref[...], total, again_ref[...])
-        everything += over_y + [over_x]
-        for cp in cps:
+        flat = [links.copy(maxima.at[0], wide.at[k], shift(*key)) for k, key in enumerate(PLANE)]
+        for cp in flat:
             cp.wait()
         mine = maxima[0]
         for k in range(15):
             mine = join(mine, wide[k])
         maxima[1] = mine
-        cps = [links.copy(maxima.at[1], deep.at[k], shift(*key)) for k, key in enumerate(DEEP)]
-        for cp in cps:
+        tall = [links.copy(maxima.at[1], deep.at[k], shift(*key)) for k, key in enumerate(DEEP)]
+        for cp in over_y:
+            cp.wait_recv()
+        for xh_ in (0, 1):
+            v = theirs[xh_, y].astype(F32)
+            for dy in (1, 3, 2):
+                v = v + came[xh_, ring(y, dy)].astype(F32)
+            theirs[xh_, y] = v.astype(BF)
+        over_x = links.copy(theirs.at[1 - xh, y], far, place(z, xl, 1 - xh, y, c))
+        for cp in tall:
             cp.wait()
         for k in range(3):
             mine = join(mine, deep[k])
@@ -544,6 +538,10 @@
         top_ref[c] = mine
         top_ref[1 - c] = other
         sum_ref[...] = mine + other
+        over_x.wait_recv()
+        total = theirs[xh, y].astype(F32) + far[...].astype(F32)
+        hid_ref[...] = layer_end(x_ref[...], total, again_ref[...])
+        everything += over_y + [over_x]
         for cp in everything:
             cp.wait_send()
         yield 0
@@ -571,7 +569,7 @@
             (jax.ShapeDtypeStruct((16, 4096), BF), VM),
         ],
         scratch,
-        4 * 3 * 10 + 5 + 22,
+        3 * 3 * 10 + 5 + 22,
         8,
         AXES + PLANE + DEEP,
     )
@@ -583,7 +581,7 @@
 
 def cached_attention(begins, ends, queries, keys, values):
     rows = queries.shape[1]
-    span = 256
+    cuts = [slice(g * HEAD_DIM, (g + 1) * HEAD_DIM) for g in (0, 1)]
 
     def kernel(lo_ref, hi_ref, q_ref, k_ref, v_ref, o_ref, s_ref, v_sc, m_sc, a_sc):
         for g in range(2):
@@ -605,24 +603,40 @@
                 m_sc[...] = jnp.full_like(m_sc, NEG)
                 a_sc[...] = jnp.zeros_like(a_sc)
 
-                def step(b, carry):
+                def step(b, span):
                     at = pl.multiple_of(b * span, span)
                     pos = at + lax.broadcasted_iota(jnp.int32, (1, span), 1)
                     bias = jnp.where((pos >= lo) & (pos < hi), 0.0, NEG)
-                    for g in range(2):
-                        cut = slice(g * HEAD_DIM, (g + 1) * HEAD_DIM)
-                        s = scores(q_ref[r, :, cut], k_ref[pl.ds(at, span), cut]) + bias
-                        old = m_sc[g]
-                        new = jnp.maximum(old, jnp.max(s, axis=-1, keepdims=True))
-                        p = jnp.exp2(s - new[:, 0:1]).astype(BF)
-                        f = jnp.exp2(old - new)
-                        a_sc[g] = a_sc[g] * jnp.concatenate([f, f], axis=1) + jnp.dot(
-                            p, v_sc[g, pl.ds(at, span), :], preferred_element_type=F32
-                        )
-                        m_sc[g] = new
-                    return carry
-
-                lax.fori_loop(lo // span, (hi + span - 1) // span, step, 0)
+                    ss = [scores(q_ref[r, :, cut], k_ref[pl.ds(at, span), cut]) for cut in cuts]
+                    ss = [s + bias for s in ss]
+                    old = [m_sc[g] for g in (0, 1)]
+                    new = [
+                        jnp.maximum(o, jnp.max(s, axis=-1, keepdims=True)) for o, s in zip(old, ss)
+                    ]
+                    ps = [jnp.exp2(s - m[:, 0:1]).astype(BF) for s, m in zip(ss, new)]
+                    fs = [jnp.exp2(o - m) for o, m in zip(old, new)]
+                    ds = [
+                        jnp.dot(p, v_sc[g, pl.ds(at, span), :], preferred_element_type=F32)
+                        for g, p in enumerate(ps)
+                    ]
+                    for g in (0, 1):
+                        a_sc[g] = a_sc[g] * jnp.concatenate([fs[g], fs[g]], axis=1) + ds[g]
+                        m_sc[g] = new[g]
+
+                small = lo // 256 == (hi - 1) // 256
+
+                @pl.when(small)
+                def _():
+                    step(lo // 256, 256)
+
+                @pl.when(jnp.logical_not(small))
+                def _():
+                    def wide_step(b, carry):
+                        step(b, 512)
+                        return carry
+
+                    lax.fori_loop(lo // 512, (hi + 511) // 512, wide_step, 0)
+
                 stats = jnp.where(lane == 0, m_sc[0], m_sc[1])
                 stats = jnp.where(lane == 2, a_sc[0, :, HEAD_DIM:], stats)
                 stats = jnp.where(lane == 3, a_sc[1, :, HEAD_DIM:], stats)

time: 218 us -> 214 us (0.982)
  Pallas kernels: 191 us -> 186 us
    pallas_call x5, Pallas kernels: 170 us -> 168 us  [comm(): pl.pallas_call(kernel, out_shape=[o[0] for t in tasks for o in t.outs], i...]
  transfers between devices with their start and end apart: 1 -> 1, of which waited for: 0 -> 0; matrix products, arithmetic and copies ran while one was open for 7% -> 8% of each run, Pallas kernels for 57% -> 57%
where the time goes in v5:
time: 214 us; the launch traced here: 213 us
  Pallas kernels  186 us (87%)
  local copies, waits for them, and re-layouts  17.6 us (8%)
  other arithmetic  7.12 us (3%)
    pallas_call x5, Pallas kernels, comm(): pl.pallas_call(kernel, out_shape=[o[0] for t in tasks for o in t.outs], i...  168 us
    pallas_call x2, Pallas kernels, cached_attention(): pl.pallas_call(kernel, in_specs=[smem, smem, VM, VM, VM], out_specs=[VM,...  13.5 us
    gather x1, local copies, waits for them, and re-layouts, shards(): looked_up = jnp.take(embed, jnp.clip(local_ids, 0, vocab_here - 1), axis=0)  10.3 us
    unnamed x37, local copies, waits for them, and re-layouts  5.67 us
    pallas_call x1, Pallas kernels, combine(): pl.pallas_call(kernel, grid=(steps,), in_specs=[whole(a) for a in (parts,...  5.26 us
  transfers between devices with their start and end apart: 1, of which 0 were waited for; matrix products, arithmetic and copies ran while one was open for 8% of the time, Pallas kernels for 57%

profile of v5, /device:TPU:1, one launch (start us, length us, event | category | flops | bytes accessed | tf_op | source)
XLA Modules:
  0.0 213.4 jit_solution(14620368165530473355)
XLA Ops:
  0.6 1.5 collective-permute-start
  2.1 0.7 compare_and_fusion.1
  2.9 0.8 reduce-window.9
  3.7 0.7 fusion
  4.4 10.3 %gather_fusion = bf16[2048,256]{1,0:T(8,128)(2,1)S(1)} fusion(bf16[12544,256]{1,0:T(8,128)(2,1)} %param.26, s32[2048]{0:T(1024)S(1)} %fusion), kind=kCustom, calls=%fused_computation | custom fusion | bytes 2105344 | tf_op jit(solution)/shard_map/jit(_take)/gather | solution.py:745
  14.7 1.5 select_select_fusion.refs_4_
  16.2 26.3 %comm_a.1 = (bf16[16,4096]{1,0:T(8,128)(2,1)}, bf16[256,256]{1,0:T(8,128)(2,1)}, bf16[256,256]{1,0:T(8,128)(2,1)}, bf16[256,256]{1,0:T(8,128)(2,1)}, bf16[8,256,256]{2,1,0:T(8,128)(2,1)}) custom-call(bf16[256,256]{1,0:T(8,128)(2,1)} %refs_0_.1, bf16[4096,256]{1,0:T(8,128)(2,1)} %refs_2_.3, bf16[4096,256]{1,0:T(8,128)(2,1)} %refs_3_.3, ...), custom_call_target="tpu_custom_call" | custom-call | tf_op jit(solution)/shard_map/comm_a/pallas_call | solution.py:116
  42.5 1.4 reduce_sum.12
  43.9 0.0 copy-done.17
  43.9 0.0 copy-done.15
  43.9 0.8 broadcast_select_fusion.refs_1_
  44.7 23.9 %comm_b.1 = (bf16[8,256,256]{2,1,0:T(8,128)(2,1)}, bf16[16,4096]{1,0:T(8,128)(2,1)}, bf16[256,256]{1,0:T(8,128)(2,1)}, bf16[256,256]{1,0:T(8,128)(2,1)}, bf16[256,256]{1,0:T(8,128)(2,1)}) custom-call(bf16[256,256]{1,0:T(8,128)(2,1)} %get-tuple-element.27.refs_0_.q_ref, bf16[256,256]{1,0:T(8,128)(2,1)} %broadcast_select_fusion.refs_1_, ...), custom_call_target="tpu_custom_call" | custom-call | tf_op jit(solution)/shard_map/comm_b/pallas_call | solution.py:116
  68.6 0.0 copy-done.16
  68.6 0.0 copy-done.1
  68.6 0.0 copy-done.2
  68.6 0.0 copy-start.4
  68.6 1.2 copy-done.4
  69.8 6.7 %cached.2 = (bf16[8,256,256]{2,1,0:T(8,128)(2,1)S(1)}, f32[8,8,256]{2,1,0:T(8,128)S(1)}) custom-call(s32[8]{0:T(128)S(1)} %get-tuple-element.54.lo_ref, s32[8]{0:T(128)S(1)} %get-tuple-element.53.hi_ref, bf16[8,256,256]{2,1,0:T(8,128)(2,1)S(1)} %copy-done.4, bf16[1024,256]{1,0:T(8,128)(2,1)S(1)} %copy-done.1, bf16[1024,256]{1,0:T(8,128)(2,1)S(1)} %copy-done.2), custom_call_target="tpu_custom_call" | custom-call | tf_op jit(solution)/shard_map/cached/pallas_call | solution.py:652
  76.6 0.0 copy-start
  76.6 0.0 copy-start.6
  76.6 0.0 copy-start.9
  76.6 0.0 copy-start.10
  76.6 0.0 copy-done.5
  76.6 27.2 %comm_c.1 = (bf16[8,256,256]{2,1,0:T(8,128)(2,1)S(1)}, f32[8,8,256]{2,1,0:T(8,128)S(1)}, bf16[8,256,256]{2,1,0:T(8,128)(2,1)S(1)}) custom-call(bf16[8,256,256]{2,1,0:T(8,128)(2,1)S(1)} %get-tuple-element.30.refs_0_, f32[8,8,256]{2,1,0:T(8,128)S(1)} %get-tuple-element.31.refs_1_, bf16[256,256]{1,0:T(8,128)(2,1)S(1)} %copy-done.5), custom_call_target="tpu_custom_call" | custom-call | tf_op jit(solution)/shard_map/comm_c/pallas_call | solution.py:116
  103.9 6.7 %cached.3 = (bf16[8,256,256]{2,1,0:T(8,128)(2,1)S(1)}, f32[8,8,256]{2,1,0:T(8,128)S(1)}) custom-call(s32[8]{0:T(128)S(1)} %get-tuple-element.54.lo_ref, s32[8]{0:T(128)S(1)} %get-tuple-element.53.hi_ref, bf16[8,256,256]{2,1,0:T(8,128)(2,1)S(1)} %get-tuple-element.38.q_ref, bf16[1024,256]{1,0:T(8,128)(2,1)S(1)} %copy-done.1, bf16[1024,256]{1,0:T(8,128)(2,1)S(1)} %copy-done.2), custom_call_target="tpu_custom_call" | custom-call | tf_op jit(solution)/shard_map/cached/pallas_call | solution.py:652
  110.6 0.0 copy-done
  110.6 0.0 copy-done.6
  110.6 0.0 copy-done.9
  110.7 0.0 copy-done.10
  110.7 0.0 copy-start.8
  110.7 0.0 copy-start.12
  110.7 0.0 copy-start.13
  110.7 5.3 %combine.1.refs_0_ = bf16[2,4,2,16,4096]{4,3,2,1,0:T(8,128)(2,1)S(1)} custom-call(bf16[8,256,256]{2,1,0:T(8,128)(2,1)S(1)} %get-tuple-element.33.p_ref, f32[8,8,256]{2,1,0:T(8,128)S(1)} %get-tuple-element.34.s_ref, bf16[256,256]{1,0:T(8,128)(2,1)S(1)} %copy-done.6, bf16[256,256]{1,0:T(8,128)(2,1)S(1)} %copy-done.9, bf16[256,256]{1,0:T(8,128)(2,1)S(1)} %copy-done.10, ...), custom_call_target="tpu_custom_call" | custom-call | tf_op jit(solution)/shard_map/combine/pallas_call | solution.py:704
  116.0 0.0 copy-done.8
  116.0 0.0 copy-done.12
  116.0 25.3 %comm_d.1 = (bf16[16,4096]{1,0:T(8,128)(2,1)S(1)}, f32[8,256]{1,0:T(8,128)S(1)}, bf16[8,256,256]{2,1,0:T(8,128)(2,1)S(1)}, f32[8,8,256]{2,1,0:T(8,128)S(1)}) custom-call(bf16[2,4,2,16,4096]{4,3,2,1,0:T(8,128)(2,1)S(1)} %combine.1.refs_0_, bf16[16,4096]{1,0:T(8,128)(2,1)S(1)} %copy-done.8, f32[1,4096]{1,0:T(1,128)S(1)} %bitcast.16, f32[1,4096]{1,0:T(1,128)S(1)} %bitcast.17, ...), custom_call_target="tpu_custom_call" | custom-call | tf_op jit(solution)/shard_map/comm_d/pallas_call | solution.py:116
  141.3 0.9 copy-done.3
  142.3 0.7 copy-done.7
  142.9 0.6 copy-done.11
  143.6 0.6 copy-done.14
  144.2 0.0 collective-permute-done.refs_5_
  144.2 64.9 %comm_e.1 = (f32[2,8,256]{2,1,0:T(8,128)}, f32[8,256]{1,0:T(8,128)}, bf16[16,4096]{1,0:T(8,128)(2,1)}) custom-call(bf16[16,4096]{1,0:T(8,128)(2,1)} %copy-done.7, f32[8,256]{1,0:T(8,128)} %copy-done.14, bf16[16,4096]{1,0:T(8,128)(2,1)} %get-tuple-element.43.refs_2_, f32[1,4096]{1,0:T(1,128)} %bitcast.15, bf16[784,4096]{1,0:T(8,128)(2,1)} %refs_4_.3, ...), custom_call_target="tpu_custom_call" | custom-call | tf_op jit(solution)/shard_map/comm_e/pallas_call | solution.py:116
  209.0 1.2 sqrt_bitcast_fusion
  210.2 0.7 slice.7
  211.0 0.1 reshape.70
  211.1 0.1 copy.17
  211.1 0.7 reshape.71
  211.8 1.6 copy.19
  (15 shorter events, 0.1 us)
Async XLA Ops:
  0.6 143.5 %collective-permute-start = (bf16[784,4096]{1,0:T(8,128)(2,1)}, bf16[784,4096]{1,0:T(8,128)(2,1)}, u32[]{:S(2)}, u32[]{:S(2)}) collective-permute-start(bf16[784,4096]{1,0:T(8,128)(2,1)} %refs_4_.3), channel_id=1, source_target_pairs={{0,1},{1,0},{2,3},{3,2},{4,5},{5,4},{6,7},{7,6},{8,9},{9,8},{10,11... | collective-permute-start | bytes 19267592 | tf_op jit(solution)/shard_map/ppermute | solution.py:734
  16.2 27.7 %copy-start.17 = (s32[256]{0:T(256)S(1)}, s32[256]{0:T(256)}, u32[]{:S(2)}) copy-start(s32[256]{0:T(256)} %param.16) | copy-start | bytes 3076
  16.2 27.7 %copy-start.15 = (bf16[256,256]{1,0:T(8,128)(2,1)S(1)}, bf16[256,256]{1,0:T(8,128)(2,1)}, u32[]{:S(2)}) copy-start(bf16[256,256]{1,0:T(8,128)(2,1)} %refs_0_.1) | copy-start | bytes 393220
  44.7 23.9 %copy-start.16 = (s32[8]{0:T(128)S(1)}, s32[8]{0:T(128)}, u32[]{:S(2)}) copy-start(s32[8]{0:T(128)} %param.17) | copy-start | bytes 100
  44.7 23.9 %copy-start.1 = (bf16[1024,256]{1,0:T(8,128)(2,1)S(1)}, bf16[1024,256]{1,0:T(8,128)(2,1)}, u32[]{:S(2)}) copy-start(bf16[1024,256]{1,0:T(8,128)(2,1)} %k_ref.3) | copy-start | bytes 1572868
  44.7 23.9 %copy-start.2 = (bf16[1024,256]{1,0:T(8,128)(2,1)S(1)}, bf16[1024,256]{1,0:T(8,128)(2,1)}, u32[]{:S(2)}) copy-start(bf16[1024,256]{1,0:T(8,128)(2,1)} %v_ref.3) | copy-start | bytes 1572868
  68.6 1.2 copy-start.4
  69.8 6.8 %copy-start.5 = (bf16[256,256]{1,0:T(8,128)(2,1)S(1)}, bf16[256,256]{1,0:T(8,128)(2,1)}, u32[]{:S(2)}) copy-start(bf16[256,256]{1,0:T(8,128)(2,1)} %get-tuple-element.32.refs_2_.refs_8_) | copy-start | bytes 393220
  76.6 34.0 %copy-start = (bf16[256,4096]{1,0:T(8,128)(2,1)S(1)}, bf16[256,4096]{1,0:T(8,128)(2,1)}, u32[]{:S(2)}) copy-start(bf16[256,4096]{1,0:T(8,128)(2,1)} %refs_11_.1) | copy-start | bytes 6291460
  76.6 34.0 %copy-start.6 = (bf16[256,256]{1,0:T(8,128)(2,1)S(1)}, bf16[256,256]{1,0:T(8,128)(2,1)}, u32[]{:S(2)}) copy-start(bf16[256,256]{1,0:T(8,128)(2,1)} %get-tuple-element.27.refs_0_.q_ref) | copy-start | bytes 393220
  76.6 34.0 %copy-start.9 = (bf16[256,256]{1,0:T(8,128)(2,1)S(1)}, bf16[256,256]{1,0:T(8,128)(2,1)}, u32[]{:S(2)}) copy-start(bf16[256,256]{1,0:T(8,128)(2,1)} %get-tuple-element.35.k_ref) | copy-start | bytes 393220
  76.6 34.0 %copy-start.10 = (bf16[256,256]{1,0:T(8,128)(2,1)S(1)}, bf16[256,256]{1,0:T(8,128)(2,1)}, u32[]{:S(2)}) copy-start(bf16[256,256]{1,0:T(8,128)(2,1)} %get-tuple-element.36.v_ref) | copy-start | bytes 393220
  110.7 5.3 %copy-start.8 = (bf16[16,4096]{1,0:T(8,128)(2,1)S(1)}, bf16[16,4096]{1,0:T(8,128)(2,1)}, u32[]{:S(2)}) copy-start(bf16[16,4096]{1,0:T(8,128)(2,1)} %get-tuple-element.37.refs_1_) | copy-start | bytes 393220
  110.7 5.3 %copy-start.12 = (f32[4096]{0:T(1024)S(1)}, f32[4096]{0:T(1024)}, u32[]{:S(2)}) copy-start(f32[4096]{0:T(1024)} %param.24) | copy-start | bytes 49156
  110.7 5.3 %copy-start.13 = (f32[4096]{0:T(1024)S(1)}, f32[4096]{0:T(1024)}, u32[]{:S(2)}) copy-start(f32[4096]{0:T(1024)} %param.25) | copy-start | bytes 49156
  141.3 1.0 copy-start.3
  142.3 0.7 copy-start.7
  142.9 0.6 copy-start.11
  143.6 0.6 copy-start.14

commit v6 on v5

--- a/solution.py
+++ b/solution.py
@@ -280,6 +280,89 @@
     )
 
 
+def exchange_embedded(embed, slots, block_states, accept):
+    vocab, wide = embed.shape
+    piece = vocab // 4
+    strip = piece // 7
+
+    def body(ins, outs, scr):
+        table_ref, slot_ref, old_ref, acc_ref = ins
+        (new_ref,) = outs
+        raw, table, stage, parts, came, send, recv, loc = scr
+        z, xl, xh, y, c = coords()
+        t = z * 2 + xl
+        links = Links(send, recv)
+        loads = [
+            pltpu.make_async_copy(table_ref.at[pl.ds(k * piece, piece)], raw.at[k], loc.at[k])
+            for k in range(4)
+        ]
+        for cp in loads:
+            cp.start()
+        table[pl.ds(vocab, 8), :] = jnp.zeros((8, wide), F32)
+        for k in range(4):
+            loads[k].wait()
+
+            def widen(j, carry, k=k):
+                at = pl.multiple_of(j * strip, strip)
+                to = pl.multiple_of(k * piece + j * strip, strip)
+                table[pl.ds(to, strip), :] = raw[k, pl.ds(at, strip), :].astype(F32)
+                return carry
+
+            lax.fori_loop(0, 7, widen, 0)
+        yield 0
+
+        def look_up(owner):
+            def rows(j, carry):
+                for k in range(16):
+                    n = j * 16 + k
+                    stage[pl.ds(n, 1), :] = table[pl.ds(slot_ref[owner * 256 + n], 1), :]
+                return carry
+
+            lax.fori_loop(0, 16, rows, 0)
+            parts[owner] = stage[...].astype(BF)
+
+        cps, sources = [], []
+        for dx, dz in REL8:
+            z_, xl_ = ring(z, dz), lax.rem(xl + dx, 2)
+            look_up(z_ * 2 + xl_)
+            cps.append(
+                links.copy(parts.at[z_ * 2 + xl_], came.at[t], place(z_, xl_, xh, y, c))
+            )
+            sources.append(z_ * 2 + xl_)
+        look_up(t)
+        yield 0
+        yield 0
+        yield 0
+        yield 0
+        total = parts[t].astype(F32)
+        for cp in cps:
+            cp.wait()
+        for source in sources:
+            total = total + came[source].astype(F32)
+        new_ref[...] = jnp.where(acc_ref[...] == 1, total, old_ref[...].astype(F32)).astype(BF)
+
+    return Task(
+        body,
+        [
+            (embed, ANY),
+            (slots, pl.BlockSpec(memory_space=pltpu.SMEM)),
+            (block_states, VM),
+            (accept, VM),
+        ],
+        [(jax.ShapeDtypeStruct(block_states.shape, BF), VM)],
+        [
+            pltpu.VMEM((4, piece, wide), BF),
+            pltpu.VMEM((vocab + 8, wide), F32),
+            pltpu.VMEM((256, wide), F32),
+            pltpu.VMEM((8, 256, wide), BF),
+            pltpu.VMEM((8, 256, wide), BF),
+        ],
+        7,
+        4,
+        TOK_ALL,
+    )
+
+
 def unit_rows(v):
     return v * lax.rsqrt(jnp.mean(v * v, axis=-1, keepdims=True) + EPSILON)
 
@@ -486,14 +569,7 @@
                 four[i + 1] = relay(i + 1, three[i + 1])
             if i + 2 < n:
                 three[i + 2] = spread(i + 2, 2, two[i + 2])
-            for pair in four[i]:
-                for cp in pair:
-                    cp.wait_recv()
-            if i == 0:
-                for cp in loads:
-                    cp.wait()
-            if i == n - 1:
-                maxima[0] = sq_ref[...]
+            if i == n - 2:
                 swap.wait()
                 for dy in (2, 1, 3, 0):
                     y_ = ring(y, dy)
@@ -506,6 +582,14 @@
                                 theirs.at[:, y_], came.at[:, y], place(z, xl, xh, y_, c)
                             )
                         )
+            for pair in four[i]:
+                for cp in pair:
+                    cp.wait_recv()
+            if i == 0:
+                for cp in loads:
+                    cp.wait()
+            if i == n - 1:
+                maxima[0] = sq_ref[...]
             multiply(i)
         top = lax.broadcasted_iota(jnp.int32, (8, 256), 0) < 4
 
@@ -535,9 +619,19 @@
         other = deep[3]
         for k in range(4, 7):
             other = join(other, deep[k])
-        top_ref[c] = mine
-        top_ref[1 - c] = other
-        sum_ref[...] = mine + other
+        even = jnp.where(c == 0, mine, other)
+        odd = jnp.where(c == 0, other, mine)
+        group = lax.broadcasted_iota(jnp.int32, (8, 128), 1) // 16
+        for q in range(4):
+            row = jnp.zeros((8, 128), F32)
+            for a in range(4):
+                for k, v in enumerate((even, odd)):
+                    half = v[:, q // 2 * 128 : q // 2 * 128 + 128]
+                    turn = (a * 16 + k * 16 - q % 2 * 64) % 128
+                    turned = pltpu.roll(half, turn, 1) if turn else half
+                    row = jnp.where(group == 2 * a + k, turned, row)
+            top_ref[:, q * 128 : q * 128 + 128] = row[:4]
+        sum_ref[...] = jnp.sqrt((mine + other) * (1.0 / (256 * 4096)))
         over_x.wait_recv()
         total = theirs[xh, y].astype(F32) + far[...].astype(F32)
         hid_ref[...] = layer_end(x_ref[...], total, again_ref[...])
@@ -564,7 +658,7 @@
         [(normed, VM), (squares, VM), (states_in, VM), (attn_gain, VM)]
         + [(a, ANY) for a in (own_head, other_head) + second],
         [
-            (jax.ShapeDtypeStruct((2, 8, 256), F32), VM),
+            (jax.ShapeDtypeStruct((4, 512), F32), VM),
             (jax.ShapeDtypeStruct((8, 256), F32), VM),
             (jax.ShapeDtypeStruct((16, 4096), BF), VM),
         ],
@@ -742,21 +836,18 @@
     vocab_here = embed.shape[0]
     local_ids = token_ids - tok * vocab_here
     inside = (local_ids >= 0) & (local_ids < vocab_here)
-    looked_up = jnp.take(embed, jnp.clip(local_ids, 0, vocab_here - 1), axis=0)
-    looked_up = jnp.where(inside[:, None], looked_up, jnp.zeros_like(looked_up))
+    slots = jnp.where(inside, local_ids, vocab_here)
 
     weights = (w_query, w_key, w_value)
-    (rows1, q1, k1, v1), (came,) = comm(
+    (rows1, q1, k1, v1), (swapped,) = comm(
         [
             gather_project(block_states, weights),
-            exchange_tok(looked_up.reshape(8, 256, 256)),
+            exchange_embedded(embed, slots, block_states, accept.reshape(-1, 1)),
         ],
         0,
         "comm_a",
         60,
     )
-    embedded = jnp.sum(came.astype(F32), axis=0).astype(BF)
-    swapped = jnp.where((accept == 1)[:, None], embedded, block_states)
 
     (qs1,), (rows2, q2, k2, v2) = comm(
         [gather_queries(q1), gather_project(swapped, weights)], 1, "comm_b", 60
@@ -778,11 +869,9 @@
         [gather_logits(normed, squares, lm_head, other_head, second, rows2, attn_gain)],
         4,
         "comm_e",
-        56,
-    )
-    top_logits = top[:, :4].reshape(2, 64, 16).transpose(1, 0, 2).reshape(-1)
-    request_norms = jnp.sqrt(sums[4, :8] / (256 * 4096))
-    return (hiddens, request_norms, top_logits)
+        52,
+    )
+    return (hiddens, sums[4, :8], top.reshape(-1))
 
 
 def solution(mesh):

time: 214 us -> 190 us (0.89)
  local copies, waits for them, and re-layouts: 17.6 us -> 4.53 us
  Pallas kernels: 186 us -> 180 us
  other arithmetic: 7.12 us -> 2.14 us
    gather x1 -> x0, local copies, waits for them, and re-layouts: 10.3 us -> none  [shards(): looked_up = jnp.take(embed, jnp.clip(local_ids, 0, vocab_here - 1), axis=0)]
    pallas_call x5, Pallas kernels: 168 us -> 162 us  [comm(): pl.pallas_call(kernel, out_shape=[o[0] for t in tasks for o in t.outs], i...]
    unnamed x37 -> x32, local copies, waits for them, and re-layouts: 5.67 us -> 2.54 us
  transfers between devices with their start and end apart: 1 -> 1, of which waited for: 0 -> 0; matrix products, arithmetic and copies ran while one was open for 8% -> 2% of each run, Pallas kernels for 57% -> 64%
where the time goes in v6:
time: 190 us; the launch traced here: 189 us
  Pallas kernels  180 us (95%)
  local copies, waits for them, and re-layouts  4.53 us (2%)
  other arithmetic  2.14 us (1%)
    pallas_call x5, Pallas kernels, comm(): pl.pallas_call(kernel, out_shape=[o[0] for t in tasks for o in t.outs], i...  162 us
    pallas_call x2, Pallas kernels, cached_attention(): pl.pallas_call(kernel, in_specs=[smem, smem, VM, VM, VM], out_specs=[VM,...  13.5 us
    pallas_call x1, Pallas kernels, combine(): pl.pallas_call(kernel, grid=(steps,), in_specs=[whole(a) for a in (parts,...  5.09 us
  transfers between devices with their start and end apart: 1, of which 0 were waited for; matrix products, arithmetic and copies ran while one was open for 2% of the time, Pallas kernels for 64%

profile of v6, /device:TPU:1, one launch (start us, length us, event | category | flops | bytes accessed | tf_op | source)
XLA Modules:
  0.0 189.4 jit_solution(11420866826563281898)
XLA Ops:
  0.6 1.5 collective-permute-start
  2.1 1.5 copy.17.refs_7_
  3.6 0.8 reduce-window.9
  4.4 1.3 and_select_fusion.refs_5_
  5.7 29.1 %comm_a.1 = (bf16[16,4096]{1,0:T(8,128)(2,1)}, bf16[256,256]{1,0:T(8,128)(2,1)}, bf16[256,256]{1,0:T(8,128)(2,1)}, bf16[256,256]{1,0:T(8,128)(2,1)}, bf16[256,256]{1,0:T(8,128)(2,1)}) custom-call(bf16[256,256]{1,0:T(8,128)(2,1)} %refs_6_.1, bf16[4096,256]{1,0:T(8,128)(2,1)} %refs_2_.3, bf16[4096,256]{1,0:T(8,128)(2,1)} %refs_3_.3, ...), custom_call_target="tpu_custom_call" | custom-call | tf_op jit(solution)/shard_map/comm_a/pallas_call | solution.py:116
  34.8 0.0 copy-start.14
  34.8 0.0 copy-start.1
  34.8 0.0 copy-start.2
  34.8 21.3 %comm_b.1 = (bf16[8,256,256]{2,1,0:T(8,128)(2,1)}, bf16[16,4096]{1,0:T(8,128)(2,1)}, bf16[256,256]{1,0:T(8,128)(2,1)}, bf16[256,256]{1,0:T(8,128)(2,1)}, bf16[256,256]{1,0:T(8,128)(2,1)}) custom-call(bf16[256,256]{1,0:T(8,128)(2,1)} %get-tuple-element.27.refs_0_.q_ref, bf16[256,256]{1,0:T(8,128)(2,1)} %get-tuple-element.28.refs_1_, ...), custom_call_target="tpu_custom_call" | custom-call | tf_op jit(solution)/shard_map/comm_b/pallas_call | solution.py:116
  56.1 0.0 copy-done.14
  56.1 0.0 copy-done.1
  56.2 0.0 copy-done.2
  56.2 0.0 copy-start.3
  56.2 1.2 copy-done.3
  57.4 0.0 copy-start.4
  57.4 6.7 %cached.2 = (bf16[8,256,256]{2,1,0:T(8,128)(2,1)S(1)}, f32[8,8,256]{2,1,0:T(8,128)S(1)}) custom-call(s32[8]{0:T(128)S(1)} %get-tuple-element.52.lo_ref, s32[8]{0:T(128)S(1)} %get-tuple-element.51.hi_ref, bf16[8,256,256]{2,1,0:T(8,128)(2,1)S(1)} %copy-done.3, bf16[1024,256]{1,0:T(8,128)(2,1)S(1)} %copy-done.1, bf16[1024,256]{1,0:T(8,128)(2,1)S(1)} %copy-done.2), custom_call_target="tpu_custom_call" | custom-call | tf_op jit(solution)/shard_map/cached/pallas_call | solution.py:746
  64.1 0.0 copy-start
  64.1 0.0 copy-start.5
  64.2 0.0 copy-start.10
  64.2 0.0 copy-start.11
  64.2 0.0 copy-done.4
  64.2 27.2 %comm_c.1 = (bf16[8,256,256]{2,1,0:T(8,128)(2,1)S(1)}, f32[8,8,256]{2,1,0:T(8,128)S(1)}, bf16[8,256,256]{2,1,0:T(8,128)(2,1)S(1)}) custom-call(bf16[8,256,256]{2,1,0:T(8,128)(2,1)S(1)} %get-tuple-element.30.refs_0_, f32[8,8,256]{2,1,0:T(8,128)S(1)} %get-tuple-element.31.refs_1_, bf16[256,256]{1,0:T(8,128)(2,1)S(1)} %copy-done.4), custom_call_target="tpu_custom_call" | custom-call | tf_op jit(solution)/shard_map/comm_c/pallas_call | solution.py:116
  91.4 6.7 %cached.3 = (bf16[8,256,256]{2,1,0:T(8,128)(2,1)S(1)}, f32[8,8,256]{2,1,0:T(8,128)S(1)}) custom-call(s32[8]{0:T(128)S(1)} %get-tuple-element.52.lo_ref, s32[8]{0:T(128)S(1)} %get-tuple-element.51.hi_ref, bf16[8,256,256]{2,1,0:T(8,128)(2,1)S(1)} %get-tuple-element.38.q_ref, bf16[1024,256]{1,0:T(8,128)(2,1)S(1)} %copy-done.1, bf16[1024,256]{1,0:T(8,128)(2,1)S(1)} %copy-done.2), custom_call_target="tpu_custom_call" | custom-call | tf_op jit(solution)/shard_map/cached/pallas_call | solution.py:746
  98.2 0.0 copy-done
  98.2 0.0 copy-done.5
  98.2 0.0 copy-done.10
  98.2 0.0 copy-done.11
  98.2 0.0 copy-start.9
  98.2 0.0 copy-start.12
  98.2 0.0 copy-start.13
  98.2 5.1 %combine.1.refs_0_ = bf16[2,4,2,16,4096]{4,3,2,1,0:T(8,128)(2,1)S(1)} custom-call(bf16[8,256,256]{2,1,0:T(8,128)(2,1)S(1)} %get-tuple-element.33.p_ref, f32[8,8,256]{2,1,0:T(8,128)S(1)} %get-tuple-element.34.s_ref, bf16[256,256]{1,0:T(8,128)(2,1)S(1)} %copy-done.5, bf16[256,256]{1,0:T(8,128)(2,1)S(1)} %copy-done.10, bf16[256,256]{1,0:T(8,128)(2,1)S(1)} %copy-done.11, ...), custom_call_target="tpu_custom_call" | custom-call | tf_op jit(solution)/shard_map/combine/pallas_call | solution.py:798
  103.3 0.0 copy-start.6
  103.4 0.0 copy-start.7
  103.4 0.0 copy-start.8
  103.4 0.0 copy-done.9
  103.4 0.0 copy-done.12
  103.4 0.0 copy-done.13
  103.4 25.0 %comm_d.1 = (bf16[16,4096]{1,0:T(8,128)(2,1)S(1)}, f32[8,256]{1,0:T(8,128)S(1)}, bf16[8,256,256]{2,1,0:T(8,128)(2,1)S(1)}, f32[8,8,256]{2,1,0:T(8,128)S(1)}) custom-call(bf16[2,4,2,16,4096]{4,3,2,1,0:T(8,128)(2,1)S(1)} %combine.1.refs_0_, bf16[16,4096]{1,0:T(8,128)(2,1)S(1)} %copy-done.9, f32[1,4096]{1,0:T(1,128)S(1)} %bitcast.16, f32[1,4096]{1,0:T(1,128)S(1)} %bitcast.18, ...), custom_call_target="tpu_custom_call" | custom-call | tf_op jit(solution)/shard_map/comm_d/pallas_call | solution.py:116
  128.4 0.0 collective-permute-done.refs_5_
  128.4 0.0 copy-done.6
  128.5 0.0 copy-done.7
  128.5 0.0 copy-done.8
  128.5 59.2 %comm_e.1 = (f32[4,512]{1,0:T(4,128)S(1)}, f32[8,256]{1,0:T(8,128)S(1)}, bf16[16,4096]{1,0:T(8,128)(2,1)S(1)}) custom-call(bf16[16,4096]{1,0:T(8,128)(2,1)S(1)} %get-tuple-element.41.refs_0_, f32[8,256]{1,0:T(8,128)S(1)} %get-tuple-element.42.refs_1_, bf16[16,4096]{1,0:T(8,128)(2,1)S(1)} %copy-done.6, f32[1,4096]{1,0:T(1,128)S(1)} %bitcast.17, ...), custom_call_target="tpu_custom_call" | custom-call | tf_op jit(solution)/shard_map/comm_e/pallas_call | solution.py:116
  187.7 0.5 slice_bitcast_fusion
  188.2 0.6 copy.18
  188.8 0.7 copy.20
  (1 shorter events, 0.0 us)
Async XLA Ops:
  0.6 127.8 %collective-permute-start = (bf16[784,4096]{1,0:T(8,128)(2,1)}, bf16[784,4096]{1,0:T(8,128)(2,1)}, u32[]{:S(2)}, u32[]{:S(2)}) collective-permute-start(bf16[784,4096]{1,0:T(8,128)(2,1)} %refs_4_.5), channel_id=1, source_target_pairs={{0,1},{1,0},{2,3},{3,2},{4,5},{5,4},{6,7},{7,6},{8,9},{9,8},{10,11... | collective-permute-start | bytes 19267592 | tf_op jit(solution)/shard_map/ppermute | solution.py:828
  34.8 21.3 %copy-start.14 = (s32[8]{0:T(128)S(1)}, s32[8]{0:T(128)}, u32[]{:S(2)}) copy-start(s32[8]{0:T(128)} %param.17) | copy-start | bytes 100
  34.8 21.3 %copy-start.1 = (bf16[1024,256]{1,0:T(8,128)(2,1)S(1)}, bf16[1024,256]{1,0:T(8,128)(2,1)}, u32[]{:S(2)}) copy-start(bf16[1024,256]{1,0:T(8,128)(2,1)} %k_ref.3) | copy-start | bytes 1572868
  34.8 21.3 %copy-start.2 = (bf16[1024,256]{1,0:T(8,128)(2,1)S(1)}, bf16[1024,256]{1,0:T(8,128)(2,1)}, u32[]{:S(2)}) copy-start(bf16[1024,256]{1,0:T(8,128)(2,1)} %v_ref.3) | copy-start | bytes 1572868
  56.2 1.2 copy-start.3
  57.4 6.8 %copy-start.4 = (bf16[256,256]{1,0:T(8,128)(2,1)S(1)}, bf16[256,256]{1,0:T(8,128)(2,1)}, u32[]{:S(2)}) copy-start(bf16[256,256]{1,0:T(8,128)(2,1)} %get-tuple-element.32.refs_2_.refs_8_) | copy-start | bytes 393220
  64.1 34.0 %copy-start = (bf16[256,4096]{1,0:T(8,128)(2,1)S(1)}, bf16[256,4096]{1,0:T(8,128)(2,1)}, u32[]{:S(2)}) copy-start(bf16[256,4096]{1,0:T(8,128)(2,1)} %refs_11_.1) | copy-start | bytes 6291460
  64.1 34.0 %copy-start.5 = (bf16[256,256]{1,0:T(8,128)(2,1)S(1)}, bf16[256,256]{1,0:T(8,128)(2,1)}, u32[]{:S(2)}) copy-start(bf16[256,256]{1,0:T(8,128)(2,1)} %get-tuple-element.27.refs_0_.q_ref) | copy-start | bytes 393220
  64.2 34.0 %copy-start.10 = (bf16[256,256]{1,0:T(8,128)(2,1)S(1)}, bf16[256,256]{1,0:T(8,128)(2,1)}, u32[]{:S(2)}) copy-start(bf16[256,256]{1,0:T(8,128)(2,1)} %get-tuple-element.35.k_ref) | copy-start | bytes 393220
  64.2 34.0 %copy-start.11 = (bf16[256,256]{1,0:T(8,128)(2,1)S(1)}, bf16[256,256]{1,0:T(8,128)(2,1)}, u32[]{:S(2)}) copy-start(bf16[256,256]{1,0:T(8,128)(2,1)} %get-tuple-element.36.v_ref) | copy-start | bytes 393220
  98.2 5.2 %copy-start.9 = (bf16[16,4096]{1,0:T(8,128)(2,1)S(1)}, bf16[16,4096]{1,0:T(8,128)(2,1)}, u32[]{:S(2)}) copy-start(bf16[16,4096]{1,0:T(8,128)(2,1)} %get-tuple-element.37.refs_1_) | copy-start | bytes 393220
  98.2 5.2 %copy-start.12 = (f32[4096]{0:T(1024)S(1)}, f32[4096]{0:T(1024)}, u32[]{:S(2)}) copy-start(f32[4096]{0:T(1024)} %param.24) | copy-start | bytes 49156
  98.2 5.2 %copy-start.13 = (f32[4096]{0:T(1024)S(1)}, f32[4096]{0:T(1024)}, u32[]{:S(2)}) copy-start(f32[4096]{0:T(1024)} %param.25) | copy-start | bytes 49156
  103.3 25.1 %copy-start.6 = (bf16[16,4096]{1,0:T(8,128)(2,1)S(1)}, bf16[16,4096]{1,0:T(8,128)(2,1)}, u32[]{:S(2)}) copy-start(bf16[16,4096]{1,0:T(8,128)(2,1)} %get-tuple-element.43.refs_2_) | copy-start | bytes 393220
  103.4 25.1 %copy-start.7 = (bf16[256,256]{1,0:T(8,128)(2,1)S(1)}, bf16[256,256]{1,0:T(8,128)(2,1)}, u32[]{:S(2)}) copy-start(bf16[256,256]{1,0:T(8,128)(2,1)} %get-tuple-element.46.refs_9_) | copy-start | bytes 393220
  103.4 25.1 %copy-start.8 = (bf16[256,256]{1,0:T(8,128)(2,1)S(1)}, bf16[256,256]{1,0:T(8,128)(2,1)}, u32[]{:S(2)}) copy-start(bf16[256,256]{1,0:T(8,128)(2,1)} %get-tuple-element.47.refs_10_) | copy-start | bytes 393220

commit v7 on v5

--- a/solution.py
+++ b/solution.py
@@ -131,117 +131,97 @@
     return res
 
 
-def gather_project(x, weights):
-    rows, wide = x.shape
-
-    def body(ins, outs, scr):
-        x_ref, w_refs = ins[0], ins[1:]
-        own_rows, outs = outs[0], outs[1:]
-        f_ref, w_ref, acc, send, recv, loc = scr
-        z, xl, xh, y, c = coords()
-        links = Links(send, recv)
-
-        def index(xh_, y_, c_):
-            return xh_ * 8 + y_ * 2 + c_
-
-        def slot(*at):
-            return f_ref.at[index(*at)]
-
-        def absorb(*at):
-            k = index(*at)
-            v = f_ref[k]
-            for n in range(3):
-                w = w_ref[n, pl.ds(pl.multiple_of(k * wide, wide), wide), :]
-                acc[n] += jnp.dot(v, w, preferred_element_type=F32)
-
-        core = place(z, xl, xh, y, 1 - c)
-        own = slot(xh, y, c)
-        keep = pltpu.make_async_copy(x_ref, own, loc.at[0])
-        keep.start()
-        landed = []
-        over_x = links.copy(x_ref, own, place(z, xl, 1 - xh, y, c))
-        over_y = {d: links.copy(x_ref, own, place(z, xl, xh, ring(y, d), c)) for d in (2, 1, 3)}
-        landed.append(links.copy(x_ref, own, core))
-        loads = [pltpu.make_async_copy(w_refs[n], w_ref.at[n], loc.at[1 + n]) for n in range(3)]
-        for cp in loads:
-            cp.start()
-        acc[...] = jnp.zeros_like(acc)
+def project_steps(links, keep_sem, x_ref, f_ref, w_ref, acc, loads, own_rows, outs):
+    wide = x_ref.shape[1]
+    z, xl, xh, y, c = coords()
+
+    def index(xh_, y_, c_):
+        return xh_ * 8 + y_ * 2 + c_
+
+    def slot(*at):
+        return f_ref.at[index(*at)]
+
+    def absorb(*at):
+        k = index(*at)
+        v = f_ref[k]
+        for n in range(3):
+            w = w_ref[n, pl.ds(pl.multiple_of(k * wide, wide), wide), :]
+            acc[n] += jnp.dot(v, w, preferred_element_type=F32)
+
+    core = place(z, xl, xh, y, 1 - c)
+    own = slot(xh, y, c)
+    keep = pltpu.make_async_copy(x_ref, own, keep_sem)
+    keep.start()
+    landed = []
+    over_x = links.copy(x_ref, own, place(z, xl, 1 - xh, y, c))
+    over_y = {d: links.copy(x_ref, own, place(z, xl, xh, ring(y, d), c)) for d in (2, 1, 3)}
+    landed.append(links.copy(x_ref, own, core))
+    acc[...] = jnp.zeros_like(acc)
+    yield 0
+    over_x.wait_recv()
+    far = slot(1 - xh, y, c)
+    far_y = {d: links.copy(far, far, place(z, xl, xh, ring(y, d), c)) for d in (2, 1, 3)}
+    landed.append(links.copy(far, far, core))
+    yield 0
+    keep.wait()
+    for cp in loads:
+        cp.wait()
+    absorb(xh, y, c)
+    absorb(1 - xh, y, c)
+    for k, xh_ in enumerate((xh, 1 - xh)):
+        landed[k].wait_recv()
+        absorb(xh_, y, 1 - c)
+    yield 0
+    for xh_, arrive in ((xh, over_y), (1 - xh, far_y)):
+        for d in (1, 3, 2):
+            y_ = ring(y, 4 - d)
+            arrive[d].wait_recv()
+            got = slot(xh_, y_, c)
+            landed.append(links.copy(got, got, core))
+            absorb(xh_, y_, c)
+        for k, d in enumerate((1, 3, 2)):
+            landed[k - 3].wait_recv()
+            absorb(xh_, ring(y, 4 - d), 1 - c)
         yield 0
-        over_x.wait_recv()
-        far = slot(1 - xh, y, c)
-        far_y = {d: links.copy(far, far, place(z, xl, xh, ring(y, d), c)) for d in (2, 1, 3)}
-        landed.append(links.copy(far, far, core))
-        yield 0
-        keep.wait()
-        for cp in loads:
-            cp.wait()
-        absorb(xh, y, c)
-        absorb(1 - xh, y, c)
-        for k, xh_ in enumerate((xh, 1 - xh)):
-            landed[k].wait_recv()
-            absorb(xh_, y, 1 - c)
-        yield 0
-        for xh_, arrive in ((xh, over_y), (1 - xh, far_y)):
-            for d in (1, 3, 2):
-                y_ = ring(y, 4 - d)
-                arrive[d].wait_recv()
-                got = slot(xh_, y_, c)
-                landed.append(links.copy(got, got, core))
-                absorb(xh_, y_, c)
-            for k, d in enumerate((1, 3, 2)):
-                landed[k - 3].wait_recv()
-                absorb(xh_, ring(y, 4 - d), 1 - c)
-            yield 0
-        h = pl.multiple_of(index(xh, y, c) * 16, 16)
-        for k in range(16):
-            own_rows[:, k * wide : (k + 1) * wide] = f_ref[k, pl.ds(h, 16), :]
-        for n in range(3):
-            outs[n][...] = acc[n].astype(BF)
-        for cp in [over_x] + list(over_y.values()) + list(far_y.values()) + landed:
-            cp.wait_send()
-
-    return Task(
-        body,
-        [(x, ANY)] + [(w, ANY) for w in weights],
-        [(jax.ShapeDtypeStruct((16, 16 * wide), BF), VM)]
-        + [(jax.ShapeDtypeStruct((rows, wide), BF), VM)] * 3,
-        [
-            pltpu.VMEM((16, rows, wide), BF),
-            pltpu.VMEM((3, 16 * wide, wide), BF),
-            pltpu.VMEM((3, rows, wide), F32),
-        ],
-        15,
-        4,
-        HEAD_AG,
-    )
+    h = pl.multiple_of(index(xh, y, c) * 16, 16)
+    for k in range(16):
+        own_rows[:, k * wide : (k + 1) * wide] = f_ref[k, pl.ds(h, 16), :]
+    for n in range(3):
+        outs[n][...] = acc[n].astype(BF)
+    yield 0
+    for cp in [over_x] + list(over_y.values()) + list(far_y.values()) + landed:
+        cp.wait_send()
+
+
+def query_steps(links, keep_sem, q_ref, o_ref):
+    z, xl, xh, y, c = coords()
+    own = o_ref.at[z * 2 + xl]
+    keep = pltpu.make_async_copy(q_ref, own, keep_sem)
+    keep.start()
+    side = place(z, 1 - xl, xh, y, c)
+    over_x = [links.copy(q_ref, own, side)]
+    over_z = {d: links.copy(q_ref, own, place(ring(z, d), xl, xh, y, c)) for d in (2, 1, 3)}
+    yield 0
+    over_x[0].wait_recv()
+    far = o_ref.at[z * 2 + 1 - xl, pl.ds(0, 128)]
+    more = [links.copy(far, far, place(ring(z, d), xl, xh, y, c)) for d in (2, 1, 3)]
+    yield 0
+    for d in (1, 3, 2):
+        over_z[d].wait_recv()
+        got = o_ref.at[ring(z, 4 - d) * 2 + xl, pl.ds(128, 128)]
+        over_x.append(links.copy(got, got, side))
+    yield 0
+    for cp in over_x[1:] + more:
+        cp.wait_recv()
+    for cp in over_x + more + list(over_z.values()):
+        cp.wait_send()
+    keep.wait()
 
 
 def gather_queries(q):
     def body(ins, outs, scr):
-        (q_ref,), (o_ref,), (send, recv, loc) = ins, outs, scr
-        z, xl, xh, y, c = coords()
-        links = Links(send, recv)
-        own = o_ref.at[z * 2 + xl]
-        keep = pltpu.make_async_copy(q_ref, own, loc.at[0])
-        keep.start()
-        side = place(z, 1 - xl, xh, y, c)
-        over_x = [links.copy(q_ref, own, side)]
-        over_z = {d: links.copy(q_ref, own, place(ring(z, d), xl, xh, y, c)) for d in (2, 1, 3)}
-        yield 0
-        over_x[0].wait_recv()
-        far = o_ref.at[z * 2 + 1 - xl, pl.ds(0, 128)]
-        more = [links.copy(far, far, place(ring(z, d), xl, xh, y, c)) for d in (2, 1, 3)]
-        yield 0
-        for d in (1, 3, 2):
-            over_z[d].wait_recv()
-            got = o_ref.at[ring(z, 4 - d) * 2 + xl, pl.ds(128, 128)]
-            over_x.append(links.copy(got, got, side))
-        yield 0
-        for cp in over_x[1:] + more:
-            cp.wait_recv()
-        for cp in over_x + more + list(over_z.values()):
-            cp.wait_send()
-        keep.wait()
+        send, recv, loc = scr
+        yield from query_steps(Links(send, recv), loc.at[0], ins[0], outs[0])
 
     return Task(
         body, [(q, ANY)], [(jax.ShapeDtypeStruct((8, 256, 256), BF), ANY)], [], 10, 1, TOK_AG
@@ -280,6 +260,133 @@
     )
 
 
+def embed_steps(links, sems, table_ref, slot_ref, old_ref, acc_ref, new_ref, scr):
+    raw, table, stage, parts, came = scr
+    vocab, wide = table_ref.shape
+    piece = vocab // 4
+    strip = piece // 7
+    z, xl, xh, y, c = coords()
+    t = z * 2 + xl
+    loads = [
+        pltpu.make_async_copy(table_ref.at[pl.ds(k * piece, piece)], raw.at[k], sems.at[k])
+        for k in range(4)
+    ]
+    for cp in loads:
+        cp.start()
+    table[pl.ds(vocab, 8), :] = jnp.zeros((8, wide), F32)
+    for k in range(4):
+        loads[k].wait()
+
+        def widen(j, carry, k=k):
+            at = pl.multiple_of(j * strip, strip)
+            to = pl.multiple_of(k * piece + j * strip, strip)
+            table[pl.ds(to, strip), :] = raw[k, pl.ds(at, strip), :].astype(F32)
+            return carry
+
+        lax.fori_loop(0, 7, widen, 0)
+    yield 0
+
+    def look_up(owner):
+        def rows(j, carry):
+            for k in range(16):
+                n = j * 16 + k
+                stage[pl.ds(n, 1), :] = table[pl.ds(slot_ref[owner * 256 + n], 1), :]
+            return carry
+
+        lax.fori_loop(0, 16, rows, 0)
+        parts[owner] = stage[...].astype(BF)
+
+    cps, sources = [], []
+    for dx, dz in REL8:
+        z_, xl_ = ring(z, dz), lax.rem(xl + dx, 2)
+        look_up(z_ * 2 + xl_)
+        cps.append(links.copy(parts.at[z_ * 2 + xl_], came.at[t], place(z_, xl_, xh, y, c)))
+        sources.append(z_ * 2 + xl_)
+    look_up(t)
+    yield 0
+    total = parts[t].astype(F32)
+    for cp in cps:
+        cp.wait()
+    for source in sources:
+        total = total + came[source].astype(F32)
+    new_ref[...] = jnp.where(acc_ref[...] == 1, total, old_ref[...].astype(F32)).astype(BF)
+
+
+def front(block_states, weights, embed, slots, accept):
+    rows, wide = block_states.shape
+    vocab = embed.shape[0]
+
+    def body(ins, outs, scr):
+        x_ref, w_refs, table_ref, slot_ref, old_ref, acc_ref = (
+            ins[0],
+            ins[1:4],
+            ins[4],
+            ins[5],
+            ins[6],
+            ins[7],
+        )
+        rows1, q1, k1, v1, qs1, rows2, q2, k2, v2 = outs
+        f1, f2, w_ref, acc, swapped = scr[:5]
+        send, recv, loc = scr[10:]
+        links = Links(send, recv)
+        loads = [pltpu.make_async_copy(w_refs[n], w_ref.at[n], loc.at[n]) for n in range(3)]
+        one = project_steps(
+            links, loc.at[3], x_ref, f1, w_ref, acc, loads, rows1, (q1, k1, v1)
+        )
+        swap = embed_steps(
+            links, loc.at[pl.ds(6, 4)], table_ref, slot_ref, old_ref, acc_ref, swapped, scr[5:10]
+        )
+        next(one)
+        next(swap)
+        for cp in loads:
+            cp.start()
+        next(one)
+        next(swap)
+        for _ in range(4):
+            next(one)
+        ask = query_steps(links, loc.at[4], q1, qs1)
+        next(ask)
+        next(swap, None)
+        two = project_steps(links, loc.at[5], swapped, f2, w_ref, acc, [], rows2, (q2, k2, v2))
+        next(two)
+        next(ask)
+        next(two)
+        next(ask)
+        for _ in range(4):
+            next(two)
+        for left in (one, ask, two):
+            next(left, None)
+        yield 0
+
+    def out(*shape):
+        return jax.ShapeDtypeStruct(shape, BF)
+
+    half = [(out(16, 16 * wide), VM)] + [(out(rows, wide), VM)] * 3
+    return Task(
+        body,
+        [(block_states, ANY)]
+        + [(w, ANY) for w in weights]
+        + [(embed, ANY), (slots, pl.BlockSpec(memory_space=pltpu.SMEM))]
+        + [(block_states, VM), (accept, VM)],
+        half + [(out(8, rows, wide), ANY)] + half,
+        [
+            pltpu.VMEM((16, rows, wide), BF),
+            pltpu.VMEM((16, rows, wide), BF),
+            pltpu.VMEM((3, 16 * wide, wide), BF),
+            pltpu.VMEM((3, rows, wide), F32),
+            pltpu.VMEM((rows, wide), BF),
+            pltpu.VMEM((4, vocab // 4, wide), BF),
+            pltpu.VMEM((vocab + 8, wide), F32),
+            pltpu.VMEM((rows, wide), F32),
+            pltpu.VMEM((8, rows, wide), BF),
+            pltpu.VMEM((8, rows, wide), BF),
+        ],
+        15 + 7 + 10 + 15,
+        10,
+        HEAD_AG + TOK_ALL,
+    )
+
+
 def unit_rows(v):
     return v * lax.rsqrt(jnp.mean(v * v, axis=-1, keepdims=True) + EPSILON)
 
@@ -288,60 +395,97 @@
     return (before.astype(F32) + unit_rows(total) * gain).astype(BF)
 
 
-def reduce_layer(part, states_in, attn_gain, final_gain):
+def end_first(first, states_in, attn_gain, final_gain):
+    chunks = 4
+
     def body(ins, outs, scr):
-        part_ref, x_ref, again_ref, fgain_ref = ins
-        mine, theirs, came, far, send, recv, loc = scr
+        x_ref, again_ref, fgain_ref = ins[6:]
+        held = scr[:6]
+        att, out, theirs, came, far, total, send, recv, loc = scr[6:]
         z, xl, xh, y, c = coords()
         links = Links(send, recv)
-        cps = []
-        l0 = pltpu.make_async_copy(part_ref.at[:, :, c], mine, loc.at[0])
-        l0.start()
-        swap = links.copy(part_ref.at[:, :, 1 - c], theirs, place(z, xl, xh, y, 1 - c))
-        yield 0
-        l0.wait()
-        swap.wait_recv()
-
-        def both(xh_, y_):
-            return mine[xh_, y_].astype(F32) + theirs[xh_, y_].astype(F32)
-
-        for dy in (2, 1, 3):
-            y_ = ring(y, dy)
-            for xh_ in (0, 1):
-                mine[xh_, y_] = both(xh_, y_).astype(BF)
-            cps.append(links.copy(mine.at[:, y_], came.at[:, y], place(z, xl, xh, y_, c)))
-        total, away = both(xh, y), both(1 - xh, y)
-        yield 0
-        for cp in cps:
+        cuts = [pl.ds(k * 1024, 1024) for k in range(chunks)]
+        fetch = [
+            pltpu.make_async_copy(src, dst, loc.at[k])
+            for k, (src, dst) in enumerate(zip(ins[:6], held))
+        ]
+        for cp in fetch:
+            cp.start()
+        for cp in fetch:
+            cp.wait()
+        attend(*held[:5], att)
+        core = place(z, xl, xh, y, 1 - c)
+        swaps, over_y, over_x = [], [], []
+        for cut in cuts:
+            o = jnp.dot(att[...], held[5][:, cut], preferred_element_type=F32).astype(BF)
+            out[:, :, :, :, cut] = o.reshape(2, 4, 2, 16, 1024)
+            swaps.append(
+                links.copy(out.at[:, :, 1 - c, :, cut], theirs.at[:, :, :, cut], core)
+            )
+
+        def both(xh_, y_, cut):
+            return out[xh_, y_, c, :, cut].astype(F32) + theirs[xh_, y_, :, cut].astype(F32)
+
+        for k, cut in enumerate(cuts):
+            swaps[k].wait_recv()
+            over_y.append([])
+            for dy in (2, 1, 3):
+                y_ = ring(y, dy)
+                for xh_ in (0, 1):
+                    theirs[xh_, y_, :, cut] = both(xh_, y_, cut).astype(BF)
+                over_y[k].append(
+                    links.copy(
+                        theirs.at[:, y_, :, cut],
+                        came.at[:, y, :, cut],
+                        place(z, xl, xh, y_, c),
+                    )
+                )
+        for k, cut in enumerate(cuts):
+            for cp in over_y[k]:
+                cp.wait_recv()
+            away, mine = both(1 - xh, y, cut), both(xh, y, cut)
+            for dy in (1, 3, 2):
+                y_ = ring(y, dy)
+                away = away + came[1 - xh, y_, :, cut].astype(F32)
+                mine = mine + came[xh, y_, :, cut].astype(F32)
+            theirs[1 - xh, y, :, cut] = away.astype(BF)
+            over_x.append(
+                links.copy(
+                    theirs.at[1 - xh, y, :, cut], far.at[:, cut], place(z, xl, 1 - xh, y, c)
+                )
+            )
+            total[:, cut] = mine
+        for cp in over_x:
             cp.wait_recv()
-        for dy in (1, 3, 2):
-            y_ = ring(y, dy)
-            away = away + came[1 - xh, y_].astype(F32)
-            total = total + came[xh, y_].astype(F32)
-        mine[1 - xh, y] = away.astype(BF)
-        over = links.copy(mine.at[1 - xh, y], far, place(z, xl, 1 - xh, y, c))
-        yield 0
-        over.wait()
-        total = total + far[...].astype(F32)
-        for cp in cps:
-            cp.wait_send()
-        swap.wait_send()
-        wide = layer_end(x_ref[...], total, again_ref[...]).astype(F32)
+        wide = layer_end(
+            x_ref[...], total[...] + far[...].astype(F32), again_ref[...]
+        ).astype(F32)
         squares = jnp.sum(wide * wide, axis=-1, keepdims=True)
         normed = wide * lax.rsqrt(squares * (1.0 / 4096) + EPSILON) * fgain_ref[...]
         outs[0][...] = normed.astype(BF)
         lane = lax.broadcasted_iota(jnp.int32, (8, 256), 1)
         row = lax.broadcasted_iota(jnp.int32, (8, 256), 0)
         outs[1][...] = jnp.where((lane == z * 2 + xl) & (row == 4), jnp.sum(squares), 0.0)
+        for cp in swaps + [cp for k in over_y for cp in k] + over_x:
+            cp.wait_send()
+        yield 0
 
     block = pltpu.VMEM((2, 4, 16, 4096), BF)
     return Task(
         body,
-        [(part, ANY), (states_in, VM), (attn_gain, VM), (final_gain, VM)],
+        [(a, ANY) for a in first] + [(states_in, VM), (attn_gain, VM), (final_gain, VM)],
         [(jax.ShapeDtypeStruct((16, 4096), BF), VM), (jax.ShapeDtypeStruct((8, 256), F32), VM)],
-        [block, block, block, pltpu.VMEM((16, 4096), BF)],
-        8,
-        1,
+        [pltpu.VMEM(a.shape, a.dtype) for a in first]
+        + [
+            pltpu.VMEM((256, 256), BF),
+            pltpu.VMEM((2, 4, 2, 16, 4096), BF),
+            block,
+            block,
+            pltpu.VMEM((16, 4096), BF),
+            pltpu.VMEM((16, 4096), F32),
+        ],
+        5 * chunks,
+        6,
         HEAD_AG,
     )
 
@@ -486,14 +630,7 @@
                 four[i + 1] = relay(i + 1, three[i + 1])
             if i + 2 < n:
                 three[i + 2] = spread(i + 2, 2, two[i + 2])
-            for pair in four[i]:
-                for cp in pair:
-                    cp.wait_recv()
-            if i == 0:
-                for cp in loads:
-                    cp.wait()
-            if i == n - 1:
-                maxima[0] = sq_ref[...]
+            if i == n - 2:
                 swap.wait()
                 for dy in (2, 1, 3, 0):
                     y_ = ring(y, dy)
@@ -506,6 +643,14 @@
                                 theirs.at[:, y_], came.at[:, y], place(z, xl, xh, y_, c)
                             )
                         )
+            for pair in four[i]:
+                for cp in pair:
+                    cp.wait_recv()
+            if i == 0:
+                for cp in loads:
+                    cp.wait()
+            if i == n - 1:
+                maxima[0] = sq_ref[...]
             multiply(i)
         top = lax.broadcasted_iota(jnp.int32, (8, 256), 0) < 4
 
@@ -535,9 +680,19 @@
         other = deep[3]
         for k in range(4, 7):
             other = join(other, deep[k])
-        top_ref[c] = mine
-        top_ref[1 - c] = other
-        sum_ref[...] = mine + other
+        even = jnp.where(c == 0, mine, other)
+        odd = jnp.where(c == 0, other, mine)
+        group = lax.broadcasted_iota(jnp.int32, (8, 128), 1) // 16
+        for q in range(4):
+            row = jnp.zeros((8, 128), F32)
+            for a in range(4):
+                for k, v in enumerate((even, odd)):
+                    half = v[:, q // 2 * 128 : q // 2 * 128 + 128]
+                    turn = (a * 16 + k * 16 - q % 2 * 64) % 128
+                    turned = pltpu.roll(half, turn, 1) if turn else half
+                    row = jnp.where(group == 2 * a + k, turned, row)
+            top_ref[:, q * 128 : q * 128 + 128] = row[:4]
+        sum_ref[...] = jnp.sqrt((mine + other) * (1.0 / (256 * 4096)))
         over_x.wait_recv()
         total = theirs[xh, y].astype(F32) + far[...].astype(F32)
         hid_ref[...] = layer_end(x_ref[...], total, again_ref[...])
@@ -564,7 +719,7 @@
         [(normed, VM), (squares, VM), (states_in, VM), (attn_gain, VM)]
         + [(a, ANY) for a in (own_head, other_head) + second],
         [
-            (jax.ShapeDtypeStruct((2, 8, 256), F32), VM),
+            (jax.ShapeDtypeStruct((4, 512), F32), VM),
             (jax.ShapeDtypeStruct((8, 256), F32), VM),
             (jax.ShapeDtypeStruct((16, 4096), BF), VM),
         ],
@@ -684,34 +839,6 @@
             mass = mass + f * st[:, i * 8 + g + 2 : i * 8 + g + 3]
             acc = acc + f * p_ref[i, :, cut].astype(F32)
         att[:, cut] = (acc / mass).astype(BF)
-
-
-def combine(parts, stats, q, k, v, w_out):
-    steps = 4
-    wide = w_out.shape[1] // steps
-
-    def kernel(p_ref, s_ref, q_ref, k_ref, v_ref, w_ref, o_ref, att):
-        @pl.when(pl.program_id(0) == 0)
-        def _():
-            attend(p_ref, s_ref, q_ref, k_ref, v_ref, att)
-
-        o = jnp.dot(att[...], w_ref[...], preferred_element_type=F32).astype(BF)
-        o_ref[...] = o.reshape(o_ref.shape)
-
-    def whole(a):
-        return pl.BlockSpec(a.shape, lambda i: (0,) * a.ndim)
-
-    return pl.pallas_call(
-        kernel,
-        grid=(steps,),
-        in_specs=[whole(a) for a in (parts, stats, q, k, v)]
-        + [pl.BlockSpec((256, wide), lambda i: (0, i))],
-        out_specs=pl.BlockSpec((2, 4, 2, 16, wide), lambda i: (0, 0, 0, 0, i)),
-        out_shape=jax.ShapeDtypeStruct((2, 4, 2, 16, w_out.shape[1]), BF),
-        scratch_shapes=[pltpu.VMEM((256, 256), BF)],
-        compiler_params=pltpu.CompilerParams(vmem_limit_bytes=16 << 20),
-        name="combine",
-    )(parts, stats, q, k, v, w_out)
 
 
 def shards(
@@ -742,47 +869,34 @@
     vocab_here = embed.shape[0]
     local_ids = token_ids - tok * vocab_here
     inside = (local_ids >= 0) & (local_ids < vocab_here)
-    looked_up = jnp.take(embed, jnp.clip(local_ids, 0, vocab_here - 1), axis=0)
-    looked_up = jnp.where(inside[:, None], looked_up, jnp.zeros_like(looked_up))
+    slots = jnp.where(inside, local_ids, vocab_here)
 
     weights = (w_query, w_key, w_value)
-    (rows1, q1, k1, v1), (came,) = comm(
-        [
-            gather_project(block_states, weights),
-            exchange_tok(looked_up.reshape(8, 256, 256)),
-        ],
-        0,
-        "comm_a",
-        60,
-    )
-    embedded = jnp.sum(came.astype(F32), axis=0).astype(BF)
-    swapped = jnp.where((accept == 1)[:, None], embedded, block_states)
-
-    (qs1,), (rows2, q2, k2, v2) = comm(
-        [gather_queries(q1), gather_project(swapped, weights)], 1, "comm_b", 60
+    ((rows1, q1, k1, v1, qs1, rows2, q2, k2, v2),) = comm(
+        [front(block_states, weights, embed, slots, accept.reshape(-1, 1))], 0, "comm_a", 60
     )
     part1, stat1 = cached_attention(begins, ends, qs1, cache_keys, cache_values)
 
-    (part1, stat1), (qs2,) = comm([exchange_tok(part1, stat1), gather_queries(q2)], 2, "comm_c")
-    sum1 = combine(part1, stat1, q1, k1, v1, w_out)
+    (qs2,), (part1, stat1) = comm(
+        [gather_queries(q2), exchange_tok(part1, stat1)], 2, "comm_c"
+    )
     part2, stat2 = cached_attention(begins, ends, qs2, cache_keys, cache_values)
 
-    (normed, squares), (part2, stat2) = comm(
-        [reduce_layer(sum1, rows1, attn_gain, final_gain), exchange_tok(part2, stat2)],
+    first = (part1, stat1, q1, k1, v1, w_out)
+    (part2, stat2), (normed, squares) = comm(
+        [exchange_tok(part2, stat2), end_first(first, rows1, attn_gain, final_gain)],
         3,
         "comm_d",
-        12,
+        16,
     )
     second = (part2, stat2, q2, k2, v2, w_out)
     ((top, sums, hiddens),) = comm(
         [gather_logits(normed, squares, lm_head, other_head, second, rows2, attn_gain)],
         4,
         "comm_e",
-        56,
-    )
-    top_logits = top[:, :4].reshape(2, 64, 16).transpose(1, 0, 2).reshape(-1)
-    request_norms = jnp.sqrt(sums[4, :8] / (256 * 4096))
-    return (hiddens, request_norms, top_logits)
+        52,
+    )
+    return (hiddens, sums[4, :8], top.reshape(-1))
 
 
 def solution(mesh):

time: 214 us -> 185 us (0.86)
  local copies, waits for them, and re-layouts: 17.6 us -> 4.52 us
  Pallas kernels: 186 us -> 176 us
  other arithmetic: 7.12 us -> 2.14 us
    gather x1 -> x0, local copies, waits for them, and re-layouts: 10.3 us -> none  [shards(): looked_up = jnp.take(embed, jnp.clip(local_ids, 0, vocab_here - 1), axis=0)]
    pallas_call x1 -> x0, Pallas kernels: 5.26 us -> none  [combine(): pl.pallas_call(kernel, grid=(steps,), in_specs=[whole(a) for a in (parts,...]
    pallas_call x5 -> x4, Pallas kernels: 168 us -> 162 us  [comm(): pl.pallas_call(kernel, out_shape=[o[0] for t in tasks for o in t.outs], i...]
    unnamed x37 -> x32, local copies, waits for them, and re-layouts: 5.67 us -> 2.54 us
  transfers between devices with their start and end apart: 1 -> 1, of which waited for: 0 -> 0; matrix products, arithmetic and copies ran while one was open for 8% -> 2% of each run, Pallas kernels for 57% -> 62%
where the time goes in v7:
time: 185 us
  Pallas kernels  176 us (95%)
  local copies, waits for them, and re-layouts  4.52 us (2%)
  other arithmetic  2.14 us (1%)
    pallas_call x4, Pallas kernels, comm(): pl.pallas_call(kernel, out_shape=[o[0] for t in tasks for o in t.outs], i...  162 us
    pallas_call x2, Pallas kernels, cached_attention(): pl.pallas_call(kernel, in_specs=[smem, smem, VM, VM, VM], out_specs=[VM,...  13.5 us
  transfers between devices with their start and end apart: 1, of which 0 were waited for; matrix products, arithmetic and copies ran while one was open for 2% of the time, Pallas kernels for 62%

profile of v7, /device:TPU:1, one launch (start us, length us, event | category | flops | bytes accessed | tf_op | source)
XLA Modules:
  0.0 184.9 jit_solution(15173959964687789145)
XLA Ops:
  0.6 1.5 collective-permute-start
  2.1 1.5 copy.17.refs_7_
  3.6 0.8 reduce-window.9
  4.4 1.3 and_select_fusion.refs_5_
  5.7 0.0 copy-start.14
  5.7 0.0 copy-start.1
  5.7 0.0 copy-start.2
  5.7 46.5 %comm_a.1 = (bf16[16,4096]{1,0:T(8,128)(2,1)}, bf16[256,256]{1,0:T(8,128)(2,1)}, bf16[256,256]{1,0:T(8,128)(2,1)}, bf16[256,256]{1,0:T(8,128)(2,1)}, bf16[8,256,...) custom-call(bf16[256,256]{1,0:T(8,128)(2,1)} %refs_6_.1, ...), custom_call_target="tpu_custom_call" | custom-call | tf_op jit(solution)/shard_map/comm_a/pallas_call | solution.py:116
  52.3 0.0 copy-done.14
  52.3 0.0 copy-done.1
  52.3 0.0 copy-done.2
  52.3 0.0 copy-start.3
  52.3 1.2 copy-done.3
  53.5 0.0 copy-start.4
  53.5 6.7 %cached.2 = (bf16[8,256,256]{2,1,0:T(8,128)(2,1)S(1)}, f32[8,8,256]{2,1,0:T(8,128)S(1)}) custom-call(s32[8]{0:T(128)S(1)} %get-tuple-element.50.lo_ref, s32[8]{0:T(128)S(1)} %get-tuple-element.49.hi_ref, bf16[8,256,256]{2,1,0:T(8,128)(2,1)S(1)} %copy-done.3, bf16[1024,256]{1,0:T(8,128)(2,1)S(1)} %copy-done.1, bf16[1024,256]{1,0:T(8,128)(2,1)S(1)} %copy-done.2), custom_call_target="tpu_custom_call" | custom-call | tf_op jit(solution)/shard_map/cached/pallas_call | solution.py:807
  60.3 0.0 copy-start
  60.3 0.0 copy-start.8
  60.3 0.0 copy-start.9
  60.3 0.0 copy-start.10
  60.3 0.0 copy-start.11
  60.3 0.0 copy-start.12
  60.3 0.0 copy-start.13
  60.4 0.0 copy-done.4
  60.4 27.0 %comm_c.1 = (bf16[8,256,256]{2,1,0:T(8,128)(2,1)S(1)}, bf16[8,256,256]{2,1,0:T(8,128)(2,1)S(1)}, f32[8,8,256]{2,1,0:T(8,128)S(1)}) custom-call(bf16[256,256]{1,0:T(8,128)(2,1)S(1)} %copy-done.4, bf16[8,256,256]{2,1,0:T(8,128)(2,1)S(1)} %get-tuple-element.28.refs_1_, f32[8,8,256]{2,1,0:T(8,128)S(1)} %get-tuple-element.29.refs_2_), custom_call_target="tpu_custom_call" | custom-call | tf_op jit(solution)/shard_map/comm_c/pallas_call | solution.py:116
  87.4 6.7 %cached.3 = (bf16[8,256,256]{2,1,0:T(8,128)(2,1)S(1)}, f32[8,8,256]{2,1,0:T(8,128)S(1)}) custom-call(s32[8]{0:T(128)S(1)} %get-tuple-element.50.lo_ref, s32[8]{0:T(128)S(1)} %get-tuple-element.49.hi_ref, bf16[8,256,256]{2,1,0:T(8,128)(2,1)S(1)} %get-tuple-element.30.q_ref, bf16[1024,256]{1,0:T(8,128)(2,1)S(1)} %copy-done.1, bf16[1024,256]{1,0:T(8,128)(2,1)S(1)} %copy-done.2), custom_call_target="tpu_custom_call" | custom-call | tf_op jit(solution)/shard_map/cached/pallas_call | solution.py:807
  94.2 0.0 copy-done
  94.2 0.0 copy-done.8
  94.2 0.0 copy-done.9
  94.2 0.0 copy-done.10
  94.2 0.0 copy-done.11
  94.2 0.0 copy-done.12
  94.2 0.0 copy-done.13
  94.2 0.0 copy-start.5
  94.2 0.0 copy-start.6
  94.2 0.0 copy-start.7
  94.3 28.1 %comm_d.1 = (bf16[8,256,256]{2,1,0:T(8,128)(2,1)S(1)}, f32[8,8,256]{2,1,0:T(8,128)S(1)}, bf16[16,4096]{1,0:T(8,128)(2,1)S(1)}, f32[8,256]{1,0:T(8,128)S(1)}) custom-call(bf16[8,256,256]{2,1,0:T(8,128)(2,1)S(1)} %get-tuple-element.31.refs_0_, f32[8,8,256]{2,1,0:T(8,128)S(1)} %get-tuple-element.32.refs_1_, bf16[8,256,256]{2,1,0:T(8,128)(2,1)S(1)} %get-tuple-element.33.refs_2_, ...), custom_call_target="tpu_custom_call" | custom-call | tf_op jit(solution)/shard_map/comm_d/pallas_call | solution.py:116
  122.3 0.0 collective-permute-done.refs_5_
  122.4 0.0 copy-done.5
  122.4 0.0 copy-done.6
  122.4 0.0 copy-done.7
  122.4 60.7 %comm_e.1 = (f32[4,512]{1,0:T(4,128)S(1)}, f32[8,256]{1,0:T(8,128)S(1)}, bf16[16,4096]{1,0:T(8,128)(2,1)S(1)}) custom-call(bf16[16,4096]{1,0:T(8,128)(2,1)S(1)} %get-tuple-element.39.refs_0_, f32[8,256]{1,0:T(8,128)S(1)} %get-tuple-element.40.refs_1_, bf16[16,4096]{1,0:T(8,128)(2,1)S(1)} %copy-done.5, f32[1,4096]{1,0:T(1,128)S(1)} %bitcast.17, ...), custom_call_target="tpu_custom_call" | custom-call | tf_op jit(solution)/shard_map/comm_e/pallas_call | solution.py:116
  183.1 0.5 slice_bitcast_fusion
  183.6 0.6 copy.18
  184.2 0.7 copy.20
  (1 shorter events, 0.0 us)
Async XLA Ops:
  0.6 121.7 %collective-permute-start = (bf16[784,4096]{1,0:T(8,128)(2,1)}, bf16[784,4096]{1,0:T(8,128)(2,1)}, u32[]{:S(2)}, u32[]{:S(2)}) collective-permute-start(bf16[784,4096]{1,0:T(8,128)(2,1)} %refs_4_.3), channel_id=1, source_target_pairs={{0,1},{1,0},{2,3},{3,2},{4,5},{5,4},{6,7},{7,6},{8,9},{9,8},{10,11... | collective-permute-start | bytes 19267592 | tf_op jit(solution)/shard_map/ppermute | solution.py:861
  5.7 46.5 %copy-start.14 = (s32[8]{0:T(128)S(1)}, s32[8]{0:T(128)}, u32[]{:S(2)}) copy-start(s32[8]{0:T(128)} %param.17) | copy-start | bytes 100
  5.7 46.6 %copy-start.1 = (bf16[1024,256]{1,0:T(8,128)(2,1)S(1)}, bf16[1024,256]{1,0:T(8,128)(2,1)}, u32[]{:S(2)}) copy-start(bf16[1024,256]{1,0:T(8,128)(2,1)} %k_ref.3) | copy-start | bytes 1572868
  5.7 46.6 %copy-start.2 = (bf16[1024,256]{1,0:T(8,128)(2,1)S(1)}, bf16[1024,256]{1,0:T(8,128)(2,1)}, u32[]{:S(2)}) copy-start(bf16[1024,256]{1,0:T(8,128)(2,1)} %v_ref.3) | copy-start | bytes 1572868
  52.3 1.2 copy-start.3
  53.5 6.8 %copy-start.4 = (bf16[256,256]{1,0:T(8,128)(2,1)S(1)}, bf16[256,256]{1,0:T(8,128)(2,1)}, u32[]{:S(2)}) copy-start(bf16[256,256]{1,0:T(8,128)(2,1)} %get-tuple-element.26.refs_0_.refs_8_) | copy-start | bytes 393220
  60.3 33.9 %copy-start = (bf16[256,4096]{1,0:T(8,128)(2,1)S(1)}, bf16[256,4096]{1,0:T(8,128)(2,1)}, u32[]{:S(2)}) copy-start(bf16[256,4096]{1,0:T(8,128)(2,1)} %refs_11_.1) | copy-start | bytes 6291460
  60.3 33.9 %copy-start.8 = (bf16[16,4096]{1,0:T(8,128)(2,1)S(1)}, bf16[16,4096]{1,0:T(8,128)(2,1)}, u32[]{:S(2)}) copy-start(bf16[16,4096]{1,0:T(8,128)(2,1)} %get-tuple-element.38.refs_8_) | copy-start | bytes 393220
  60.3 33.9 %copy-start.9 = (bf16[256,256]{1,0:T(8,128)(2,1)S(1)}, bf16[256,256]{1,0:T(8,128)(2,1)}, u32[]{:S(2)}) copy-start(bf16[256,256]{1,0:T(8,128)(2,1)} %get-tuple-element.35.refs_4_) | copy-start | bytes 393220
  60.3 33.9 %copy-start.10 = (bf16[256,256]{1,0:T(8,128)(2,1)S(1)}, bf16[256,256]{1,0:T(8,128)(2,1)}, u32[]{:S(2)}) copy-start(bf16[256,256]{1,0:T(8,128)(2,1)} %get-tuple-element.36.refs_5_) | copy-start | bytes 393220
  60.3 33.9 %copy-start.11 = (bf16[256,256]{1,0:T(8,128)(2,1)S(1)}, bf16[256,256]{1,0:T(8,128)(2,1)}, u32[]{:S(2)}) copy-start(bf16[256,256]{1,0:T(8,128)(2,1)} %get-tuple-element.37.refs_6_) | copy-start | bytes 393220
  60.3 33.9 %copy-start.12 = (f32[4096]{0:T(1024)S(1)}, f32[4096]{0:T(1024)}, u32[]{:S(2)}) copy-start(f32[4096]{0:T(1024)} %param.24) | copy-start | bytes 49156
  60.3 33.9 %copy-start.13 = (f32[4096]{0:T(1024)S(1)}, f32[4096]{0:T(1024)}, u32[]{:S(2)}) copy-start(f32[4096]{0:T(1024)} %param.25) | copy-start | bytes 49156
  94.2 28.1 %copy-start.5 = (bf16[16,4096]{1,0:T(8,128)(2,1)S(1)}, bf16[16,4096]{1,0:T(8,128)(2,1)}, u32[]{:S(2)}) copy-start(bf16[16,4096]{1,0:T(8,128)(2,1)} %get-tuple-element.41.refs_2_) | copy-start | bytes 393220
  94.2 28.1 %copy-start.6 = (bf16[256,256]{1,0:T(8,128)(2,1)S(1)}, bf16[256,256]{1,0:T(8,128)(2,1)}, u32[]{:S(2)}) copy-start(bf16[256,256]{1,0:T(8,128)(2,1)} %get-tuple-element.44.refs_9_) | copy-start | bytes 393220
  94.2 28.1 %copy-start.7 = (bf16[256,256]{1,0:T(8,128)(2,1)S(1)}, bf16[256,256]{1,0:T(8,128)(2,1)}, u32[]{:S(2)}) copy-start(bf16[256,256]{1,0:T(8,128)(2,1)} %get-tuple-element.45.refs_10_) | copy-start | bytes 393220

commit v8 on v7

--- a/solution.py
+++ b/solution.py
@@ -309,7 +309,8 @@
         cp.wait()
     for source in sources:
         total = total + came[source].astype(F32)
-    new_ref[...] = jnp.where(acc_ref[...] == 1, total, old_ref[...].astype(F32)).astype(BF)
+    taken = jnp.transpose(jnp.broadcast_to(acc_ref[...].astype(F32), (256, 256)))
+    new_ref[...] = jnp.where(taken == 1.0, total, old_ref[...].astype(F32)).astype(BF)
 
 
 def front(block_states, weights, embed, slots, accept):
@@ -519,6 +520,10 @@
             for k, src in enumerate((own_ref, other_ref))
         ]
 
+        for cp in loads:
+            cp.start()
+        yield 0
+
         def block(i, p, known, step=0, half=None):
             last = ORDERS[p][2]
             z_, y_, x_ = z, y, x
@@ -607,7 +612,7 @@
             for k, (src, dst) in enumerate(zip(ins[6:], held))
         ]
         one = [spread(i, 0, None) for i in range(n)]
-        for cp in fetch + loads:
+        for cp in fetch:
             cp.start()
         two = [spread(i, 1, one[i]) for i in range(n)]
         three = {0: spread(0, 2, two[0]), 1: spread(1, 2, two[1])}
@@ -730,23 +735,73 @@
     )
 
 
+def back(part2, stat2, first, rows1, gains, heads, second, rows2):
+    attn_gain, final_gain = gains
+    home = exchange_tok(part2, stat2)
+    end = end_first(first, rows1, attn_gain, final_gain)
+    normed, squares = (o[0] for o in end.outs)
+    shapes = [o[0] for o in home.outs]
+    last = gather_logits(normed, squares, *heads, (*shapes, *second), rows2, attn_gain)
+    tasks = (home, end, last)
+    extra = [(rows2, VM), (heads[0], ANY), (heads[1], ANY)] + [(v, ANY) for v in second]
+
+    def body(ins, outs, scr):
+        n_home, n_end = len(home.ins), len(home.ins) + len(end.ins)
+        in_home, in_end, more = ins[:n_home], ins[n_home:n_end], ins[n_end:]
+        again = in_end[7]
+        parts, k = [], 0
+        for task in tasks:
+            parts.append(scr[k : k + len(task.scratch)])
+            k += len(task.scratch)
+        n_ref, sq_ref = scr[k:]
+        in_last = (n_ref, sq_ref, more[0], again, more[1], more[2], *outs[:2], *more[3:])
+        three = last.body(in_last, outs[2:], parts[2])
+        one = home.body(in_home, outs[:2], parts[0])
+        two = end.body(in_end, (n_ref, sq_ref), parts[1])
+        next(one)
+        next(three)
+        next(two)
+        next(one, None)
+        next(three)
+        next(two, None)
+        next(three, None)
+        yield 0
+
+    task = Task(
+        body,
+        list(home.ins) + list(end.ins) + extra,
+        list(home.outs) + list(last.outs),
+        [],
+        1,
+        1,
+        HEAD_AG + TOK_ALL + AXES + PLANE + DEEP,
+    )
+    task.scratch = [v for t in tasks for v in t.scratch]
+    task.scratch += [pltpu.VMEM(v.shape, v.dtype) for v in (normed, squares)]
+    return task
+
+
 def scores(q, k):
     return lax.dot_general(q, k, (((1,), (1,)), ((), ())), preferred_element_type=F32) * SCALE2
 
 
-def cached_attention(begins, ends, queries, keys, values):
+def cached_attention(lengths, queries, keys, values):
     rows = queries.shape[1]
     cuts = [slice(g * HEAD_DIM, (g + 1) * HEAD_DIM) for g in (0, 1)]
 
-    def kernel(lo_ref, hi_ref, q_ref, k_ref, v_ref, o_ref, s_ref, v_sc, m_sc, a_sc):
+    def kernel(len_ref, q_ref, k_ref, v_ref, o_ref, s_ref, v_sc, m_sc, a_sc):
         for g in range(2):
             v_sc[g, :, :HEAD_DIM] = v_ref[:, g * HEAD_DIM : (g + 1) * HEAD_DIM]
             v_sc[g, :, HEAD_DIM:] = jnp.ones((v_ref.shape[0], HEAD_DIM), BF)
         lane = lax.broadcasted_iota(jnp.int32, (rows, 128), 1)
         sub = lax.broadcasted_iota(jnp.int32, (8, rows), 0)
 
-        def request(r, carry):
-            lo, hi = lo_ref[r], hi_ref[r]
+        held = k_ref.shape[0]
+
+        def request(r, before):
+            after = before + len_ref[r]
+            lo = jnp.minimum(jnp.maximum(before, 0), held)
+            hi = jnp.minimum(jnp.maximum(after, 0), held)
 
             @pl.when(hi <= lo)
             def _():
@@ -799,14 +854,14 @@
                 for g in range(2):
                     o_ref[r, :, g * HEAD_DIM : (g + 1) * HEAD_DIM] = a_sc[g, :, :HEAD_DIM].astype(BF)
 
-            return carry
-
-        lax.fori_loop(0, 8, request, 0)
+            return after
+
+        lax.fori_loop(0, 8, request, -lax.axis_index("tok") * held)
 
     smem = pl.BlockSpec(memory_space=pltpu.SMEM)
     return pl.pallas_call(
         kernel,
-        in_specs=[smem, smem, VM, VM, VM],
+        in_specs=[smem, VM, VM, VM],
         out_specs=[VM, VM],
         scratch_shapes=[
             pltpu.VMEM((2, values.shape[0], 256), BF),
@@ -819,7 +874,7 @@
         ],
         compiler_params=pltpu.CompilerParams(vmem_limit_bytes=16 << 20),
         name="cached",
-    )(begins, ends, queries, keys, values)
+    )(lengths, queries, keys, values)
 
 
 def attend(p_ref, s_ref, q_ref, k_ref, v_ref, att):
@@ -859,10 +914,6 @@
 ):
     tok = lax.axis_index("tok")
     other_head = lax.ppermute(lm_head, "head", [(i, i ^ 1) for i in range(16)])
-    cache_here = cache_keys.shape[0]
-    offsets = jnp.cumsum(cache_lengths) - cache_lengths - tok * cache_here
-    begins = jnp.clip(offsets, 0, cache_here)
-    ends = jnp.clip(offsets + cache_lengths, 0, cache_here)
     attn_gain = attn_gain.reshape(1, -1)
     final_gain = final_gain.reshape(1, -1)
 
@@ -873,28 +924,32 @@
 
     weights = (w_query, w_key, w_value)
     ((rows1, q1, k1, v1, qs1, rows2, q2, k2, v2),) = comm(
-        [front(block_states, weights, embed, slots, accept.reshape(-1, 1))], 0, "comm_a", 60
-    )
-    part1, stat1 = cached_attention(begins, ends, qs1, cache_keys, cache_values)
+        [front(block_states, weights, embed, slots, accept.reshape(1, -1))], 0, "comm_a", 60
+    )
+    part1, stat1 = cached_attention(cache_lengths, qs1, cache_keys, cache_values)
 
     (qs2,), (part1, stat1) = comm(
         [gather_queries(q2), exchange_tok(part1, stat1)], 2, "comm_c"
     )
-    part2, stat2 = cached_attention(begins, ends, qs2, cache_keys, cache_values)
+    part2, stat2 = cached_attention(cache_lengths, qs2, cache_keys, cache_values)
 
     first = (part1, stat1, q1, k1, v1, w_out)
-    (part2, stat2), (normed, squares) = comm(
-        [exchange_tok(part2, stat2), end_first(first, rows1, attn_gain, final_gain)],
+    ((_, _, top, sums, hiddens),) = comm(
+        [
+            back(
+                part2,
+                stat2,
+                first,
+                rows1,
+                (attn_gain, final_gain),
+                (lm_head, other_head),
+                (q2, k2, v2, w_out),
+                rows2,
+            )
+        ],
         3,
         "comm_d",
-        16,
-    )
-    second = (part2, stat2, q2, k2, v2, w_out)
-    ((top, sums, hiddens),) = comm(
-        [gather_logits(normed, squares, lm_head, other_head, second, rows2, attn_gain)],
-        4,
-        "comm_e",
-        52,
+        50,
     )
     return (hiddens, sums[4, :8], top.reshape(-1))
 

time: 185 us -> 185 us (level)
    pallas_call x4 -> x3, Pallas kernels: 162 us -> 165 us  [comm(): pl.pallas_call(kernel, out_shape=[o[0] for t in tasks for o in t.outs], i...]
  transfers between devices with their start and end apart: 1 -> 1, of which waited for: 0 -> 0; matrix products, arithmetic and copies ran while one was open for 2% -> 1% of each run, Pallas kernels for 62% -> 46%
where the time goes in v8:
time: 185 us
  Pallas kernels  177 us (96%)
  local copies, waits for them, and re-layouts  4 us (2%)
    pallas_call x3, Pallas kernels, comm(): pl.pallas_call(kernel, out_shape=[o[0] for t in tasks for o in t.outs], i...  165 us
    pallas_call x2, Pallas kernels, cached_attention(): pl.pallas_call(kernel, in_specs=[smem, VM, VM, VM], out_specs=[VM, VM], s...  12.2 us
  transfers between devices with their start and end apart: 1, of which 0 were waited for; matrix products, arithmetic and copies ran while one was open for 1% of the time, Pallas kernels for 46%

profile of v8, /device:TPU:1, one launch (start us, length us, event | category | flops | bytes accessed | tf_op | source)
XLA Modules:
  0.0 185.0 jit_solution(18347738183648157688)
XLA Ops:
  0.6 1.5 collective-permute-start
  2.1 1.3 and_select_fusion.refs_5_
  3.4 0.0 copy-start
  3.4 0.0 copy-start.1
  3.4 0.0 copy-start.14
  3.4 46.5 %comm_a.1 = (bf16[16,4096]{1,0:T(8,128)(2,1)}, bf16[256,256]{1,0:T(8,128)(2,1)}, bf16[256,256]{1,0:T(8,128)(2,1)}, bf16[256,256]{1,0:T(8,128)(2,1)}, bf16[8,256,...) custom-call(bf16[256,256]{1,0:T(8,128)(2,1)} %refs_6_.1, ...), custom_call_target="tpu_custom_call" | custom-call | tf_op jit(solution)/shard_map/comm_a/pallas_call | solution.py:116
  49.9 0.0 copy-done
  49.9 0.0 copy-done.1
  49.9 0.0 copy-done.14
  49.9 0.0 copy-start.3
  49.9 1.2 copy-done.3
  51.2 0.0 copy-start.4
  51.2 6.1 %cached.2 = (bf16[8,256,256]{2,1,0:T(8,128)(2,1)S(1)}, f32[8,8,256]{2,1,0:T(8,128)S(1)}) custom-call(s32[8]{0:T(128)S(1)} %copy-done.14, bf16[8,256,256]{2,1,0:T(8,128)(2,1)S(1)} %copy-done.3, bf16[1024,256]{1,0:T(8,128)(2,1)S(1)} %copy-done, bf16[1024,256]{1,0:T(8,128)(2,1)S(1)} %copy-done.1), custom_call_target="tpu_custom_call" | custom-call | tf_op jit(solution)/shard_map/cached/pallas_call | solution.py:862
  57.2 0.0 copy-start.5
  57.3 0.0 copy-start.6
  57.3 0.0 copy-start.7
  57.3 0.0 copy-start.8
  57.3 0.0 copy-start.9
  57.3 0.0 copy-start.10
  57.3 0.0 copy-start.11
  57.3 0.0 copy-start.12
  57.3 0.0 copy-start.13
  57.3 0.0 copy-done.4
  57.4 27.0 %comm_c.1 = (bf16[8,256,256]{2,1,0:T(8,128)(2,1)S(1)}, bf16[8,256,256]{2,1,0:T(8,128)(2,1)S(1)}, f32[8,8,256]{2,1,0:T(8,128)S(1)}) custom-call(bf16[256,256]{1,0:T(8,128)(2,1)S(1)} %copy-done.4, bf16[8,256,256]{2,1,0:T(8,128)(2,1)S(1)} %get-tuple-element.24.refs_1_, f32[8,8,256]{2,1,0:T(8,128)S(1)} %get-tuple-element.25.refs_2_), custom_call_target="tpu_custom_call" | custom-call | tf_op jit(solution)/shard_map/comm_c/pallas_call | solution.py:116
  84.4 0.0 copy-start.2
  84.4 1.0 copy-done.2
  85.4 6.1 %cached.3 = (bf16[8,256,256]{2,1,0:T(8,128)(2,1)S(1)}, f32[8,8,256]{2,1,0:T(8,128)S(1)}) custom-call(s32[8]{0:T(128)S(1)} %copy-done.14, bf16[8,256,256]{2,1,0:T(8,128)(2,1)S(1)} %get-tuple-element.26.q_ref, bf16[1024,256]{1,0:T(8,128)(2,1)S(1)} %copy-done, bf16[1024,256]{1,0:T(8,128)(2,1)S(1)} %copy-done.1), custom_call_target="tpu_custom_call" | custom-call | tf_op jit(solution)/shard_map/cached/pallas_call | solution.py:862
  91.4 0.0 collective-permute-done.refs_13_
  91.4 0.0 copy-done.5
  91.5 0.0 copy-done.6
  91.5 0.0 copy-done.7
  91.5 0.0 copy-done.8
  91.5 0.0 copy-done.9
  91.5 0.0 copy-done.10
  91.5 0.0 copy-done.11
  91.5 0.0 copy-done.12
  91.5 0.0 copy-done.13
  91.5 91.7 %comm_d.1 = (bf16[8,256,256]{2,1,0:T(8,128)(2,1)}, f32[8,8,256]{2,1,0:T(8,128)}, f32[4,512]{1,0:T(4,128)S(1)}, f32[8,256]{1,0:T(8,128)S(1)}, bf16[16,4096]{1,0:T(8,128)(2,1)S(1)}) custom-call(bf16[8,256,256]{2,1,0:T(8,128)(2,1)S(1)} %get-tuple-element.27.refs_0_, f32[8,8,256]{2,1,0:T(8,128)S(1)} %get-tuple-element.28.refs_1_, ...), custom_call_target="tpu_custom_call" | custom-call | tf_op jit(solution)/shard_map/comm_d/pallas_call | solution.py:116
  183.2 0.5 slice_bitcast_fusion
  183.7 0.6 copy.17
  184.3 0.7 copy.19
Async XLA Ops:
  0.6 90.8 %collective-permute-start = (bf16[784,4096]{1,0:T(8,128)(2,1)}, bf16[784,4096]{1,0:T(8,128)(2,1)}, u32[]{:S(2)}, u32[]{:S(2)}) collective-permute-start(bf16[784,4096]{1,0:T(8,128)(2,1)} %refs_12_.1), channel_id=1, source_target_pairs={{0,1},{1,0},{2,3},{3,2},{4,5},{5,4},{6,7},{7,6},{8,9},{9,8},{10,11... | collective-permute-start | bytes 19267592 | tf_op jit(solution)/shard_map/ppermute | solution.py:916
  3.4 46.5 %copy-start = (bf16[1024,256]{1,0:T(8,128)(2,1)S(1)}, bf16[1024,256]{1,0:T(8,128)(2,1)}, u32[]{:S(2)}) copy-start(bf16[1024,256]{1,0:T(8,128)(2,1)} %k_ref.3) | copy-start | bytes 1572868
  3.4 46.5 %copy-start.1 = (bf16[1024,256]{1,0:T(8,128)(2,1)S(1)}, bf16[1024,256]{1,0:T(8,128)(2,1)}, u32[]{:S(2)}) copy-start(bf16[1024,256]{1,0:T(8,128)(2,1)} %v_ref.3) | copy-start | bytes 1572868
  3.4 46.5 %copy-start.14 = (s32[8]{0:T(128)S(1)}, s32[8]{0:T(128)}, u32[]{:S(2)}) copy-start(s32[8]{0:T(128)} %len_ref.3) | copy-start | bytes 100
  49.9 1.2 copy-start.3
  51.2 6.2 %copy-start.4 = (bf16[256,256]{1,0:T(8,128)(2,1)S(1)}, bf16[256,256]{1,0:T(8,128)(2,1)}, u32[]{:S(2)}) copy-start(bf16[256,256]{1,0:T(8,128)(2,1)} %get-tuple-element.22.refs_0_.refs_14_) | copy-start | bytes 393220
  57.2 34.2 %copy-start.5 = (bf16[16,4096]{1,0:T(8,128)(2,1)S(1)}, bf16[16,4096]{1,0:T(8,128)(2,1)}, u32[]{:S(2)}) copy-start(bf16[16,4096]{1,0:T(8,128)(2,1)} %get-tuple-element.34.refs_8_) | copy-start | bytes 393220
  57.3 34.2 %copy-start.6 = (bf16[256,256]{1,0:T(8,128)(2,1)S(1)}, bf16[256,256]{1,0:T(8,128)(2,1)}, u32[]{:S(2)}) copy-start(bf16[256,256]{1,0:T(8,128)(2,1)} %get-tuple-element.31.refs_4_) | copy-start | bytes 393220
  57.3 34.2 %copy-start.7 = (bf16[256,256]{1,0:T(8,128)(2,1)S(1)}, bf16[256,256]{1,0:T(8,128)(2,1)}, u32[]{:S(2)}) copy-start(bf16[256,256]{1,0:T(8,128)(2,1)} %get-tuple-element.32.refs_5_) | copy-start | bytes 393220
  57.3 34.2 %copy-start.8 = (bf16[256,256]{1,0:T(8,128)(2,1)S(1)}, bf16[256,256]{1,0:T(8,128)(2,1)}, u32[]{:S(2)}) copy-start(bf16[256,256]{1,0:T(8,128)(2,1)} %get-tuple-element.33.refs_6_) | copy-start | bytes 393220
  57.3 34.2 %copy-start.9 = (bf16[16,4096]{1,0:T(8,128)(2,1)S(1)}, bf16[16,4096]{1,0:T(8,128)(2,1)}, u32[]{:S(2)}) copy-start(bf16[16,4096]{1,0:T(8,128)(2,1)} %get-tuple-element.35.refs_11_) | copy-start | bytes 393220
  57.3 34.2 %copy-start.10 = (bf16[256,256]{1,0:T(8,128)(2,1)S(1)}, bf16[256,256]{1,0:T(8,128)(2,1)}, u32[]{:S(2)}) copy-start(bf16[256,256]{1,0:T(8,128)(2,1)} %get-tuple-element.36.refs_15_) | copy-start | bytes 393220
  57.3 34.2 %copy-start.11 = (bf16[256,256]{1,0:T(8,128)(2,1)S(1)}, bf16[256,256]{1,0:T(8,128)(2,1)}, u32[]{:S(2)}) copy-start(bf16[256,256]{1,0:T(8,128)(2,1)} %get-tuple-element.37.refs_16_) | copy-start | bytes 393220
  57.3 34.2 %copy-start.12 = (f32[4096]{0:T(1024)S(1)}, f32[4096]{0:T(1024)}, u32[]{:S(2)}) copy-start(f32[4096]{0:T(1024)} %param.24) | copy-start | bytes 49156
  57.3 34.2 %copy-start.13 = (f32[4096]{0:T(1024)S(1)}, f32[4096]{0:T(1024)}, u32[]{:S(2)}) copy-start(f32[4096]{0:T(1024)} %param.25) | copy-start | bytes 49156
  84.4 1.0 copy-start.2

commit v9 on v8

--- a/solution.py
+++ b/solution.py
@@ -423,6 +423,7 @@
             swaps.append(
                 links.copy(out.at[:, :, 1 - c, :, cut], theirs.at[:, :, :, cut], core)
             )
+        yield 0
 
         def both(xh_, y_, cut):
             return out[xh_, y_, c, :, cut].astype(F32) + theirs[xh_, y_, :, cut].astype(F32)
@@ -759,6 +760,7 @@
         one = home.body(in_home, outs[:2], parts[0])
         two = end.body(in_end, (n_ref, sq_ref), parts[1])
         next(one)
+        next(two)
         next(three)
         next(two)
         next(one, None)
@@ -949,7 +951,7 @@
         ],
         3,
         "comm_d",
-        50,
+        47,
     )
     return (hiddens, sums[4, :8], top.reshape(-1))
 

time: 185 us -> 178 us (0.962)
  Pallas kernels: 177 us -> 171 us
    pallas_call x3, Pallas kernels: 165 us -> 160 us  [comm(): pl.pallas_call(kernel, out_shape=[o[0] for t in tasks for o in t.outs], i...]
  transfers between devices with their start and end apart: 1 -> 1, of which waited for: 0 -> 0; matrix products, arithmetic and copies ran while one was open for 1% -> 1% of each run, Pallas kernels for 46% -> 47%
where the time goes in v9:
time: 178 us
  Pallas kernels  171 us (96%)
  local copies, waits for them, and re-layouts  3.05 us (2%)
    pallas_call x3, Pallas kernels, comm(): pl.pallas_call(kernel, out_shape=[o[0] for t in tasks for o in t.outs], i...  160 us
    pallas_call x2, Pallas kernels, cached_attention(): pl.pallas_call(kernel, in_specs=[smem, VM, VM, VM], out_specs=[VM, VM], s...  10.4 us
  transfers between devices with their start and end apart: 1, of which 0 were waited for; matrix products, arithmetic and copies ran while one was open for 1% of the time, Pallas kernels for 47%

profile of v9, /device:TPU:1, one launch (start us, length us, event | category | flops | bytes accessed | tf_op | source)
XLA Modules:
  0.0 177.5 jit_solution(6258848692605993484)
XLA Ops:
  0.6 1.5 collective-permute-start
  2.1 1.3 and_select_fusion.refs_5_
  3.4 0.0 copy-start.1
  3.4 0.0 copy-start.2
  3.4 0.0 copy-start.14
  3.4 46.5 %comm_a.1 = (bf16[16,4096]{1,0:T(8,128)(2,1)}, bf16[256,256]{1,0:T(8,128)(2,1)}, bf16[256,256]{1,0:T(8,128)(2,1)}, bf16[256,256]{1,0:T(8,128)(2,1)}, bf16[8,256,...) custom-call(bf16[256,256]{1,0:T(8,128)(2,1)} %refs_6_.1, ...), custom_call_target="tpu_custom_call" | custom-call | tf_op jit(solution)/shard_map/comm_a/pallas_call | solution.py:116
  49.9 0.0 copy-done.1
  49.9 0.0 copy-done.2
  49.9 0.0 copy-done.14
  49.9 0.0 copy-start.3
  49.9 1.2 copy-done.3
  51.2 0.0 copy-start.4
  51.2 5.2 %cached.2 = (bf16[8,256,256]{2,1,0:T(8,128)(2,1)S(1)}, f32[8,8,256]{2,1,0:T(8,128)S(1)}) custom-call(s32[8]{0:T(128)S(1)} %copy-done.14, bf16[8,256,256]{2,1,0:T(8,128)(2,1)S(1)} %copy-done.3, bf16[1024,256]{1,0:T(8,128)(2,1)S(1)} %copy-done.1, bf16[1024,256]{1,0:T(8,128)(2,1)S(1)} %copy-done.2), custom_call_target="tpu_custom_call" | custom-call | tf_op jit(solution)/shard_map/cached/pallas_call | solution.py:864
  56.4 0.0 copy-start
  56.4 0.0 copy-start.5
  56.4 0.0 copy-start.6
  56.4 0.0 copy-start.7
  56.4 0.0 copy-start.8
  56.4 0.0 copy-start.9
  56.4 0.0 copy-start.10
  56.4 0.0 copy-start.11
  56.4 0.0 copy-start.12
  56.5 0.0 copy-start.13
  56.5 0.0 copy-done.4
  56.5 27.0 %comm_c.1 = (bf16[8,256,256]{2,1,0:T(8,128)(2,1)S(1)}, bf16[8,256,256]{2,1,0:T(8,128)(2,1)S(1)}, f32[8,8,256]{2,1,0:T(8,128)S(1)}) custom-call(bf16[256,256]{1,0:T(8,128)(2,1)S(1)} %copy-done.4, bf16[8,256,256]{2,1,0:T(8,128)(2,1)S(1)} %get-tuple-element.24.refs_1_, f32[8,8,256]{2,1,0:T(8,128)S(1)} %get-tuple-element.25.refs_2_), custom_call_target="tpu_custom_call" | custom-call | tf_op jit(solution)/shard_map/comm_c/pallas_call | solution.py:116
  83.5 5.2 %cached.3 = (bf16[8,256,256]{2,1,0:T(8,128)(2,1)S(1)}, f32[8,8,256]{2,1,0:T(8,128)S(1)}) custom-call(s32[8]{0:T(128)S(1)} %copy-done.14, bf16[8,256,256]{2,1,0:T(8,128)(2,1)S(1)} %get-tuple-element.26.q_ref, bf16[1024,256]{1,0:T(8,128)(2,1)S(1)} %copy-done.1, bf16[1024,256]{1,0:T(8,128)(2,1)S(1)} %copy-done.2), custom_call_target="tpu_custom_call" | custom-call | tf_op jit(solution)/shard_map/cached/pallas_call | solution.py:864
  88.7 0.0 collective-permute-done.refs_13_
  88.7 0.0 copy-done
  88.7 0.0 copy-done.5
  88.7 0.0 copy-done.6
  88.8 0.0 copy-done.7
  88.8 0.0 copy-done.8
  88.8 0.0 copy-done.9
  88.8 0.0 copy-done.10
  88.8 0.0 copy-done.11
  88.8 0.0 copy-done.12
  88.8 0.0 copy-done.13
  88.8 86.9 %comm_d.1 = (bf16[8,256,256]{2,1,0:T(8,128)(2,1)}, f32[8,8,256]{2,1,0:T(8,128)}, f32[4,512]{1,0:T(4,128)S(1)}, f32[8,256]{1,0:T(8,128)S(1)}, bf16[16,4096]{1,0:T(8,128)(2,1)S(1)}) custom-call(bf16[8,256,256]{2,1,0:T(8,128)(2,1)S(1)} %get-tuple-element.27.refs_0_, f32[8,8,256]{2,1,0:T(8,128)S(1)} %get-tuple-element.28.refs_1_, ...), custom_call_target="tpu_custom_call" | custom-call | tf_op jit(solution)/shard_map/comm_d/pallas_call | solution.py:116
  175.8 0.5 slice_bitcast_fusion
  176.3 0.6 copy.17
  176.9 0.7 copy.19
Async XLA Ops:
  0.6 88.1 %collective-permute-start = (bf16[784,4096]{1,0:T(8,128)(2,1)}, bf16[784,4096]{1,0:T(8,128)(2,1)}, u32[]{:S(2)}, u32[]{:S(2)}) collective-permute-start(bf16[784,4096]{1,0:T(8,128)(2,1)} %refs_12_.1), channel_id=1, source_target_pairs={{0,1},{1,0},{2,3},{3,2},{4,5},{5,4},{6,7},{7,6},{8,9},{9,8},{10,11... | collective-permute-start | bytes 19267592 | tf_op jit(solution)/shard_map/ppermute | solution.py:918
  3.4 46.5 %copy-start.1 = (bf16[1024,256]{1,0:T(8,128)(2,1)S(1)}, bf16[1024,256]{1,0:T(8,128)(2,1)}, u32[]{:S(2)}) copy-start(bf16[1024,256]{1,0:T(8,128)(2,1)} %k_ref.3) | copy-start | bytes 1572868
  3.4 46.5 %copy-start.2 = (bf16[1024,256]{1,0:T(8,128)(2,1)S(1)}, bf16[1024,256]{1,0:T(8,128)(2,1)}, u32[]{:S(2)}) copy-start(bf16[1024,256]{1,0:T(8,128)(2,1)} %v_ref.3) | copy-start | bytes 1572868
  3.4 46.5 %copy-start.14 = (s32[8]{0:T(128)S(1)}, s32[8]{0:T(128)}, u32[]{:S(2)}) copy-start(s32[8]{0:T(128)} %len_ref.3) | copy-start | bytes 100
  49.9 1.2 copy-start.3
  51.2 5.3 %copy-start.4 = (bf16[256,256]{1,0:T(8,128)(2,1)S(1)}, bf16[256,256]{1,0:T(8,128)(2,1)}, u32[]{:S(2)}) copy-start(bf16[256,256]{1,0:T(8,128)(2,1)} %get-tuple-element.22.refs_0_.refs_14_) | copy-start | bytes 393220
  56.4 32.4 %copy-start = (bf16[256,4096]{1,0:T(8,128)(2,1)S(1)}, bf16[256,4096]{1,0:T(8,128)(2,1)}, u32[]{:S(2)}) copy-start(bf16[256,4096]{1,0:T(8,128)(2,1)} %refs_17_.1) | copy-start | bytes 6291460
  56.4 32.4 %copy-start.5 = (bf16[16,4096]{1,0:T(8,128)(2,1)S(1)}, bf16[16,4096]{1,0:T(8,128)(2,1)}, u32[]{:S(2)}) copy-start(bf16[16,4096]{1,0:T(8,128)(2,1)} %get-tuple-element.34.refs_8_) | copy-start | bytes 393220
  56.4 32.4 %copy-start.6 = (bf16[256,256]{1,0:T(8,128)(2,1)S(1)}, bf16[256,256]{1,0:T(8,128)(2,1)}, u32[]{:S(2)}) copy-start(bf16[256,256]{1,0:T(8,128)(2,1)} %get-tuple-element.31.refs_4_) | copy-start | bytes 393220
  56.4 32.4 %copy-start.7 = (bf16[256,256]{1,0:T(8,128)(2,1)S(1)}, bf16[256,256]{1,0:T(8,128)(2,1)}, u32[]{:S(2)}) copy-start(bf16[256,256]{1,0:T(8,128)(2,1)} %get-tuple-element.32.refs_5_) | copy-start | bytes 393220
  56.4 32.4 %copy-start.8 = (bf16[256,256]{1,0:T(8,128)(2,1)S(1)}, bf16[256,256]{1,0:T(8,128)(2,1)}, u32[]{:S(2)}) copy-start(bf16[256,256]{1,0:T(8,128)(2,1)} %get-tuple-element.33.refs_6_) | copy-start | bytes 393220
  56.4 32.4 %copy-start.9 = (bf16[16,4096]{1,0:T(8,128)(2,1)S(1)}, bf16[16,4096]{1,0:T(8,128)(2,1)}, u32[]{:S(2)}) copy-start(bf16[16,4096]{1,0:T(8,128)(2,1)} %get-tuple-element.35.refs_11_) | copy-start | bytes 393220
  56.4 32.4 %copy-start.10 = (bf16[256,256]{1,0:T(8,128)(2,1)S(1)}, bf16[256,256]{1,0:T(8,128)(2,1)}, u32[]{:S(2)}) copy-start(bf16[256,256]{1,0:T(8,128)(2,1)} %get-tuple-element.36.refs_15_) | copy-start | bytes 393220
  56.4 32.4 %copy-start.11 = (bf16[256,256]{1,0:T(8,128)(2,1)S(1)}, bf16[256,256]{1,0:T(8,128)(2,1)}, u32[]{:S(2)}) copy-start(bf16[256,256]{1,0:T(8,128)(2,1)} %get-tuple-element.37.refs_16_) | copy-start | bytes 393220
  56.4 32.4 %copy-start.12 = (f32[4096]{0:T(1024)S(1)}, f32[4096]{0:T(1024)}, u32[]{:S(2)}) copy-start(f32[4096]{0:T(1024)} %param.24) | copy-start | bytes 49156
  56.5 32.4 %copy-start.13 = (f32[4096]{0:T(1024)S(1)}, f32[4096]{0:T(1024)}, u32[]{:S(2)}) copy-start(f32[4096]{0:T(1024)} %param.25) | copy-start | bytes 49156
